TPU v7x, 128 devices: a whole 4x4x4 slice. The times are simulated.
128 devices in a mesh: tile: 32 (over z_hi, x, y), blk: 4 (over z_lo, core).
Axes of the slice: x: 4, y: 4, z: 4 (z_hi: 2, z_lo: 2; z = z_hi * 2 + z_lo), core: 2. Of those that a mesh axis runs over, the one named last changes fastest.
Arguments:
- image_tokens: bfloat16 [16, 1024, 1536], P(None, 'tile', 'blk'), may hold values from -10 to 10
- text_tokens: bfloat16 [16, 160, 1536], P(None, 'tile', 'blk'), may hold values from -10 to 10
- step_index: int32 [16], replicated, may hold values from 0 to 27
- text_length: int32 [16], replicated, may hold values from 1 to 160, as said below
- image_table: bfloat16 [28, 6, 1536], replicated, may hold values from -3 to 3
- text_table: bfloat16 [28, 3, 1536], replicated, may hold values from -3 to 3
- qkv_image: bfloat16 [1536, 3, 1536], P(None, None, 'blk'), may hold values from -0.15625 to 0.15625
- qkv_text: bfloat16 [1536, 3, 1536], P(None, None, 'blk'), may hold values from -0.15625 to 0.15625
- attn_out_image: bfloat16 [1536, 1536], P('blk'), may hold values from -0.15625 to 0.15625
- attn_out_text: bfloat16 [1536, 1536], P('blk'), may hold values from -0.15625 to 0.15625
- query_gain_image: float32 [64], replicated, may hold values from 1 to 12
- key_gain_image: float32 [64], replicated, may hold values from 1 to 12
- query_gain_text: float32 [64], replicated, may hold values from 1 to 12
- key_gain_text: float32 [64], replicated, may hold values from 1 to 12
- up_weight: bfloat16 [1536, 6144], P(None, 'blk'), may hold values from -0.15625 to 0.15625
- down_weight: bfloat16 [6144, 1536], P('blk'), may hold values from -0.078125 to 0.078125
Outputs:
- image_out: bfloat16 [16, 1024, 1536], P(None, 'tile', 'blk')
- text_out: bfloat16 [16, 160, 1536], P(None, 'tile', 'blk')
Inputs may be any that keep to these rules, and one draw needn't show every extreme that they name: `text_length`: some request has all 160 slots valid.
All inputs are finite; a program needn't handle non-finite values.
Results may differ from a plain program's by a relative error of at most 0.015.
The roundings to bfloat16 on the way count: a program that leaves them out, or rounds other values in their place, can miss the bound.
Values may be sent and summed in bfloat16 or wider, within the bound.
No kernel may reach another device: no remote copies, remote signals or barrier semaphores. Data moves between devices by JAX's collectives and lax.ppermute only.
A program may use at most 192 MiB of HBM per device.

v0:
```python
import jax
import jax.numpy as jnp
from jax import lax
from jax.sharding import PartitionSpec as P

HEAD_DIM = 64


masked_score = -1e30


def layer_norm(values):
    centre = jnp.mean(values, axis=-1, keepdims=True)
    spread = jnp.mean(jnp.square(values - centre), axis=-1, keepdims=True)
    return (values - centre) * lax.rsqrt(spread + 1e-06)


def modulate(normed, shift_rows, scale_rows):
    return (normed * (1.0 + scale_rows[:, None, :]) + shift_rows[:, None, :]).astype(jnp.bfloat16)


def lookup(table_rows, step_index):
    picker = (step_index[:, None] == jnp.arange(table_rows.shape[0])[None, :]).astype(
        table_rows.dtype
    )
    return jnp.einsum("rs,skd->rkd", picker, table_rows, preferred_element_type=jnp.float32)


def head_norm(values, gain_vector):
    inverse_rms = lax.rsqrt(jnp.mean(jnp.square(values), axis=-1, keepdims=True) + 1e-06)
    return (values * inverse_rms * gain_vector).astype(jnp.bfloat16)


def project_heads(activations, weight, gain_query, gain_key):
    projected = jnp.einsum("rsd,dke->rske", activations, weight, preferred_element_type=jnp.float32)
    split_shape = projected.shape[:2] + (projected.shape[3] // HEAD_DIM, HEAD_DIM)
    query_heads = head_norm(projected[:, :, 0].reshape(split_shape), gain_query)
    key_heads = head_norm(projected[:, :, 1].reshape(split_shape), gain_key)
    value_heads = projected[:, :, 2].reshape(split_shape).astype(jnp.bfloat16)
    return (query_heads, key_heads, value_heads)


def per_device(
    image_tokens,
    text_tokens,
    step_index,
    text_length,
    image_table,
    text_table,
    qkv_image,
    qkv_text,
    attn_out_image,
    attn_out_text,
    query_gain_image,
    key_gain_image,
    query_gain_text,
    key_gain_text,
    up_weight,
    down_weight,
):
    requests = image_tokens.shape[0]
    image_rows = image_tokens.shape[1]
    text_rows = text_tokens.shape[1]
    joint_rows = image_rows + text_rows
    part_width = image_tokens.shape[2]
    column_start = lax.axis_index("blk") * part_width
    scale_factor = HEAD_DIM ** (-0.5)
    image_mods = lookup(image_table, step_index)
    text_mods = lookup(text_table, step_index)
    image_local = lax.dynamic_slice_in_dim(image_mods, column_start, part_width, 2)
    text_local = lax.dynamic_slice_in_dim(text_mods, column_start, part_width, 2)
    image_float = image_tokens.astype(jnp.float32)
    text_float = text_tokens.astype(jnp.float32)
    image_whole, text_whole = (
        lax.all_gather(image_tokens, "blk", axis=2, tiled=True),
        lax.all_gather(text_tokens, "blk", axis=2, tiled=True),
    )
    image_acts = modulate(
        layer_norm(image_whole.astype(jnp.float32)), image_mods[:, 0], image_mods[:, 1]
    )
    text_acts = modulate(
        layer_norm(text_whole.astype(jnp.float32)), text_mods[:, 0], text_mods[:, 1]
    )
    image_q, image_k, image_v = project_heads(
        image_acts, qkv_image, query_gain_image, key_gain_image
    )
    text_q, text_k, text_v = project_heads(text_acts, qkv_text, query_gain_text, key_gain_text)
    joint_q = jnp.concatenate([image_q, text_q], axis=1)
    joint_k = jnp.concatenate([image_k, text_k], axis=1)
    joint_v = jnp.concatenate([image_v, text_v], axis=1)
    head_count = joint_q.shape[2]
    key_value = jnp.stack(
        [
            joint_k.reshape(requests, joint_rows, part_width),
            joint_v.reshape(requests, joint_rows, part_width),
        ],
        axis=2,
    )
    shard_piece = lax.all_gather(key_value, "tile", axis=1, tiled=True)
    running_max = jnp.full((requests, head_count, joint_rows, 1), masked_score, jnp.float32)
    piece_rows = shard_piece.shape[1]
    position = jnp.arange(piece_rows, dtype=jnp.int32)
    offset = position % joint_rows
    text_slot = position // joint_rows * text_rows + offset - image_rows
    visible = (offset < image_rows)[None, :] | (text_slot[None, :] < text_length[:, None])
    piece_keys = shard_piece[:, :, 0].reshape(requests, piece_rows, head_count, HEAD_DIM)
    piece_values = shard_piece[:, :, 1].reshape(requests, piece_rows, head_count, HEAD_DIM)
    scores = (
        jnp.einsum("rqhe,rkhe->rhqk", joint_q, piece_keys, preferred_element_type=jnp.float32)
        * scale_factor
    )
    visible_mask = visible[:, None, None, :]
    new_max = jnp.maximum(
        running_max, jnp.max(jnp.where(visible_mask, scores, masked_score), axis=-1, keepdims=True)
    )
    weights = jnp.where(visible_mask, jnp.exp(scores - new_max), 0.0)
    running_sum = jnp.sum(weights, axis=-1, keepdims=True)
    running_out = jnp.einsum(
        "rhqk,rkhe->rhqe",
        weights.astype(jnp.bfloat16),
        piece_values,
        preferred_element_type=jnp.float32,
    )
    attended = (
        jnp.transpose(running_out / running_sum, (0, 2, 1, 3))
        .astype(jnp.bfloat16)
        .reshape(requests, joint_rows, part_width)
    )
    image_term = jnp.einsum(
        "rsd,de->rse", attended[:, :image_rows], attn_out_image, preferred_element_type=jnp.float32
    )
    text_term = jnp.einsum(
        "rsd,de->rse", attended[:, image_rows:], attn_out_text, preferred_element_type=jnp.float32
    )
    image_proj, text_proj = (
        lax.psum_scatter(
            image_term.astype(jnp.bfloat16), "blk", scatter_dimension=2, tiled=True
        ).astype(jnp.float32),
        lax.psum_scatter(
            text_term.astype(jnp.bfloat16), "blk", scatter_dimension=2, tiled=True
        ).astype(jnp.float32),
    )
    image_mid = (image_float + image_local[:, 2][:, None, :] * image_proj).astype(jnp.bfloat16)
    text_out = (text_float + text_local[:, 2][:, None, :] * text_proj).astype(jnp.bfloat16)
    middle_float = image_mid.astype(jnp.float32)
    middle_whole = lax.all_gather(image_mid, "blk", axis=2, tiled=True)
    mlp_input = modulate(
        layer_norm(middle_whole.astype(jnp.float32)), image_mods[:, 3], image_mods[:, 4]
    )
    hidden = jax.nn.gelu(
        jnp.einsum("rsd,df->rsf", mlp_input, up_weight, preferred_element_type=jnp.float32),
        approximate=True,
    ).astype(jnp.bfloat16)
    down_term = jnp.einsum("rsf,fd->rsd", hidden, down_weight, preferred_element_type=jnp.float32)
    down_sum = lax.psum_scatter(
        down_term.astype(jnp.bfloat16), "blk", scatter_dimension=2, tiled=True
    ).astype(jnp.float32)
    image_out = (middle_float + image_local[:, 5][:, None, :] * down_sum).astype(jnp.bfloat16)
    return (image_out, text_out)


def solution(mesh):
    in_specs = (
        P(None, "tile", "blk"),
        P(None, "tile", "blk"),
        P(),
        P(),
        P(),
        P(),
        P(None, None, "blk"),
        P(None, None, "blk"),
        P("blk", None),
        P("blk", None),
        P(),
        P(),
        P(),
        P(),
        P(None, "blk"),
        P("blk", None),
    )
    out_specs = (P(None, "tile", "blk"), P(None, "tile", "blk"))
    return jax.shard_map(
        per_device, mesh=mesh, in_specs=in_specs, out_specs=out_specs, check_vma=False
    )
```

profile of v0, /device:TPU:0, one launch (start us, length us, event | category | flops | bytes accessed | tf_op | source)
XLA Modules:
  0.0 522.7 jit_solution(4415324707470170074)
XLA Ops:
  9.7 6.4 %all_gather.13 = bf16[16,5,1536]{2,0,1:T(8,128)(2,1)S(1)} all-gather(bf16[16,5,384]{2,0,1:T(8,128)(2,1)} %param.17), channel_id=1, replica_groups=mesh['tile'=32,'blk'=4] {'blk'}, dimensions={2}, use_global_device_ids=true | all-gather | bytes 307200 | tf_op jit(solution)/shard_map/all_gather | solution.py:76
  18.4 2.8 fusion.16
  34.8 2.2 all-gather.4.cloned.1.call-done
  37.0 1.8 convert_reduce_fusion.1
  38.8 2.0 fusion.24
  40.8 2.4 fusion.18
  48.3 1.8 fusion.115
  54.4 231.6 %all-gather.6.cloned.1.call-done = bf16[16,1184,2,384]{3,0,2,1:T(8,128)(2,1)} async-done(((bf16[16,37,2,384]{3,0,2,1:T(8,128)(2,1)}), bf16[16,1184,2,384]{3,0,2,1:T(8,128)(2,1)}) %all-gather.6.cloned.1.call-update) | async-done | bytes 29098000 | tf_op jit(solution)/shard_map/all_gather | solution.py:99
  286.0 21.9 %fusion.114 = (bf16[16,1184,1,384]{3,0,2,1:T(8,128)(2,1)}, bf16[16,1184,1,384]{3,0,2,1:T(8,128)(2,1)}) fusion(bf16[16,1184,2,384]{3,0,2,1:T(8,128)(2,1)} %all-gather.6.cloned.1.call-done), kind=kLoop, calls=%fused_computation.149 | loop fusion | bytes 58195968 | tf_op jit(solution)/shard_map/slice | solution.py:106
  307.9 20.2 %copy.78 = bf16[16,1184,1,384]{1,3,0,2:T(8,128)(2,1)} copy(bf16[16,1184,1,384]{3,0,2,1:T(8,128)(2,1)} %get-tuple-element.2) | data formatting | bytes 29097984
  328.1 12.2 %select_reduce_fusion = (f32[16,6,37]{2,1,0:T(8,128)S(1)}, f32[16,6,37,1184]{3,2,1,0:T(8,128)}) fusion(pred[16,1184]{1,0:T(8,128)(4,1)S(1)} %compare_or_fusion, bf16[16,1184,6,64]{1,3,2,0:T(8,128)(2,1)} %bitcast.109, bf16[16,5,6,64]{3,1,2,0:T(8,128)(2,1)S(1)} %fusion.79, bf16[16,32,6,64]{3,1,2,0:T(8,128)(2,1)S(1)} %fusion.50), kind=kOutput, calls=%fused_computation.1 | convolution fusion | flops 551835136 | bytes 31859072 | tf_op jit(solution)/shard_map/rqhe,rkhe->rhqk/dot_general | solution.py:109
  340.3 20.2 %copy.79 = bf16[16,1184,1,384]{1,3,0,2:T(8,128)(2,1)} copy(bf16[16,1184,1,384]{3,0,2,1:T(8,128)(2,1)} %get-tuple-element.3) | data formatting | bytes 29097984
  360.6 9.8 %fusion = f32[16,6,37]{2,1,0:T(8,128)S(1)} fusion(f32[16,6,37,1184]{3,2,1,0:T(8,128)} %get-tuple-element.17, f32[16,6,37]{2,1,0:T(8,128)S(1)} %broadcast_maximum_fusion, pred[16,1184]{1,0:T(8,128)(4,1)S(1)} %compare_or_fusion), kind=kLoop, calls=%fused_computation.2 | loop fusion | flops 16818720 | bytes 16869632 | tf_op jit(solution)/shard_map/reduce_sum | solution.py:117
  370.4 13.1 %fusion.43 = bf16[16,37,6,64]{3,1,2,0:T(8,128)(2,1)S(1)} fusion(bf16[16,1184,6,64]{1,3,2,0:T(8,128)(2,1)} %bitcast.112, f32[16,6,37,1184]{3,2,1,0:T(8,128)} %get-tuple-element.17, f32[16,6,37]{2,1,0:T(8,128)S(1)} %broadcast_maximum_fusion, pred[16,1184]{1,0:T(8,128)(4,1)S(1)} %compare_or_fusion, f32[16,37,6]{1,2,0:T(8,128)S(1)} %bitcast.117), kind=kOutput, calls=%fused_computation.47 | convolution fusion | flops 555589632 | bytes 31873280 | tf_op jit(solution)/shard_map/rhqk,rkhe->rhqe/dot_general | solution.py:118
  384.6 2.3 convolution_convert_fusion
  386.9 6.6 %copy.72 = bf16[16,32,1536]{1,0,2:T(8,128)(2,1)} copy(bf16[16,32,1536]{2,1,0:T(8,128)(2,1)S(1)} %convolution_convert_fusion) | data formatting | bytes 3145728
  393.5 9.3 %reshape.168 = bf16[1536,512]{1,0:T(8,128)(2,1)} reshape(bf16[1536,16,32]{2,1,0:T(8,128)(2,1)} %bitcast.110) | data formatting | bytes 3145728
  404.5 20.1 %reduce-scatter.10.cloned.1.call-done = bf16[384,512]{1,0:T(8,128)(2,1)} async-done(((bf16[1536,512]{1,0:T(8,128)(2,1)}), bf16[384,512]{1,0:T(8,128)(2,1)}) %reduce-scatter.10.cloned.1.call-update) | async-done | bytes 393232
  424.6 2.0 reshape.169
  430.4 2.4 copy.76
  432.8 2.4 reshape.172
  435.2 19.4 %all-gather.8.cloned.1.call-done = bf16[16,32,1536]{2,1,0:T(8,128)(2,1)} async-done(((bf16[16,32,384]{2,1,0:T(8,128)(2,1)}), bf16[16,32,1536]{2,1,0:T(8,128)(2,1)}) %all-gather.8.cloned.1.call-update) | async-done | bytes 1572880 | tf_op jit(solution)/shard_map/all_gather | solution.py:146
  456.4 2.0 fusion.20
  458.4 8.9 %fusion.37 = bf16[16,32,1536]{2,1,0:T(8,128)(2,1)S(1)} fusion(bf16[1536,1536]{1,0:T(8,128)(2,1)} %param.31, bf16[1536,1536]{1,0:T(8,128)(2,1)} %param.30, bf16[16,32,1536]{2,1,0:T(8,128)(2,1)S(1)} %copy-done.3, f32[16,1536]{1,0:T(8,128)S(1)} %copy-done.14, f32[16,1536]{1,0:T(8,128)S(1)} %copy-done.13, f32[16,32]{1,0:T(8,128)S(1)} %add_rsqrt_fusion.4, ...), kind=kOutput, calls=%fused_computation.41 | convolution fusion | flops 4844421120 | bytes 12783616 | tf_op jit(solution)/shard_map/rsf,fd->rsd/dot_general | solution.py:154
  467.3 6.6 %copy.74 = bf16[16,32,1536]{1,0,2:T(8,128)(2,1)} copy(bf16[16,32,1536]{2,1,0:T(8,128)(2,1)S(1)} %fusion.37) | data formatting | bytes 3145728
  474.0 9.3 %reshape.170 = bf16[1536,512]{1,0:T(8,128)(2,1)} reshape(bf16[1536,16,32]{2,1,0:T(8,128)(2,1)} %bitcast.111) | data formatting | bytes 3145728
  483.3 2.3 reshape.173
  485.6 2.1 copy.77
  489.2 19.2 %reduce-scatter.12.cloned.1.call-done = bf16[384,512]{1,0:T(8,128)(2,1)} async-done(((bf16[1536,512]{1,0:T(8,128)(2,1)}), bf16[384,512]{1,0:T(8,128)(2,1)}) %reduce-scatter.12.cloned.1.call-update) | async-done | bytes 393232
  508.4 2.9 reshape.171
  511.3 2.6 copy.75
  513.9 2.0 add_convert_fusion
  (116 shorter events, 37.3 us)
Async XLA Ops:
  7.2 33.6 %copy-start = (bf16[1536,3,384]{2,0,1:T(8,128)(2,1)S(1)}, bf16[1536,3,384]{2,0,1:T(8,128)(2,1)}, u32[]{:S(2)}) copy-start(bf16[1536,3,384]{2,0,1:T(8,128)(2,1)} %param.22) | copy-start | bytes 10616836
  7.2 29.8 %all-gather.4.cloned.1.call-start = ((), (), s32[]{:S(2)}) async-start(), calls=%async_computation.3 | async-start | bytes 1966080 | tf_op jit(solution)/shard_map/all_gather | solution.py:75
  7.9 278.1 %all-gather.6.cloned.1.call-start = ((), (), s32[]{:S(2)}) async-start(), calls=%async_computation.4 | async-start | bytes 30007296 | tf_op jit(solution)/shard_map/all_gather | solution.py:99
  17.6 0.7 copy-start.8
  18.4 13.5 %copy-start.17 = (s32[16]{0:T(128)S(1)}, s32[16]{0:T(128)}, u32[]{:S(2)}) copy-start(s32[16]{0:T(128)} %param.18) | copy-start | bytes 196
  21.2 0.8 copy-start.9
  33.2 0.8 copy-start.5
  37.0 3.8 copy-start.2
  37.0 3.8 copy-start.15
  37.0 3.8 copy-start.16
  43.3 1.5 copy-start.4
  46.9 3.2 copy-start.11
  48.3 1.9 copy-start.7
  48.3 1.9 copy-start.12
  50.2 1.6 copy-start.10
  50.2 2.1 copy-start.20
  50.2 2.3 copy-start.18
  51.5 373.1 %reduce-scatter.10.cloned.1.call-start = ((), (), s32[]{:S(2)}) async-start(), calls=%async_computation.6 | async-start | bytes 1966080
  52.3 1.6 copy-start.19
  402.8 25.0 %copy-start.6 = (bf16[16,32,384]{2,1,0:T(8,128)(2,1)S(1)}, bf16[16,32,384]{2,1,0:T(8,128)(2,1)}, u32[]{:S(2)}) copy-start(bf16[16,32,384]{2,1,0:T(8,128)(2,1)} %param.16) | copy-start | bytes 1179652
  402.8 51.8 %all-gather.8.cloned.1.call-start = ((), (), s32[]{:S(2)}) async-start(), calls=%async_computation.5 | async-start | bytes 1966080 | tf_op jit(solution)/shard_map/all_gather | solution.py:146
  428.7 54.6 %reduce-scatter.14.cloned.1.call-start = ((), (), s32[]{:S(2)}) async-start(), calls=%async_computation.8 | async-start | bytes 491520
  432.8 25.6 %copy-start.13 = (f32[16,1536]{1,0:T(8,128)S(1)}, f32[16,1536]{1,0:T(8,128)}, u32[]{:S(2)}) copy-start(f32[16,1536]{1,0:T(8,128)} %get-tuple-element.8) | copy-start | bytes 294916
  432.8 25.6 %copy-start.14 = (f32[16,1536]{1,0:T(8,128)S(1)}, f32[16,1536]{1,0:T(8,128)}, u32[]{:S(2)}) copy-start(f32[16,1536]{1,0:T(8,128)} %get-tuple-element.9) | copy-start | bytes 294916
  435.2 73.2 %reduce-scatter.12.cloned.1.call-start = ((), (), s32[]{:S(2)}) async-start(), calls=%async_computation.7 | async-start | bytes 1966080
  454.6 3.8 copy-start.3
  483.3 32.6 %copy-start.1 = (bf16[1536,3,384]{2,0,1:T(8,128)(2,1)S(1)}, bf16[1536,3,384]{2,0,1:T(8,128)(2,1)}, u32[]{:S(2)}) copy-start(bf16[1536,3,384]{2,0,1:T(8,128)(2,1)} %param.22) | copy-start | bytes 10616836
Sparse Core Ops, SparseCore 0:
  9.7 27.2 all-gather.3
  51.6 234.3 all-gather.5
  402.9 21.6 reduce-scatter.9
  428.8 25.7 all-gather.7
  456.9 18.6 reduce-scatter.13
  483.4 24.9 reduce-scatter.11
where the time goes:
time: 526 us; the launch traced here: 523 us
  waiting for transfers between devices  293 us (56%)
  local copies, waits for them, and re-layouts  130 us (25%)
  matrix products  45.9 us (9%)
  other arithmetic  32 us (6%)
  between operations  14.6 us (3%)
  blocking collectives  6.36 us (1%)
    all_gather x1, waiting for transfers between devices, per_device(): shard_piece = lax.all_gather(key_value, 'tile', axis=1, tiled=True)  232 us
    unnamed x56, local copies, waits for them, and re-layouts  92.3 us
    unnamed x9, waiting for transfers between devices  40.2 us
    slice x1, local copies, waits for them, and re-layouts, per_device(): shard_piece[:, :, 0].reshape(requests, piece_rows, head_count, HEAD_DIM)  21.9 us
    all_gather x1, waiting for transfers between devices, per_device(): middle_whole = lax.all_gather(image_mid, 'blk', axis=2, tiled=True)  19.4 us
    dot_general x1, matrix products, per_device(): jnp.einsum('rhqk,rkhe->rhqe', weights.astype(jnp.bfloat16), piece_values,...  13.1 us
    dot_general x1, matrix products, per_device(): jnp.einsum('rqhe,rkhe->rhqk', joint_q, piece_keys, preferred_element_type...  12.2 us
  transfers between devices with their start and end apart: 6, of which 5 were waited for; matrix products, arithmetic and copies ran while one was open for 12% of the time, Pallas kernels for 0%

commit v1 on v0

v1 whole, which is shorter than its diff:
```python
import functools

import jax
import jax.numpy as jnp
from jax import lax
from jax.experimental import pallas as pl
from jax.experimental.pallas import tpu as pltpu
from jax.sharding import PartitionSpec as P

HEAD_DIM = 64
BF = jnp.bfloat16
F32 = jnp.float32
HIDDEN_BIAS = -32768.0
TXT_PAD = 8
VMEM_LIMIT = 56 << 20


def dot(left, right):
    return jnp.dot(left, right, preferred_element_type=F32)


def dot_t(left, right):
    return lax.dot_general(left, right, (((1,), (1,)), ((), ())), preferred_element_type=F32)


def normed_acts(pieces, mods, shift_row, scale_row, width):
    total = sum(jnp.sum(piece, axis=-1, keepdims=True) for piece in pieces)
    centre = total * (1.0 / width)
    moved = [piece - centre for piece in pieces]
    spread = sum(jnp.sum(piece * piece, axis=-1, keepdims=True) for piece in moved) * (1.0 / width)
    inverse = lax.rsqrt(spread + 1e-06)
    return [
        (piece * inverse * (1.0 + mod[scale_row : scale_row + 1]) + mod[shift_row : shift_row + 1]).astype(BF)
        for piece, mod in zip(moved, mods)
    ]


def head_scale(values, group_ref):
    squares = values * values
    high = squares.astype(BF)
    low = (squares - high.astype(F32)).astype(BF)
    return lax.rsqrt(dot(high, group_ref[...]) + dot(low, group_ref[...]) + 1e-06)


def qkv_kernel(
    place_ref, x0, x1, x2, x3, imod_ref, tmod_ref, wimg_ref, wtxt_ref, gain_ref, group_ref,
    q_ref, kv_ref, acts_ref,
):
    step = pl.program_id(0)
    blk = place_ref[0]
    part = x0.shape[2]
    img_rows = x0.shape[0] * (x0.shape[1] - TXT_PAD)
    rows = x0.shape[0] * x0.shape[1]

    @pl.when(step == 0)
    def _():
        for text in (False, True):
            pieces, mods = [], []
            for j, ref in enumerate((x0, x1, x2, x3)):
                if text:
                    value = ref[:, ref.shape[1] - TXT_PAD :, :].astype(F32)
                    mods.append(tmod_ref[blk ^ j])
                else:
                    value = ref[:, : ref.shape[1] - TXT_PAD, :].astype(F32)
                    mods.append(imod_ref[blk ^ j])
                pieces.append(value.reshape(-1, part))
            acts = normed_acts(pieces, mods, 0, 1, 4 * part)
            for j in range(4):
                if text:
                    acts_ref[j, img_rows:rows, :] = acts[j]
                else:
                    acts_ref[j, :img_rows, :] = acts[j]

    def project(w_ref, start, stop):
        out = None
        for j in range(4):
            offset = pl.multiple_of((blk ^ j) * part, part)
            term = dot(acts_ref[j, start:stop, :], w_ref[0, pl.ds(offset, part), :])
            out = term if out is None else out + term
        return out

    for w_ref, start, stop, row in ((wimg_ref, 0, img_rows, 0), (wtxt_ref, img_rows, rows, 1)):
        values = project(w_ref, start, stop)

        @pl.when(step == 0)
        def _():
            kv_ref[0, start:stop, :] = (
                values * head_scale(values, group_ref) * gain_ref[2 + row : 3 + row, :]
            ).astype(BF)

        @pl.when(step == 1)
        def _():
            kv_ref[0, start:stop, :] = values.astype(BF)

        @pl.when(step == 2)
        def _():
            normed = (values * head_scale(values, group_ref) * gain_ref[row : row + 1, :]).astype(BF)
            q_ref[start:stop, :] = normed * BF(HEAD_DIM**-0.5)


def qkv_call(place, pieces, imod, tmod, wimg, wtxt, gains, group):
    sources, slot, part = pieces[0].shape
    rows = sources * slot
    width = 4 * part

    def whole(shape):
        return pl.BlockSpec(shape, lambda i, s: (0,) * len(shape))

    third = pl.BlockSpec((1, width, part), lambda i, s: ((i + 1) % 3, 0, 0))
    return pl.pallas_call(
        qkv_kernel,
        out_shape=(
            jax.ShapeDtypeStruct((rows, part), BF),
            jax.ShapeDtypeStruct((2, rows, part), BF),
        ),
        grid_spec=pltpu.PrefetchScalarGridSpec(
            num_scalar_prefetch=1,
            grid=(3,),
            in_specs=[whole(pieces[0].shape)] * 4
            + [whole(imod.shape), whole(tmod.shape), third, third, whole(gains.shape), whole(group.shape)],
            out_specs=(
                whole((rows, part)),
                pl.BlockSpec((1, rows, part), lambda i, s: (jnp.minimum(i, 1), 0, 0)),
            ),
            scratch_shapes=[pltpu.VMEM((4, rows, part), BF)],
        ),
        compiler_params=pltpu.CompilerParams(
            dimension_semantics=("arbitrary",), vmem_limit_bytes=VMEM_LIMIT
        ),
        cost_estimate=pl.CostEstimate(
            flops=2 * rows * width * part * 3, transcendentals=0, bytes_accessed=9 << 20
        ),
        name="qkv",
    )(place, *pieces, imod, tmod, wimg, wtxt, gains, group)


def key_bias(place_ref, rows, img_rows, other):
    row = lax.broadcasted_iota(jnp.int32, (rows, 128), 0)
    inner = row - img_rows
    source = inner >> 3
    slot = inner & 7
    parity = place_ref[1] ^ other
    tile = (source >> 2) * 8 + parity * 4 + (source & 3)
    seen = (inner < 0) | ((slot < 5) & (tile * 5 + slot < place_ref[2]))
    return jnp.where(seen, 0.0, HIDDEN_BIAS).astype(BF)


def attend_kernel(place_ref, q_ref, kv_ref, ko_ref, wimg_ref, wtxt_ref, out_ref, att_ref):
    blk = place_ref[0]
    rows, part = q_ref.shape
    img_rows = rows // 5 * 4
    pairs = part // 128
    lane = lax.broadcasted_iota(jnp.int32, (rows, 128), 1)
    one_lane = jnp.where(lane == 0, 1.0, 0.0).astype(BF)
    ones = jnp.ones((rows, 128), BF)
    biases = [key_bias(place_ref, rows, img_rows, other) for other in (0, 1)]
    half = rows // 2
    for pair in range(pairs):
        cols = slice(pair * 128, pair * 128 + 128)
        keys = [
            jnp.concatenate([ref[0, :, cols], bias], axis=1)
            for ref, bias in zip((kv_ref, ko_ref), biases)
        ]
        vals = [jnp.concatenate([ref[1, :, cols], ones], axis=1) for ref in (kv_ref, ko_ref)]
        query = q_ref[:, cols]
        for piece in range(2):
            span = slice(piece * half, piece * half + half)
            outs = []
            for head in range(2):
                mine = (lane[span] < 64) if head == 0 else (lane[span] >= 64)
                masked = jnp.where(mine, query[span], BF(0.0))
                left = jnp.concatenate([masked, one_lane[span]], axis=1)
                scores = [dot_t(left, key) for key in keys]
                top = jnp.maximum(
                    jnp.max(scores[0], axis=-1, keepdims=True),
                    jnp.max(scores[1], axis=-1, keepdims=True),
                )
                weights = [jnp.exp(score - top).astype(BF) for score in scores]
                both = dot(weights[0], vals[0]) + dot(weights[1], vals[1])
                outs.append(both[:, :128] / both[:, 128:])
            att_ref[span, cols] = jnp.where(lane[span] < 64, outs[0], outs[1]).astype(BF)
    for j in range(4):
        offset = pl.multiple_of((blk ^ j) * part, part)
        out_ref[j, :img_rows, :] = dot(att_ref[:img_rows, :], wimg_ref[:, pl.ds(offset, part)]).astype(BF)
        out_ref[j, img_rows:, :] = dot(att_ref[img_rows:, :], wtxt_ref[:, pl.ds(offset, part)]).astype(BF)


def attend_call(place, query, mine, other, wimg, wtxt):
    rows, part = query.shape

    def whole(shape):
        return pl.BlockSpec(shape, lambda i, s: (0,) * len(shape))

    return pl.pallas_call(
        attend_kernel,
        out_shape=jax.ShapeDtypeStruct((4, rows, part), BF),
        grid_spec=pltpu.PrefetchScalarGridSpec(
            num_scalar_prefetch=1,
            grid=(1,),
            in_specs=[whole(a.shape) for a in (query, mine, other, wimg, wtxt)],
            out_specs=whole((4, rows, part)),
            scratch_shapes=[pltpu.VMEM((rows, part), BF)],
        ),
        compiler_params=pltpu.CompilerParams(
            dimension_semantics=("arbitrary",), vmem_limit_bytes=VMEM_LIMIT
        ),
        cost_estimate=pl.CostEstimate(
            flops=4 * rows * rows * 2 * 6 * 256, transcendentals=rows * rows * 12, bytes_accessed=6 << 20
        ),
        name="attend",
    )(place, query, mine, other, wimg, wtxt)


def mlp_kernel(place_ref, x0, x1, x2, x3, imod_ref, up_ref, down_ref, out_ref, acts_ref, sum_ref):
    step = pl.program_id(0)
    blk = place_ref[0]
    part = x0.shape[1]

    @pl.when(step == 0)
    def _():
        pieces = [ref[...].astype(F32) for ref in (x0, x1, x2, x3)]
        mods = [imod_ref[blk ^ j] for j in range(4)]
        for j, value in enumerate(normed_acts(pieces, mods, 3, 4, 4 * part)):
            acts_ref[j] = value

    hidden = None
    for j in range(4):
        offset = pl.multiple_of((blk ^ j) * part, part)
        term = dot(acts_ref[j], up_ref[pl.ds(offset, part), :])
        hidden = term if hidden is None else hidden + term
    hidden = jax.nn.gelu(hidden, approximate=True).astype(BF)
    last = pl.num_programs(0) - 1
    for j in range(4):
        offset = pl.multiple_of((blk ^ j) * part, part)
        term = dot(hidden, down_ref[:, pl.ds(offset, part)])

        @pl.when(step == 0)
        def _():
            sum_ref[j] = term

        @pl.when((step > 0) & (step < last))
        def _():
            sum_ref[j] += term

        @pl.when(step == last)
        def _():
            out_ref[j] = (sum_ref[j] + term).astype(BF)


def mlp_call(place, pieces, imod, up, down):
    rows, part = pieces[0].shape
    width = 4 * part
    steps = 4
    span = up.shape[1] // steps

    def whole(shape):
        return pl.BlockSpec(shape, lambda i, s: (0,) * len(shape))

    return pl.pallas_call(
        mlp_kernel,
        out_shape=jax.ShapeDtypeStruct((4, rows, part), BF),
        grid_spec=pltpu.PrefetchScalarGridSpec(
            num_scalar_prefetch=1,
            grid=(steps,),
            in_specs=[whole((rows, part))] * 4
            + [
                whole(imod.shape),
                pl.BlockSpec((width, span), lambda i, s: (0, i)),
                pl.BlockSpec((span, width), lambda i, s: (i, 0)),
            ],
            out_specs=whole((4, rows, part)),
            scratch_shapes=[pltpu.VMEM((4, rows, part), BF), pltpu.VMEM((4, rows, part), F32)],
        ),
        compiler_params=pltpu.CompilerParams(
            dimension_semantics=("arbitrary",), vmem_limit_bytes=VMEM_LIMIT
        ),
        cost_estimate=pl.CostEstimate(
            flops=4 * rows * width * up.shape[1], transcendentals=rows * up.shape[1], bytes_accessed=12 << 20
        ),
        name="mlp",
    )(place, *pieces, imod, up, down)


def swap(values, axis, size, bit):
    return lax.ppermute(values, axis, [(i, i ^ bit) for i in range(size)])


def per_device(
    tiles,
    image_tokens,
    text_tokens,
    step_index,
    text_length,
    image_table,
    text_table,
    qkv_image,
    qkv_text,
    attn_out_image,
    attn_out_text,
    query_gain_image,
    key_gain_image,
    query_gain_text,
    key_gain_text,
    up_weight,
    down_weight,
):
    requests, image_rows, part = image_tokens.shape
    text_rows = text_tokens.shape[1]
    tile = lax.axis_index("tile")
    blk = lax.axis_index("blk")
    groups = [[t for t in range(tiles) if (t >> 2) & 1 == p] for p in (0, 1)]
    parity = (tile >> 2) & 1
    request = (tile >> 3) * 4 + (tile & 3)
    place = jnp.stack([blk, parity, text_length[request]]).astype(jnp.int32)

    step = step_index[request]
    imod = lax.dynamic_index_in_dim(image_table, step, 0, keepdims=False).astype(F32)
    tmod = lax.dynamic_index_in_dim(text_table, step, 0, keepdims=False).astype(F32)
    imod = jnp.transpose(imod.reshape(6, 4, part), (1, 0, 2))
    tmod = jnp.transpose(tmod.reshape(3, 4, part), (1, 0, 2))
    imod_own = lax.dynamic_index_in_dim(imod, blk, 0, keepdims=False)
    tmod_own = lax.dynamic_index_in_dim(tmod, blk, 0, keepdims=False)

    packed = jnp.concatenate(
        [image_tokens, jnp.pad(text_tokens, ((0, 0), (0, TXT_PAD - text_rows), (0, 0)))], axis=1
    )
    own = lax.all_to_all(packed, "tile", 0, 0, axis_index_groups=groups, tiled=True)
    far = swap(own, "blk", 4, 2)
    near = swap(own, "blk", 4, 1)
    diag = swap(far, "blk", 4, 1)

    wimg = jnp.transpose(qkv_image, (1, 0, 2))
    wtxt = jnp.transpose(qkv_text, (1, 0, 2))
    heads = part // HEAD_DIM
    gains = jnp.stack(
        [jnp.tile(g, heads) for g in (query_gain_image, query_gain_text, key_gain_image, key_gain_text)]
    )
    index = jnp.arange(part) // HEAD_DIM
    group = jnp.where(index[:, None] == index[None, :], 1.0 / HEAD_DIM, 0.0).astype(BF)

    query, mine = qkv_call(place, [own, near, far, diag], imod, tmod, wimg, wtxt, gains, group)
    other = swap(mine, "tile", tiles, 4)
    terms = attend_call(place, query, mine, other, attn_out_image, attn_out_text)

    def scatter(blocks):
        came = swap(jnp.stack([blocks[1], blocks[3]]), "blk", 4, 1)
        away = (blocks[2].astype(F32) + came[1].astype(F32)).astype(BF)
        back = swap(away, "blk", 4, 2)
        return blocks[0].astype(F32) + came[0].astype(F32) + back.astype(F32)

    proj = scatter(terms)
    img_rows = requests * image_rows
    image_own = own[:, :image_rows].reshape(img_rows, part)
    text_own = own[:, image_rows:].reshape(requests * TXT_PAD, part)
    image_mid = (image_own.astype(F32) + imod_own[2:3] * proj[:img_rows]).astype(BF)
    text_out = (text_own.astype(F32) + tmod_own[2:3] * proj[img_rows:]).astype(BF)
    mid_far = swap(image_mid, "blk", 4, 2)
    mid_near = swap(image_mid, "blk", 4, 1)
    mid_diag = swap(mid_far, "blk", 4, 1)
    downs = mlp_call(place, [image_mid, mid_near, mid_far, mid_diag], imod, up_weight, down_weight)
    image_out = (image_mid.astype(F32) + imod_own[5:6] * scatter(downs)).astype(BF)

    result = jnp.concatenate(
        [image_out.reshape(requests, image_rows, part), text_out.reshape(requests, TXT_PAD, part)], axis=1
    )
    result = lax.all_to_all(result, "tile", 0, 0, axis_index_groups=groups, tiled=True)
    return (result[:, :image_rows], result[:, image_rows : image_rows + text_rows])


def solution(mesh):
    in_specs = (
        P(None, "tile", "blk"),
        P(None, "tile", "blk"),
        P(),
        P(),
        P(),
        P(),
        P(None, None, "blk"),
        P(None, None, "blk"),
        P("blk", None),
        P("blk", None),
        P(),
        P(),
        P(),
        P(),
        P(None, "blk"),
        P("blk", None),
    )
    out_specs = (P(None, "tile", "blk"), P(None, "tile", "blk"))
    return jax.shard_map(
        functools.partial(per_device, mesh.shape["tile"]),
        mesh=mesh,
        in_specs=in_specs,
        out_specs=out_specs,
        check_vma=False,
    )
```

time: 526 us -> 186 us (0.35)
  waiting for transfers between devices: 293 us -> 72.2 us
  local copies, waits for them, and re-layouts: 130 us -> 9.39 us
  matrix products: 45.9 us -> 0 us
  Pallas kernels: 0 us -> 43.1 us
  blocking collectives: 6.36 us -> 40.3 us
  other arithmetic: 32 us -> 12.9 us
  between operations: 14.6 us -> 2.86 us
    all_gather x3 -> x0, waiting for transfers between devices: 253 us -> none  [the longest x1 232 us: per_device(): shard_piece = lax.all_gather(key_value, 'tile', axis=1, tiled=True)]
    unnamed x56 -> x46, local copies, waits for them, and re-layouts: 92.3 us -> 4.22 us
    ppermute x0 -> x11, waiting for transfers between devices: none -> 72.2 us  [swap(): return lax.ppermute(values, axis, [(i, i ^ bit) for i in range(size)])]
    dot_general x9 -> x0, matrix products: 45.9 us -> none  [the longest x1 13.1 us: per_device(): jnp.einsum('rhqk,rkhe->rhqe', weights.astype(jnp.bfloat16), piece_values,...]
    pallas_call x0 -> x3, Pallas kernels: none -> 43.1 us  [the longest x1 18.1 us: mlp_call(): pl.pallas_call(mlp_kernel, out_shape=jax.ShapeDtypeStruct((4, rows, part)...]
    all_to_all x0 -> x2, blocking collectives: none -> 40.3 us  [the longest x1 24.1 us: per_device(): lax.all_to_all(packed, 'tile', 0, 0, axis_index_groups=groups, tiled=True)]
    unnamed x9 -> x0, waiting for transfers between devices: 40.2 us -> none
    reduce_sum x11 -> x0, other arithmetic: 20.8 us -> none  [the longest x1 9.82 us: per_device(): running_sum = jnp.sum(weights, axis=-1, keepdims=True)]
  transfers between devices with their start and end apart: 6 -> 11, of which waited for: 5 -> 8; matrix products, arithmetic and copies ran while one was open for 12% -> 4% of each run, Pallas kernels for 0% -> 0%
where the time goes in v1:
time: 186 us
  waiting for transfers between devices  72.2 us (39%)
  Pallas kernels  43.1 us (23%)
  blocking collectives  40.3 us (22%)
  other arithmetic  12.9 us (7%)
  local copies, waits for them, and re-layouts  9.39 us (5%)
  starting transfers between devices  5.09 us (3%)
  between operations  2.86 us (2%)
    ppermute x11, waiting for transfers between devices, swap(): return lax.ppermute(values, axis, [(i, i ^ bit) for i in range(size)])  72.2 us
    all_to_all x1, blocking collectives, per_device(): lax.all_to_all(packed, 'tile', 0, 0, axis_index_groups=groups, tiled=True)  24.1 us
    pallas_call x1, Pallas kernels, mlp_call(): pl.pallas_call(mlp_kernel, out_shape=jax.ShapeDtypeStruct((4, rows, part)...  18.1 us
    all_to_all x1, blocking collectives, per_device(): lax.all_to_all(result, 'tile', 0, 0, axis_index_groups=groups, tiled=True)  16.2 us
    pallas_call x1, Pallas kernels, attend_call(): pl.pallas_call(attend_kernel, out_shape=jax.ShapeDtypeStruct((4, rows, pa...  12.6 us
    pallas_call x1, Pallas kernels, qkv_call(): pl.pallas_call(qkv_kernel, out_shape=(jax.ShapeDtypeStruct((rows, part),...  12.4 us
    ppermute x11, starting transfers between devices, swap(): return lax.ppermute(values, axis, [(i, i ^ bit) for i in range(size)])  5.09 us
    unnamed x46, local copies, waits for them, and re-layouts  4.22 us
  transfers between devices with their start and end apart: 11, of which 8 were waited for; matrix products, arithmetic and copies ran while one was open for 4% of the time, Pallas kernels for 0%

profile of v1, /device:TPU:0, one launch (start us, length us, event | category | flops | bytes accessed | tf_op | source)
XLA Modules:
  0.0 185.8 jit_solution(5707721649889782903)
XLA Ops:
  0.7 0.9 copy.28
  1.6 1.1 fusion.6
  2.6 24.1 %all_to_all.10.x0 = bf16[16,40,384]{2,1,0:T(8,128)(2,1)S(1)} all-to-all(bf16[16,40,384]{2,1,0:T(8,128)(2,1)S(1)} %fusion.6), channel_id=1, replica_groups={{0,4,8,12,32,36,40,44,64,68,72,76,96,100,104,108},{16,20,24,28,48,52,56..., dimensions={0} | all-to-all | bytes 983040 | tf_op jit(solution)/shard_map/all_to_all | solution.py:327
  26.7 1.0 collective-permute-start.1
  28.3 9.9 %collective-permute-done.1.x2 = bf16[16,40,384]{2,1,0:T(8,128)(2,1)S(1)} collective-permute-done((bf16[16,40,384]{2,1,0:T(8,128)(2,1)S(1)}, bf16[16,40,384]{2,1,0:T(8,128)(2,1)S(1)}, u32[]{:S(2)}, u32[]{:S(2)}) %collective-permute-start.1) | collective-permute-done | bytes 491552 | tf_op jit(solution)/shard_map/ppermute | solution.py:285
  38.2 1.2 pad_add_fusion.place_ref
  42.3 1.6 convert_reduce_fusion.1
  43.9 1.6 convert_reduce_fusion
  46.2 0.8 select_convert_fusion.group_ref
  47.9 12.4 %qkv.1 = (bf16[640,384]{1,0:T(8,128)(2,1)}, bf16[2,640,384]{2,1,0:T(8,128)(2,1)}) custom-call(s32[3]{0:T(128)} %pad_add_fusion.place_ref, bf16[16,40,384]{2,1,0:T(8,128)(2,1)} %copy-done, bf16[16,40,384]{2,1,0:T(8,128)(2,1)} %copy-done.8, bf16[16,40,384]{2,1,0:T(8,128)(2,1)} %copy-done.7, bf16[16,40,384]{2,1,0:T(8,128)(2,1)} %copy-done.9, ...), custom_call_target="tpu_custom_call" | custom-call | flops 2264924160 | bytes 9437184 | tf_op jit(solution)/shard_map/qkv/pallas_call | solution.py:110
  60.9 23.8 %collective-permute-done.3.ko_ref = bf16[2,640,384]{2,1,0:T(8,128)(2,1)S(1)} collective-permute-done((bf16[2,640,384]{2,1,0:T(8,128)(2,1)}, bf16[2,640,384]{2,1,0:T(8,128)(2,1)S(1)}, u32[]{:S(2)}, u32[]{:S(2)}) %collective-permute-start.3) | collective-permute-done | bytes 983072 | tf_op jit(solution)/shard_map/ppermute | solution.py:285
  84.7 1.0 copy-done.16
  85.7 12.6 %attend.1 = bf16[4,640,384]{2,1,0:T(8,128)(2,1)} custom-call(s32[3]{0:T(128)} %pad_add_fusion.place_ref, bf16[640,384]{1,0:T(8,128)(2,1)} %get-tuple-element.4.q_ref, bf16[2,640,384]{2,1,0:T(8,128)(2,1)} %get-tuple-element.5.kv_ref, bf16[2,640,384]{2,1,0:T(8,128)(2,1)} %copy-done.16, bf16[384,1536]{1,0:T(8,128)(2,1)} %wimg_ref.1, bf16[384,1536]{1,0:T(8,128)(2,1)} %wtxt_ref.1), custom_call_target="tpu_custom_call" | custom-call | flops 5033164800 | bytes 6291456 | tf_op jit(solution)/shard_map/attend/pallas_call | solution.py:194
  98.3 1.4 fusion.15
  99.9 2.6 %collective-permute-done.4 = bf16[2,640,384]{2,1,0:T(8,128)(2,1)S(1)} collective-permute-done((bf16[2,640,384]{2,1,0:T(8,128)(2,1)S(1)}, bf16[2,640,384]{2,1,0:T(8,128)(2,1)S(1)}, u32[]{:S(2)}, u32[]{:S(2)}) %collective-permute-start.4) | collective-permute-done | bytes 983072 | tf_op jit(solution)/shard_map/ppermute | solution.py:285
  102.5 1.0 fusion.7
  103.5 1.0 collective-permute-start.5
  104.7 12.4 %collective-permute-done.5 = bf16[640,384]{1,0:T(8,128)(2,1)} collective-permute-done((bf16[640,384]{1,0:T(8,128)(2,1)}, bf16[640,384]{1,0:T(8,128)(2,1)}, u32[]{:S(2)}, u32[]{:S(2)}) %collective-permute-start.5) | collective-permute-done | bytes 491552 | tf_op jit(solution)/shard_map/ppermute | solution.py:285
  117.1 1.3 bitcast_add_fusion
  118.6 1.1 collective-permute-start.7
  119.7 9.3 %collective-permute-done.7.x2 = bf16[512,384]{1,0:T(8,128)(2,1)S(1)} collective-permute-done((bf16[512,384]{1,0:T(8,128)(2,1)S(1)}, bf16[512,384]{1,0:T(8,128)(2,1)S(1)}, u32[]{:S(2)}, u32[]{:S(2)}) %collective-permute-start.7) | collective-permute-done | bytes 393248 | tf_op jit(solution)/shard_map/ppermute | solution.py:285
  129.0 1.7 collective-permute-done.8.x3
  131.5 18.1 %mlp.1 = bf16[4,512,384]{2,1,0:T(8,128)(2,1)} custom-call(s32[3]{0:T(128)} %pad_add_fusion.place_ref, bf16[512,384]{1,0:T(8,128)(2,1)} %copy-done.4, bf16[512,384]{1,0:T(8,128)(2,1)} %copy-done.18, bf16[512,384]{1,0:T(8,128)(2,1)} %copy-done.17, bf16[512,384]{1,0:T(8,128)(2,1)} %copy-done.19, f32[4,6,384]{2,1,0:T(8,128)} %bitcast.44, ...), custom_call_target="tpu_custom_call" | custom-call | flops 4831838208 | bytes 12582912 | tf_op jit(solution)/shard_map/mlp/pallas_call | solution.py:259
  149.6 1.3 fusion.16
  150.9 1.0 pad_maximum_fusion.1
  152.0 2.5 %collective-permute-done.9 = bf16[2,512,384]{2,1,0:T(8,128)(2,1)} collective-permute-done((bf16[2,512,384]{2,1,0:T(8,128)(2,1)}, bf16[2,512,384]{2,1,0:T(8,128)(2,1)}, u32[]{:S(2)}, u32[]{:S(2)}) %collective-permute-start.9) | collective-permute-done | bytes 786464 | tf_op jit(solution)/shard_map/ppermute | solution.py:285
  154.5 1.1 fusion.8
  155.6 1.1 collective-permute-start.10
  156.8 10.1 %collective-permute-done.10 = bf16[512,384]{1,0:T(8,128)(2,1)S(1)} collective-permute-done((bf16[512,384]{1,0:T(8,128)(2,1)S(1)}, bf16[512,384]{1,0:T(8,128)(2,1)S(1)}, u32[]{:S(2)}, u32[]{:S(2)}) %collective-permute-start.10) | collective-permute-done | bytes 393248 | tf_op jit(solution)/shard_map/ppermute | solution.py:285
  166.9 1.2 fusion.5
  168.1 16.2 %all_to_all.11 = bf16[16,40,384]{2,1,0:T(8,128)(2,1)S(1)} all-to-all(bf16[16,40,384]{2,1,0:T(8,128)(2,1)S(1)} %pad_maximum_fusion.2), channel_id=1, replica_groups={{0,4,8,12,32,36,40,44,64,68,72,76,96,100,104,108},{16,20,24,28,48,52,56..., dimensions={0} | all-to-all | bytes 983040 | tf_op jit(solution)/shard_map/all_to_all | solution.py:366
  185.0 0.8 slice.106
  (78 shorter events, 5.8 us)
Async XLA Ops:
  0.6 27.1 %copy-start.20 = (s32[16]{0:T(128)S(1)}, s32[16]{0:T(128)}, u32[]{:S(2)}) copy-start(s32[16]{0:T(128)} %param.19) | copy-start | bytes 196
  0.6 38.8 %copy-start.21 = (s32[16]{0:T(128)S(1)}, s32[16]{0:T(128)}, u32[]{:S(2)}) copy-start(s32[16]{0:T(128)} %param.18) | copy-start | bytes 196
  0.7 40.7 %copy-start.12 = (f32[64]{0:T(128)S(1)}, f32[64]{0:T(128)}, u32[]{:S(2)}) copy-start(f32[64]{0:T(128)} %param.29) | copy-start | bytes 772
  0.7 40.8 %copy-start.13 = (f32[64]{0:T(128)S(1)}, f32[64]{0:T(128)}, u32[]{:S(2)}) copy-start(f32[64]{0:T(128)} %param.27) | copy-start | bytes 772
  0.7 40.8 %copy-start.14 = (f32[64]{0:T(128)S(1)}, f32[64]{0:T(128)}, u32[]{:S(2)}) copy-start(f32[64]{0:T(128)} %param.28) | copy-start | bytes 772
  0.7 40.9 %copy-start.15 = (f32[64]{0:T(128)S(1)}, f32[64]{0:T(128)}, u32[]{:S(2)}) copy-start(f32[64]{0:T(128)} %param.26) | copy-start | bytes 772
  26.7 20.3 %copy-start = (bf16[16,40,384]{2,1,0:T(8,128)(2,1)}, bf16[16,40,384]{2,1,0:T(8,128)(2,1)S(1)}, u32[]{:S(2)}) copy-start(bf16[16,40,384]{2,1,0:T(8,128)(2,1)S(1)} %all_to_all.10.x0) | copy-start | bytes 1474564
  26.7 11.5 %collective-permute-start.1 = (bf16[16,40,384]{2,1,0:T(8,128)(2,1)S(1)}, bf16[16,40,384]{2,1,0:T(8,128)(2,1)S(1)}, u32[]{:S(2)}, u32[]{:S(2)}) collective-permute-start(bf16[16,40,384]{2,1,0:T(8,128)(2,1)S(1)} %all_to_all.10.x0), channel_id=1, source_target_pairs={{0,2},{1,3},{2,0},{3,1},{4,6},{5,7},{6,4},{7,5},{8,10},{9,11},{10,... | collective-permute-start | bytes 1474568 | tf_op jit(solution)/shard_map/ppermute | solution.py:285
  28.3 18.7 %collective-permute-start = (bf16[16,40,384]{2,1,0:T(8,128)(2,1)S(1)}, bf16[16,40,384]{2,1,0:T(8,128)(2,1)S(1)}, u32[]{:S(2)}, u32[]{:S(2)}) collective-permute-start(bf16[16,40,384]{2,1,0:T(8,128)(2,1)S(1)} %all_to_all.10.x0), channel_id=1, source_target_pairs={{0,1},{1,0},{2,3},{3,2},{4,5},{5,4},{6,7},{7,6},{8,9},{9,8},{10,11... | collective-permute-start | bytes 1474568 | tf_op jit(solution)/shard_map/ppermute | solution.py:285
  38.2 8.8 %copy-start.7 = (bf16[16,40,384]{2,1,0:T(8,128)(2,1)}, bf16[16,40,384]{2,1,0:T(8,128)(2,1)S(1)}, u32[]{:S(2)}) copy-start(bf16[16,40,384]{2,1,0:T(8,128)(2,1)S(1)} %collective-permute-done.1.x2) | copy-start | bytes 1474564
  38.2 8.8 %collective-permute-start.2 = (bf16[16,40,384]{2,1,0:T(8,128)(2,1)S(1)}, bf16[16,40,384]{2,1,0:T(8,128)(2,1)S(1)}, u32[]{:S(2)}, u32[]{:S(2)}) collective-permute-start(bf16[16,40,384]{2,1,0:T(8,128)(2,1)S(1)} %collective-permute-done.1.x2), channel_id=1, source_target_pairs={{0,1},{1,0},{2,3},{3,2},{4,5},{5,4},{6,7},{7,6},{8,9},{9,8},{10,11... | collective-permute-start | bytes 1474568 | tf_op jit(solution)/shard_map/ppermute | solution.py:285
  47.0 0.8 copy-start.8
  47.0 0.9 copy-start.9
  60.3 24.4 %collective-permute-start.3 = (bf16[2,640,384]{2,1,0:T(8,128)(2,1)}, bf16[2,640,384]{2,1,0:T(8,128)(2,1)S(1)}, u32[]{:S(2)}, u32[]{:S(2)}) collective-permute-start(bf16[2,640,384]{2,1,0:T(8,128)(2,1)} %get-tuple-element.5.kv_ref), channel_id=1, source_target_pairs={{0,16},{4,20},{8,24},{12,28},{16,0},{20,4},{24,8},{28,12},{32,48},... | collective-permute-start | bytes 2949128 | tf_op jit(solution)/shard_map/ppermute | solution.py:285
  84.7 1.0 copy-start.16
  98.3 4.2 %copy-start.2 = (bf16[4,640,384]{2,1,0:T(8,128)(2,1)S(1)}, bf16[4,640,384]{2,1,0:T(8,128)(2,1)}, u32[]{:S(2)}) copy-start(bf16[4,640,384]{2,1,0:T(8,128)(2,1)} %attend.1) | copy-start | bytes 5898244
  99.7 4.8 %copy-start.10 = (f32[6,1536]{1,0:T(8,128)S(1)}, f32[6,1536]{1,0:T(8,128)}, u32[]{:S(2)}) copy-start(f32[6,1536]{1,0:T(8,128)} %convert_reduce_fusion) | copy-start | bytes 110596
  99.7 4.9 %copy-start.1 = (bf16[16,40,384]{2,1,0:T(8,128)(2,1)S(1)}, bf16[16,40,384]{2,1,0:T(8,128)(2,1)}, u32[]{:S(2)}) copy-start(bf16[16,40,384]{2,1,0:T(8,128)(2,1)} %copy-done) | copy-start | bytes 1474564
  99.8 2.6 %collective-permute-start.4 = (bf16[2,640,384]{2,1,0:T(8,128)(2,1)S(1)}, bf16[2,640,384]{2,1,0:T(8,128)(2,1)S(1)}, u32[]{:S(2)}, u32[]{:S(2)}) collective-permute-start(bf16[2,640,384]{2,1,0:T(8,128)(2,1)S(1)} %pad_maximum_fusion), channel_id=1, source_target_pairs={{0,1},{1,0},{2,3},{3,2},{4,5},{5,4},{6,7},{7,6},{8,9},{9,8},{10,11... | collective-permute-start | bytes 2949128 | tf_op jit(solution)/shard_map/ppermute | solution.py:285
  102.5 2.2 %copy-start.6 = (bf16[2,640,384]{2,1,0:T(8,128)(2,1)}, bf16[2,640,384]{2,1,0:T(8,128)(2,1)S(1)}, u32[]{:S(2)}) copy-start(bf16[2,640,384]{2,1,0:T(8,128)(2,1)S(1)} %collective-permute-done.4) | copy-start | bytes 2949124
  103.5 13.6 %collective-permute-start.5 = (bf16[640,384]{1,0:T(8,128)(2,1)}, bf16[640,384]{1,0:T(8,128)(2,1)}, u32[]{:S(2)}, u32[]{:S(2)}) collective-permute-start(bf16[640,384]{1,0:T(8,128)(2,1)} %fusion.7), channel_id=1, source_target_pairs={{0,2},{1,3},{2,0},{3,1},{4,6},{5,7},{6,4},{7,5},{8,10},{9,11},{10,... | collective-permute-start | bytes 1474568 | tf_op jit(solution)/shard_map/ppermute | solution.py:285
  118.6 12.1 %copy-start.4 = (bf16[512,384]{1,0:T(8,128)(2,1)}, bf16[512,384]{1,0:T(8,128)(2,1)S(1)}, u32[]{:S(2)}) copy-start(bf16[512,384]{1,0:T(8,128)(2,1)S(1)} %fusion.2.x0) | copy-start | bytes 1179652
  118.6 10.4 %collective-permute-start.7 = (bf16[512,384]{1,0:T(8,128)(2,1)S(1)}, bf16[512,384]{1,0:T(8,128)(2,1)S(1)}, u32[]{:S(2)}, u32[]{:S(2)}) collective-permute-start(bf16[512,384]{1,0:T(8,128)(2,1)S(1)} %fusion.2.x0), channel_id=1, source_target_pairs={{0,2},{1,3},{2,0},{3,1},{4,6},{5,7},{6,4},{7,5},{8,10},{9,11},{10,... | collective-permute-start | bytes 1179656 | tf_op jit(solution)/shard_map/ppermute | solution.py:285
  119.7 9.3 %collective-permute-start.6 = (bf16[512,384]{1,0:T(8,128)(2,1)S(1)}, bf16[512,384]{1,0:T(8,128)(2,1)S(1)}, u32[]{:S(2)}, u32[]{:S(2)}) collective-permute-start(bf16[512,384]{1,0:T(8,128)(2,1)S(1)} %fusion.2.x0), channel_id=1, source_target_pairs={{0,1},{1,0},{2,3},{3,2},{4,5},{5,4},{6,7},{7,6},{8,9},{9,8},{10,11... | collective-permute-start | bytes 1179656 | tf_op jit(solution)/shard_map/ppermute | solution.py:285
  129.0 1.7 copy-start.17
  129.0 1.7 collective-permute-start.8
  129.0 1.7 copy-start.18
  149.6 2.4 %copy-start.11 = (f32[3,1536]{1,0:T(4,128)S(1)}, f32[3,1536]{1,0:T(4,128)}, u32[]{:S(2)}) copy-start(f32[3,1536]{1,0:T(4,128)} %convert_reduce_fusion.1) | copy-start | bytes 55300
  149.6 4.9 %copy-start.3 = (bf16[4,512,384]{2,1,0:T(8,128)(2,1)S(1)}, bf16[4,512,384]{2,1,0:T(8,128)(2,1)}, u32[]{:S(2)}) copy-start(bf16[4,512,384]{2,1,0:T(8,128)(2,1)} %mlp.1) | copy-start | bytes 4718596
  150.9 16.0 %copy-start.5 = (bf16[512,384]{1,0:T(8,128)(2,1)S(1)}, bf16[512,384]{1,0:T(8,128)(2,1)}, u32[]{:S(2)}) copy-start(bf16[512,384]{1,0:T(8,128)(2,1)} %copy-done.4) | copy-start | bytes 1179652
  151.9 2.6 %collective-permute-start.9 = (bf16[2,512,384]{2,1,0:T(8,128)(2,1)}, bf16[2,512,384]{2,1,0:T(8,128)(2,1)}, u32[]{:S(2)}, u32[]{:S(2)}) collective-permute-start(bf16[2,512,384]{2,1,0:T(8,128)(2,1)} %pad_maximum_fusion.1), channel_id=1, source_target_pairs={{0,1},{1,0},{2,3},{3,2},{4,5},{5,4},{6,7},{7,6},{8,9},{9,8},{10,11... | collective-permute-start | bytes 2359304 | tf_op jit(solution)/shard_map/ppermute | solution.py:285
  155.6 11.2 %collective-permute-start.10 = (bf16[512,384]{1,0:T(8,128)(2,1)S(1)}, bf16[512,384]{1,0:T(8,128)(2,1)S(1)}, u32[]{:S(2)}, u32[]{:S(2)}) collective-permute-start(bf16[512,384]{1,0:T(8,128)(2,1)S(1)} %fusion.8), channel_id=1, source_target_pairs={{0,2},{1,3},{2,0},{3,1},{4,6},{5,7},{6,4},{7,5},{8,10},{9,11},{10,... | collective-permute-start | bytes 1179656 | tf_op jit(solution)/shard_map/ppermute | solution.py:285
  (1 other events, 0.8 us)

commit v2 on v0

v2 whole, which is shorter than its diff:
```python
import functools

import jax
import jax.numpy as jnp
from jax import lax
from jax.experimental import pallas as pl
from jax.experimental.pallas import tpu as pltpu
from jax.sharding import PartitionSpec as P

HEAD_DIM = 64
BF = jnp.bfloat16
F32 = jnp.float32
HIDDEN_BIAS = -32768.0
TXT_PAD = 8
VMEM_LIMIT = 24 << 20
VM = pl.BlockSpec(memory_space=pltpu.VMEM)
SM = pl.BlockSpec(memory_space=pltpu.SMEM)


def dot(left, right):
    return jnp.dot(left, right, preferred_element_type=F32)


def dot_t(left, right):
    return lax.dot_general(left, right, (((1,), (1,)), ((), ())), preferred_element_type=F32)


def my_request():
    tile = lax.axis_index("tile")
    return (tile >> 2) * 2 + (tile & 1)


def table_rows(table_ref, step, rows):
    plane = table_ref[rows[0]]
    here = lax.broadcasted_iota(jnp.int32, plane.shape, 0) == step
    return [
        jnp.sum(jnp.where(here, table_ref[row].astype(F32), 0.0), axis=0, keepdims=True) for row in rows
    ]


def norm_rows(raw_ref, acts_ref, start, count, shift, scale, block=32):
    width = raw_ref.shape[1]
    gain = 1.0 + scale

    def body(i, carry):
        rows = pl.ds(pl.multiple_of(start + i * block, block), block)
        values = raw_ref[rows, :].astype(F32)
        centre = jnp.sum(values, axis=-1, keepdims=True) * (1.0 / width)
        moved = values - centre
        spread = jnp.sum(moved * moved, axis=-1, keepdims=True) * (1.0 / width)
        acts_ref[rows, :] = (moved * lax.rsqrt(spread + 1e-06) * gain + shift).astype(BF)
        return carry

    lax.fori_loop(0, count // block, body, 0, unroll=2)


def head_scale(values, group):
    parts = []
    for col in range(0, values.shape[1], 128):
        piece = values[:, col : col + 128]
        squares = piece * piece
        high = squares.astype(BF)
        low = (squares - high.astype(F32)).astype(BF)
        parts.append(dot(jnp.concatenate([high, low], axis=1), group))
    return lax.rsqrt(jnp.concatenate(parts, axis=1) + 1e-06)


def group_matrix():
    row = lax.broadcasted_iota(jnp.int32, (256, 128), 0)
    col = lax.broadcasted_iota(jnp.int32, (256, 128), 1)
    same = ((row & 127) >> 6) == (col >> 6)
    return jnp.where(same, 1.0 / HEAD_DIM, 0.0).astype(BF)


def wide_gain(ref, width):
    pair = jnp.concatenate([ref[...], ref[...]], axis=1)
    return jnp.concatenate([pair] * (width // 128), axis=1)


def qkv_kernel(first, sources, with_query, *refs):
    step_ref, x0, x1, x2, x3, itab, ttab, wimg, wtxt, gqi, gki, gqt, gkt = refs[:13]
    outs, (raw_ref, acts_ref) = refs[13:-2], refs[-2:]
    blk = lax.axis_index("blk")
    step = step_ref[my_request()]
    part = x0.shape[2]
    image_rows = x0.shape[1] - TXT_PAD
    img, txt = sources * image_rows, sources * TXT_PAD
    for j, (ref, begin) in enumerate(zip((x0, x1, x2, x3), first)):
        cols = pl.ds(pl.multiple_of((blk ^ j) * part, part), part)
        raw_ref[:img, cols] = ref[begin : begin + sources, :image_rows, :].reshape(img, part)
        text = ref[begin : begin + sources, image_rows:, :].astype(F32).reshape(txt, part)
        raw_ref[img:, cols] = text.astype(BF)
    shift, scale = table_rows(itab, step, (0, 1))
    norm_rows(raw_ref, acts_ref, 0, img, shift, scale)
    shift, scale = table_rows(ttab, step, (0, 1))
    norm_rows(raw_ref, acts_ref, img, txt, shift, scale)
    group = group_matrix()
    kv_ref = outs[-1]
    for w_ref, begin, end, query_gain, key_gain in (
        (wtxt, img, img + txt, gqt, gkt),
        (wimg, 0, img, gqi, gki),
    ):
        acts = acts_ref[begin:end, :]
        values = dot(acts, w_ref[1])
        kv_ref[0, begin:end, :] = (values * head_scale(values, group) * wide_gain(key_gain, part)).astype(BF)
        kv_ref[1, begin:end, :] = dot(acts, w_ref[2]).astype(BF)
        if with_query:
            values = dot(acts, w_ref[0])
            normed = (values * head_scale(values, group) * wide_gain(query_gain, part)).astype(BF)
            outs[0][begin:end, :] = normed * BF(HEAD_DIM**-0.5)


def qkv_call(step_index, pieces, first, sources, tables, weights, gains, with_query):
    part = pieces[0].shape[2]
    rows = sources * pieces[0].shape[1]
    outs = [jax.ShapeDtypeStruct((2, rows, part), BF)]
    if with_query:
        outs = [jax.ShapeDtypeStruct((rows, part), BF)] + outs
    return pl.pallas_call(
        functools.partial(qkv_kernel, first, sources, with_query),
        out_shape=outs,
        in_specs=[SM] + [VM] * 12,
        out_specs=[VM] * len(outs),
        scratch_shapes=[pltpu.VMEM((rows, 4 * part), BF), pltpu.VMEM((rows, 4 * part), BF)],
        compiler_params=pltpu.CompilerParams(vmem_limit_bytes=VMEM_LIMIT),
        cost_estimate=pl.CostEstimate(
            flops=rows * 6000000, transcendentals=0, bytes_accessed=rows * 4096
        ),
        name="qkv",
    )(step_index, *pieces, *tables, *weights, *gains)


def key_bias(length, rows, img_rows, parity, source_start):
    inner = lax.broadcasted_iota(jnp.int32, (rows - img_rows, 128), 0)
    source = (inner >> 3) + source_start
    slot = inner & 7
    tile = (source >> 1) * 4 + parity * 2 + (source & 1)
    seen = (slot < 5) & (tile * 5 + slot < length)
    return jnp.concatenate(
        [jnp.zeros((img_rows, 128), F32), jnp.where(seen, 0.0, HIDDEN_BIAS)], axis=0
    ).astype(BF)


def store_blocks(value, pair, odd, keep_ref, send_ref):
    part = keep_ref.shape[2]
    low, high = value[:, :part].astype(BF), value[:, part:].astype(BF)

    @pl.when(odd == 0)
    def _():
        keep_ref[pair] = low
        send_ref[pair] = high

    @pl.when(odd == 1)
    def _():
        keep_ref[pair] = high
        send_ref[pair] = low


def attend_kernel(start, count, gate_row, *refs):
    step_ref, length_ref, q_ref, kv_ref, ka_ref, kb_ref, table, w_ref, keep_ref, send_ref = refs
    blk = lax.axis_index("blk")
    parity = (lax.axis_index("tile") >> 1) & 1
    request = my_request()
    step, length = step_ref[request], length_ref[request]
    part = q_ref.shape[1]
    lane = lax.broadcasted_iota(jnp.int32, (count, 128), 1)
    one_lane = jnp.where(lane == 0, 1.0, 0.0).astype(BF)
    key_refs = (kv_ref, ka_ref, kb_ref)
    biases = []
    for ref, side, source in zip(key_refs, (0, 1, 1), (0, 0, 8)):
        rows = ref.shape[1]
        biases.append(key_bias(length, rows, rows // 5 * 4, parity ^ side, source))
    att = []
    for col in range(0, part, 128):
        cols = slice(col, col + 128)
        keys = [jnp.concatenate([ref[0, :, cols], bias], axis=1) for ref, bias in zip(key_refs, biases)]
        vals = [
            jnp.concatenate([ref[1, :, cols], jnp.ones((ref.shape[1], 128), BF)], axis=1) for ref in key_refs
        ]
        query = q_ref[start : start + count, cols]
        outs = []
        for head in range(2):
            mine = (lane < 64) if head == 0 else (lane >= 64)
            left = jnp.concatenate([jnp.where(mine, query, BF(0.0)), one_lane], axis=1)
            scores = [dot_t(left, key) for key in keys]
            tops = [jnp.max(score, axis=-1, keepdims=True) for score in scores]
            top = functools.reduce(jnp.maximum, tops)
            both = sum(dot(jnp.exp(score - top).astype(BF), val) for score, val in zip(scores, vals))
            outs.append(both[:, :128] / both[:, 128:])
        att.append(jnp.where(lane < 64, outs[0], outs[1]).astype(BF))
    att = jnp.concatenate(att, axis=1)
    gate = table_rows(table, step, (gate_row,))[0]
    project_out(att, gate, w_ref, blk, keep_ref, send_ref)


def project_out(left, gate, w_ref, blk, keep_ref, send_ref):
    part = keep_ref.shape[2]
    for pair in range(2):
        which = (blk >> 1) ^ pair
        value = dot(left, w_ref[:, pl.ds(pl.multiple_of(which * 2 * part, 2 * part), 2 * part)])
        width = gate.shape[1]
        mine = jnp.where(which == 0, gate[:, : width // 2], gate[:, width // 2 :])
        store_blocks(value * mine, pair, blk & 1, keep_ref, send_ref)


def attend_call(step_index, lengths, query, keys, start, count, table, gate_row, weight):
    part = query.shape[1]
    shape = jax.ShapeDtypeStruct((2, count, part), BF)
    return pl.pallas_call(
        functools.partial(attend_kernel, start, count, gate_row),
        out_shape=[shape, shape],
        in_specs=[SM, SM] + [VM] * 6,
        out_specs=[VM, VM],
        compiler_params=pltpu.CompilerParams(vmem_limit_bytes=VMEM_LIMIT),
        cost_estimate=pl.CostEstimate(
            flops=count * 16000000, transcendentals=0, bytes_accessed=count * 4096
        ),
        name="attend",
    )(step_index, lengths, query, *keys, table, weight)


def mlp_kernel(step_ref, x0, x1, x2, x3, table, up_ref, down_ref, keep_ref, send_ref, raw_ref, acts_ref):
    blk = lax.axis_index("blk")
    step = step_ref[my_request()]
    rows, part = x0.shape
    for j, ref in enumerate((x0, x1, x2, x3)):
        raw_ref[:, pl.ds(pl.multiple_of((blk ^ j) * part, part), part)] = ref[...]
    shift, scale, gate = table_rows(table, step, (3, 4, 5))
    norm_rows(raw_ref, acts_ref, 0, rows, shift, scale)
    for col in range(0, up_ref.shape[1], 512):
        hidden = dot(acts_ref[...], up_ref[:, col : col + 512])
        raw_ref[:, col : col + 512] = jax.nn.gelu(hidden, approximate=True).astype(BF)
    project_out(raw_ref[...], gate, down_ref, blk, keep_ref, send_ref)


def mlp_call(step_index, pieces, table, up, down):
    rows, part = pieces[0].shape
    shape = jax.ShapeDtypeStruct((2, rows, part), BF)
    return pl.pallas_call(
        mlp_kernel,
        out_shape=[shape, shape],
        in_specs=[SM] + [VM] * 7,
        out_specs=[VM, VM],
        scratch_shapes=[pltpu.VMEM((rows, 4 * part), BF), pltpu.VMEM((rows, 4 * part), BF)],
        compiler_params=pltpu.CompilerParams(vmem_limit_bytes=VMEM_LIMIT),
        cost_estimate=pl.CostEstimate(
            flops=rows * 16000000, transcendentals=0, bytes_accessed=rows * 4096
        ),
        name="mlp",
    )(step_index, *pieces, table, up, down)


def swap(values, axis, size, bit):
    return lax.ppermute(values, axis, [(i, i ^ bit) for i in range(size)])


def add(*terms):
    return sum(term.astype(F32) for term in terms).astype(BF)


def per_device(
    tiles,
    image_tokens,
    text_tokens,
    step_index,
    text_length,
    image_table,
    text_table,
    qkv_image,
    qkv_text,
    attn_out_image,
    attn_out_text,
    query_gain_image,
    key_gain_image,
    query_gain_text,
    key_gain_text,
    up_weight,
    down_weight,
):
    requests, image_rows, part = image_tokens.shape
    text_rows = text_tokens.shape[1]
    half = requests // 2
    groups = [[t for t in range(tiles) if (t >> 1) & 1 == p] for p in (0, 1)]
    tables = [jnp.transpose(table, (1, 0, 2)) for table in (image_table, text_table)]
    weights = [jnp.transpose(weight, (1, 0, 2)) for weight in (qkv_image, qkv_text)]
    gains = [
        gain.reshape(1, HEAD_DIM)
        for gain in (query_gain_image, key_gain_image, query_gain_text, key_gain_text)
    ]

    packed = jnp.concatenate(
        [image_tokens, jnp.pad(text_tokens, ((0, 0), (0, TXT_PAD - text_rows), (0, 0)))], axis=1
    )
    own = lax.all_to_all(packed, "tile", 0, 0, axis_index_groups=groups, tiled=True)
    far = swap(own, "blk", 4, 2)
    other = swap(own, "tile", tiles, 2)
    near = swap(own, "blk", 4, 1)
    diag = swap(far, "blk", 4, 1)
    other_far = [swap(other[c * half : c * half + half], "blk", 4, 2) for c in range(2)]
    other_near = swap(other, "blk", 4, 1)

    query, mine = qkv_call(
        step_index, [own, near, far, diag], (0, 0, 0, 0), requests, tables, weights, gains, True
    )
    keys = [mine]
    for c in range(2):
        other_diag = swap(other_far[c], "blk", 4, 1)
        begin = c * half
        keys += qkv_call(
            step_index, [other, other_near, other_far[c], other_diag], (begin, begin, 0, 0), half,
            tables, weights, gains, False,
        )

    def attend(start, count, table, weight):
        return attend_call(step_index, text_length, query, keys, start, count, table, 2, weight)

    def scatter(keep, send):
        came = swap(send, "blk", 4, 1)
        back = swap(add(keep[1], came[1]), "blk", 4, 2)
        return keep[0], came[0], back

    img_rows = requests * image_rows
    chunk = img_rows // 2
    mids, downs = [], []
    shares = [attend(c * chunk, chunk, tables[0], attn_out_image) for c in range(2)]
    text_share = attend(img_rows, requests * TXT_PAD, tables[1], attn_out_text)
    for c in range(2):
        start = own[c * half : c * half + half, :image_rows].reshape(chunk, part)
        mids.append(add(start, *scatter(*shares[c])))
    text_own = own[:, image_rows:].reshape(requests * TXT_PAD, part)
    text_out = add(text_own, *scatter(*text_share))
    for mid in mids:
        mid_far = swap(mid, "blk", 4, 2)
        mid_near = swap(mid, "blk", 4, 1)
        mid_diag = swap(mid_far, "blk", 4, 1)
        downs.append(
            mlp_call(step_index, [mid, mid_near, mid_far, mid_diag], tables[0], up_weight, down_weight)
        )
    image_out = [add(mid, *scatter(*down)) for mid, down in zip(mids, downs)]

    result = jnp.concatenate(
        [
            jnp.concatenate(image_out, axis=0).reshape(requests, image_rows, part),
            text_out.reshape(requests, TXT_PAD, part),
        ],
        axis=1,
    )
    result = lax.all_to_all(result, "tile", 0, 0, axis_index_groups=groups, tiled=True)
    return (result[:, :image_rows], result[:, image_rows : image_rows + text_rows])


def solution(mesh):
    in_specs = (
        P(None, "tile", "blk"),
        P(None, "tile", "blk"),
        P(),
        P(),
        P(),
        P(),
        P(None, None, "blk"),
        P(None, None, "blk"),
        P("blk", None),
        P("blk", None),
        P(),
        P(),
        P(),
        P(),
        P(None, "blk"),
        P("blk", None),
    )
    out_specs = (P(None, "tile", "blk"), P(None, "tile", "blk"))
    return jax.shard_map(
        functools.partial(per_device, mesh.shape["tile"]),
        mesh=mesh,
        in_specs=in_specs,
        out_specs=out_specs,
        check_vma=False,
    )
```

time: 526 us -> 142 us (0.27)
  waiting for transfers between devices: 293 us -> 40.8 us
  local copies, waits for them, and re-layouts: 130 us -> 5.67 us
  matrix products: 45.9 us -> 0 us
  Pallas kernels: 0 us -> 39.7 us
  other arithmetic: 32 us -> 2.08 us
  blocking collectives: 6.36 us -> 35.3 us
  starting transfers between devices: 0.64 us -> 16.7 us
  between operations: 14.6 us -> 1.13 us
    all_gather x3 -> x0, waiting for transfers between devices: 253 us -> none  [the longest x1 232 us: per_device(): shard_piece = lax.all_gather(key_value, 'tile', axis=1, tiled=True)]
    unnamed x56 -> x38, local copies, waits for them, and re-layouts: 92.3 us -> 4.78 us
    dot_general x9 -> x0, matrix products: 45.9 us -> none  [the longest x1 13.1 us: per_device(): jnp.einsum('rhqk,rkhe->rhqe', weights.astype(jnp.bfloat16), piece_values,...]
    ppermute x0 -> x25, waiting for transfers between devices: none -> 40.8 us  [swap(): return lax.ppermute(values, axis, [(i, i ^ bit) for i in range(size)])]
    unnamed x9 -> x0, waiting for transfers between devices: 40.2 us -> none
    pallas_call x0 -> x8, Pallas kernels: none -> 39.7 us  [the longest x3 14.9 us: attend_call(): pl.pallas_call(functools.partial(attend_kernel, start, count, gate_row),...]
    all_to_all x0 -> x2, blocking collectives: none -> 35.3 us  [the longest x1 20.3 us: per_device(): lax.all_to_all(packed, 'tile', 0, 0, axis_index_groups=groups, tiled=True)]
    slice x5 -> x4, local copies, waits for them, and re-layouts: 23.5 us -> 0.89 us  [the longest x1 0.79 us: per_device(): result[:, :image_rows]]
  transfers between devices with their start and end apart: 6 -> 25, of which waited for: 5 -> 10; matrix products, arithmetic and copies ran while one was open for 12% -> 1% of each run, Pallas kernels for 0% -> 19%
where the time goes in v2:
time: 142 us; the launch traced here: 141 us
  waiting for transfers between devices  40.8 us (29%)
  Pallas kernels  39.7 us (28%)
  blocking collectives  35.3 us (25%)
  starting transfers between devices  16.7 us (12%)
  local copies, waits for them, and re-layouts  5.67 us (4%)
  other arithmetic  2.08 us (1%)
    ppermute x25, waiting for transfers between devices, swap(): return lax.ppermute(values, axis, [(i, i ^ bit) for i in range(size)])  40.8 us
    all_to_all x1, blocking collectives, per_device(): lax.all_to_all(packed, 'tile', 0, 0, axis_index_groups=groups, tiled=True)  20.3 us
    ppermute x25, starting transfers between devices, swap(): return lax.ppermute(values, axis, [(i, i ^ bit) for i in range(size)])  16.7 us
    all_to_all x1, blocking collectives, per_device(): lax.all_to_all(result, 'tile', 0, 0, axis_index_groups=groups, tiled=True)  15 us
    pallas_call x3, Pallas kernels, attend_call(): pl.pallas_call(functools.partial(attend_kernel, start, count, gate_row),...  14.9 us
    pallas_call x3, Pallas kernels, qkv_call(): pl.pallas_call(functools.partial(qkv_kernel, first, sources, with_query),...  14.7 us
    pallas_call x2, Pallas kernels, mlp_call(): pl.pallas_call(mlp_kernel, out_shape=[shape, shape], in_specs=[SM] + [VM]...  10.1 us
    unnamed x38, local copies, waits for them, and re-layouts  4.78 us
  transfers between devices with their start and end apart: 25, of which 10 were waited for; matrix products, arithmetic and copies ran while one was open for 1% of the time, Pallas kernels for 19%

profile of v2, /device:TPU:0, one launch (start us, length us, event | category | flops | bytes accessed | tf_op | source)
XLA Modules:
  0.0 141.3 jit_solution(13064617446300851963)
XLA Ops:
  1.7 1.2 fusion.1
  2.9 20.3 %all_to_all.10.refs_1_ = bf16[16,40,384]{2,1,0:T(8,128)(2,1)S(1)} all-to-all(bf16[16,40,384]{2,1,0:T(8,128)(2,1)S(1)} %fusion.1), channel_id=1, replica_groups={{0,4,16,20,32,36,48,52,64,68,80,84,96,100,112,116},{8,12,24,28,40,44,56..., dimensions={0} | all-to-all | bytes 983040 | tf_op jit(solution)/shard_map/all_to_all | solution.py:294
  23.2 2.9 %collective-permute-start.3 = (bf16[16,40,384]{2,1,0:T(8,128)(2,1)S(1)}, bf16[16,40,384]{2,1,0:T(8,128)(2,1)S(1)}, u32[]{:S(2)}, u32[]{:S(2)}) collective-permute-start(bf16[16,40,384]{2,1,0:T(8,128)(2,1)S(1)} %all_to_all.10.refs_1_), channel_id=1, source_target_pairs={{0,8},{4,12},{8,0},{12,4},{16,24},{20,28},{24,16},{28,20},{32,40},... | collective-permute-start | bytes 1474568 | tf_op jit(solution)/shard_map/ppermute | solution.py:254
  26.1 1.0 collective-permute-start.1
  27.1 8.9 %collective-permute-done.3.refs_1_ = bf16[16,40,384]{2,1,0:T(8,128)(2,1)S(1)} collective-permute-done((bf16[16,40,384]{2,1,0:T(8,128)(2,1)S(1)}, bf16[16,40,384]{2,1,0:T(8,128)(2,1)S(1)}, u32[]{:S(2)}, u32[]{:S(2)}) %collective-permute-start.3) | collective-permute-done | bytes 491552 | tf_op jit(solution)/shard_map/ppermute | solution.py:254
  36.0 1.1 collective-permute-start.5
  38.1 6.4 %collective-permute-done.5.refs_3_ = bf16[8,40,384]{2,1,0:T(8,128)(2,1)S(1)} collective-permute-done((bf16[8,40,384]{2,1,0:T(8,128)(2,1)S(1)}, bf16[8,40,384]{2,1,0:T(8,128)(2,1)S(1)}, u32[]{:S(2)}, u32[]{:S(2)}) %collective-permute-start.5) | collective-permute-done | bytes 245792 | tf_op jit(solution)/shard_map/ppermute | solution.py:254
  45.1 2.6 %collective-permute-done.7.refs_3_ = bf16[8,40,384]{2,1,0:T(8,128)(2,1)S(1)} collective-permute-done((bf16[8,40,384]{2,1,0:T(8,128)(2,1)S(1)}, bf16[8,40,384]{2,1,0:T(8,128)(2,1)S(1)}, u32[]{:S(2)}, u32[]{:S(2)}) %collective-permute-start.7) | collective-permute-done | bytes 245792 | tf_op jit(solution)/shard_map/ppermute | solution.py:254
  47.8 2.0 %copy-done.1 = bf16[1536,3,384]{2,0,1:T(8,128)(2,1)S(1)} copy-done((bf16[1536,3,384]{2,0,1:T(8,128)(2,1)S(1)}, bf16[1536,3,384]{2,0,1:T(8,128)(2,1)}, u32[]{:S(2)}) %copy-start.1) | copy-done | bytes 3538968
  49.8 1.1 copy-done.3
  50.8 3.6 %qkv.4.refs_4_ = bf16[2,320,384]{2,1,0:T(8,128)(2,1)S(1)} custom-call(s32[16]{0:T(128)S(1)} %copy-done.10, bf16[16,40,384]{2,1,0:T(8,128)(2,1)S(1)} %collective-permute-done.3.refs_1_, bf16[16,40,384]{2,1,0:T(8,128)(2,1)S(1)} %collective-permute-done.4.refs_2_, bf16[8,40,384]{2,1,0:T(8,128)(2,1)S(1)} %collective-permute-done.5.refs_3_, ...), custom_call_target="tpu_custom_call" | custom-call | flops 1920000000 | bytes 1310720 | tf_op jit(solution)/shard_map/qkv/pallas_call | solution.py:119
  54.5 3.7 %qkv.5.refs_5_ = bf16[2,320,384]{2,1,0:T(8,128)(2,1)S(1)} custom-call(s32[16]{0:T(128)S(1)} %copy-done.10, bf16[16,40,384]{2,1,0:T(8,128)(2,1)S(1)} %collective-permute-done.3.refs_1_, bf16[16,40,384]{2,1,0:T(8,128)(2,1)S(1)} %collective-permute-done.4.refs_2_, bf16[8,40,384]{2,1,0:T(8,128)(2,1)S(1)} %collective-permute-done.7.refs_3_, ...), custom_call_target="tpu_custom_call" | custom-call | flops 1920000000 | bytes 1310720 | tf_op jit(solution)/shard_map/qkv/pallas_call | solution.py:119
  58.3 7.4 %qkv.3 = (bf16[640,384]{1,0:T(8,128)(2,1)S(1)}, bf16[2,640,384]{2,1,0:T(8,128)(2,1)S(1)}) custom-call(s32[16]{0:T(128)S(1)} %copy-done.10, bf16[16,40,384]{2,1,0:T(8,128)(2,1)S(1)} %all_to_all.10.refs_1_, bf16[16,40,384]{2,1,0:T(8,128)(2,1)S(1)} %collective-permute-done.refs_2_, bf16[16,40,384]{2,1,0:T(8,128)(2,1)S(1)} %collective-permute-done.1.refs_3_, ...), custom_call_target="tpu_custom_call" | custom-call | flops 3840000000 | bytes 2621440 | tf_op jit(solution)/shard_map/qkv/pallas_call | solution.py:119
  65.7 5.3 %attend.4 = (bf16[2,256,384]{2,1,0:T(8,128)(2,1)S(1)}, bf16[2,256,384]{2,1,0:T(8,128)(2,1)S(1)}) custom-call(s32[16]{0:T(128)S(1)} %copy-done.10, s32[16]{0:T(128)S(1)} %copy-done.13, bf16[640,384]{1,0:T(8,128)(2,1)S(1)} %get-tuple-element.14.refs_2_, bf16[2,640,384]{2,1,0:T(8,128)(2,1)S(1)} %get-tuple-element.15.refs_3_, ...), custom_call_target="tpu_custom_call" | custom-call | flops 4096000000 | bytes 1048576 | tf_op jit(solution)/shard_map/attend/pallas_call | solution.py:209
  71.6 5.1 %attend.3 = (bf16[2,256,384]{2,1,0:T(8,128)(2,1)S(1)}, bf16[2,256,384]{2,1,0:T(8,128)(2,1)S(1)}) custom-call(s32[16]{0:T(128)S(1)} %copy-done.10, s32[16]{0:T(128)S(1)} %copy-done.13, bf16[640,384]{1,0:T(8,128)(2,1)S(1)} %get-tuple-element.14.refs_2_, bf16[2,640,384]{2,1,0:T(8,128)(2,1)S(1)} %get-tuple-element.15.refs_3_, ...), custom_call_target="tpu_custom_call" | custom-call | flops 4096000000 | bytes 1048576 | tf_op jit(solution)/shard_map/attend/pallas_call | solution.py:209
  76.9 4.5 %attend.5 = (bf16[2,128,384]{2,1,0:T(8,128)(2,1)S(1)}, bf16[2,128,384]{2,1,0:T(8,128)(2,1)S(1)}) custom-call(s32[16]{0:T(128)S(1)} %copy-done.10, s32[16]{0:T(128)S(1)} %copy-done.13, bf16[640,384]{1,0:T(8,128)(2,1)S(1)} %get-tuple-element.14.refs_2_, bf16[2,640,384]{2,1,0:T(8,128)(2,1)S(1)} %get-tuple-element.15.refs_3_, ...), custom_call_target="tpu_custom_call" | custom-call | flops 2048000000 | bytes 524288 | tf_op jit(solution)/shard_map/attend/pallas_call | solution.py:209
  82.0 1.1 collective-permute-start.17
  83.2 1.1 collective-permute-start.10
  84.2 5.6 %collective-permute-done.17 = bf16[256,384]{1,0:T(8,128)(2,1)S(1)} collective-permute-done((bf16[256,384]{1,0:T(8,128)(2,1)S(1)}, bf16[256,384]{1,0:T(8,128)(2,1)S(1)}, u32[]{:S(2)}, u32[]{:S(2)}) %collective-permute-start.17) | collective-permute-done | bytes 196640 | tf_op jit(solution)/shard_map/ppermute | solution.py:254
  90.0 1.1 collective-permute-start.19
  91.2 1.9 %collective-permute-done.10 = bf16[256,384]{1,0:T(8,128)(2,1)S(1)} collective-permute-done((bf16[256,384]{1,0:T(8,128)(2,1)S(1)}, bf16[256,384]{1,0:T(8,128)(2,1)S(1)}, u32[]{:S(2)}, u32[]{:S(2)}) %collective-permute-start.10) | collective-permute-done | bytes 196640 | tf_op jit(solution)/shard_map/ppermute | solution.py:254
  93.2 1.1 collective-permute-start.12
  94.3 3.5 %collective-permute-done.19.x2 = bf16[256,384]{1,0:T(8,128)(2,1)S(1)} collective-permute-done((bf16[256,384]{1,0:T(8,128)(2,1)S(1)}, bf16[256,384]{1,0:T(8,128)(2,1)S(1)}, u32[]{:S(2)}, u32[]{:S(2)}) %collective-permute-start.19) | collective-permute-done | bytes 196640 | tf_op jit(solution)/shard_map/ppermute | solution.py:254
  97.9 1.1 collective-permute-start.24
  99.2 2.8 %collective-permute-done.12.x2 = bf16[256,384]{1,0:T(8,128)(2,1)S(1)} collective-permute-done((bf16[256,384]{1,0:T(8,128)(2,1)S(1)}, bf16[256,384]{1,0:T(8,128)(2,1)S(1)}, u32[]{:S(2)}, u32[]{:S(2)}) %collective-permute-start.12) | collective-permute-done | bytes 196640 | tf_op jit(solution)/shard_map/ppermute | solution.py:254
  102.1 5.1 %mlp.3 = (bf16[2,256,384]{2,1,0:T(8,128)(2,1)S(1)}, bf16[2,256,384]{2,1,0:T(8,128)(2,1)S(1)}) custom-call(s32[16]{0:T(128)S(1)} %copy-done.10, bf16[256,384]{1,0:T(8,128)(2,1)S(1)} %fusion.5.x0, bf16[256,384]{1,0:T(8,128)(2,1)S(1)} %collective-permute-done.18.x1, bf16[256,384]{1,0:T(8,128)(2,1)S(1)} %collective-permute-done.19.x2, ...), custom_call_target="tpu_custom_call" | custom-call | flops 4096000000 | bytes 1048576 | tf_op jit(solution)/shard_map/mlp/pallas_call | solution.py:239
  107.8 5.1 %mlp.2 = (bf16[2,256,384]{2,1,0:T(8,128)(2,1)S(1)}, bf16[2,256,384]{2,1,0:T(8,128)(2,1)S(1)}) custom-call(s32[16]{0:T(128)S(1)} %copy-done.10, bf16[256,384]{1,0:T(8,128)(2,1)S(1)} %fusion.9.x0, bf16[256,384]{1,0:T(8,128)(2,1)S(1)} %collective-permute-done.11.x1, bf16[256,384]{1,0:T(8,128)(2,1)S(1)} %collective-permute-done.12.x2, ...), custom_call_target="tpu_custom_call" | custom-call | flops 4096000000 | bytes 1048576 | tf_op jit(solution)/shard_map/mlp/pallas_call | solution.py:239
  113.1 1.1 collective-permute-start.22
  114.7 1.1 collective-permute-start.15
  115.8 5.0 %collective-permute-done.22 = bf16[256,384]{1,0:T(8,128)(2,1)S(1)} collective-permute-done((bf16[256,384]{1,0:T(8,128)(2,1)S(1)}, bf16[256,384]{1,0:T(8,128)(2,1)S(1)}, u32[]{:S(2)}, u32[]{:S(2)}) %collective-permute-start.22) | collective-permute-done | bytes 196640 | tf_op jit(solution)/shard_map/ppermute | solution.py:254
  121.0 3.7 %collective-permute-done.15 = bf16[256,384]{1,0:T(8,128)(2,1)S(1)} collective-permute-done((bf16[256,384]{1,0:T(8,128)(2,1)S(1)}, bf16[256,384]{1,0:T(8,128)(2,1)S(1)}, u32[]{:S(2)}, u32[]{:S(2)}) %collective-permute-start.15) | collective-permute-done | bytes 196640 | tf_op jit(solution)/shard_map/ppermute | solution.py:254
  124.9 15.0 %all_to_all.11 = bf16[16,40,384]{2,1,0:T(8,128)(2,1)S(1)} all-to-all(bf16[16,40,384]{2,1,0:T(8,128)(2,1)S(1)} %pad_maximum_fusion), channel_id=1, replica_groups={{0,4,16,20,32,36,48,52,64,68,80,84,96,100,112,116},{8,12,24,28,40,44,56..., dimensions={0} | all-to-all | bytes 983040 | tf_op jit(solution)/shard_map/all_to_all | solution.py:348
  (85 shorter events, 7.7 us)
Async XLA Ops:
  0.6 47.1 %copy-start.10 = (s32[16]{0:T(128)S(1)}, s32[16]{0:T(128)}, u32[]{:S(2)}) copy-start(s32[16]{0:T(128)} %refs_0_.11) | copy-start | bytes 196
  0.6 47.1 %copy-start.5 = (bf16[28,3,1536]{2,0,1:T(8,128)(2,1)S(1)}, bf16[28,3,1536]{2,0,1:T(8,128)(2,1)}, u32[]{:S(2)}) copy-start(bf16[28,3,1536]{2,0,1:T(8,128)(2,1)} %param.21) | copy-start | bytes 774148
  0.7 47.1 %copy-start = (bf16[1536,3,384]{2,0,1:T(8,128)(2,1)S(1)}, bf16[1536,3,384]{2,0,1:T(8,128)(2,1)}, u32[]{:S(2)}) copy-start(bf16[1536,3,384]{2,0,1:T(8,128)(2,1)} %param.22) | copy-start | bytes 10616836
  0.7 47.1 %copy-start.6 = (f32[64]{0:T(128)S(1)}, f32[64]{0:T(128)}, u32[]{:S(2)}) copy-start(f32[64]{0:T(128)} %param.26) | copy-start | bytes 772
  0.7 47.1 %copy-start.7 = (f32[64]{0:T(128)S(1)}, f32[64]{0:T(128)}, u32[]{:S(2)}) copy-start(f32[64]{0:T(128)} %param.27) | copy-start | bytes 772
  0.7 47.1 %copy-start.8 = (f32[64]{0:T(128)S(1)}, f32[64]{0:T(128)}, u32[]{:S(2)}) copy-start(f32[64]{0:T(128)} %param.28) | copy-start | bytes 772
  0.7 47.1 %copy-start.9 = (f32[64]{0:T(128)S(1)}, f32[64]{0:T(128)}, u32[]{:S(2)}) copy-start(f32[64]{0:T(128)} %param.29) | copy-start | bytes 772
  23.2 12.8 %collective-permute-start.3 = (bf16[16,40,384]{2,1,0:T(8,128)(2,1)S(1)}, bf16[16,40,384]{2,1,0:T(8,128)(2,1)S(1)}, u32[]{:S(2)}, u32[]{:S(2)}) collective-permute-start(bf16[16,40,384]{2,1,0:T(8,128)(2,1)S(1)} %all_to_all.10.refs_1_), channel_id=1, source_target_pairs={{0,8},{4,12},{8,0},{12,4},{16,24},{20,28},{24,16},{28,20},{32,40},... | collective-permute-start | bytes 1474568 | tf_op jit(solution)/shard_map/ppermute | solution.py:254
  26.1 19.0 %collective-permute-start.1 = (bf16[16,40,384]{2,1,0:T(8,128)(2,1)S(1)}, bf16[16,40,384]{2,1,0:T(8,128)(2,1)S(1)}, u32[]{:S(2)}, u32[]{:S(2)}) collective-permute-start(bf16[16,40,384]{2,1,0:T(8,128)(2,1)S(1)} %all_to_all.10.refs_1_), channel_id=1, source_target_pairs={{0,2},{1,3},{2,0},{3,1},{4,6},{5,7},{6,4},{7,5},{8,10},{9,11},{10,... | collective-permute-start | bytes 1474568 | tf_op jit(solution)/shard_map/ppermute | solution.py:254
  36.0 8.5 %collective-permute-start.5 = (bf16[8,40,384]{2,1,0:T(8,128)(2,1)S(1)}, bf16[8,40,384]{2,1,0:T(8,128)(2,1)S(1)}, u32[]{:S(2)}, u32[]{:S(2)}) collective-permute-start(bf16[8,40,384]{2,1,0:T(8,128)(2,1)S(1)} %get-tuple-element.33), channel_id=1, source_target_pairs={{0,2},{1,3},{2,0},{3,1},{4,6},{5,7},{6,4},{7,5},{8,10},{9,11},{10,... | collective-permute-start | bytes 737288 | tf_op jit(solution)/shard_map/ppermute | solution.py:254
  37.1 10.6 %collective-permute-start.4 = (bf16[16,40,384]{2,1,0:T(8,128)(2,1)S(1)}, bf16[16,40,384]{2,1,0:T(8,128)(2,1)S(1)}, u32[]{:S(2)}, u32[]{:S(2)}) collective-permute-start(bf16[16,40,384]{2,1,0:T(8,128)(2,1)S(1)} %collective-permute-done.3.refs_1_), channel_id=1, source_target_pairs={{0,1},{1,0},{2,3},{3,2},{4,5},{5,4},{6,7},{7,6},{8,9},{9,8},{10,11... | collective-permute-start | bytes 1474568 | tf_op jit(solution)/shard_map/ppermute | solution.py:254
  37.1 10.5 %collective-permute-start.7 = (bf16[8,40,384]{2,1,0:T(8,128)(2,1)S(1)}, bf16[8,40,384]{2,1,0:T(8,128)(2,1)S(1)}, u32[]{:S(2)}, u32[]{:S(2)}) collective-permute-start(bf16[8,40,384]{2,1,0:T(8,128)(2,1)S(1)} %get-tuple-element.32), channel_id=1, source_target_pairs={{0,2},{1,3},{2,0},{3,1},{4,6},{5,7},{6,4},{7,5},{8,10},{9,11},{10,... | collective-permute-start | bytes 737288 | tf_op jit(solution)/shard_map/ppermute | solution.py:254
  44.5 3.1 %collective-permute-start.6 = (bf16[8,40,384]{2,1,0:T(8,128)(2,1)S(1)}, bf16[8,40,384]{2,1,0:T(8,128)(2,1)S(1)}, u32[]{:S(2)}, u32[]{:S(2)}) collective-permute-start(bf16[8,40,384]{2,1,0:T(8,128)(2,1)S(1)} %collective-permute-done.5.refs_3_), channel_id=1, source_target_pairs={{0,1},{1,0},{2,3},{3,2},{4,5},{5,4},{6,7},{7,6},{8,9},{9,8},{10,11... | collective-permute-start | bytes 737288 | tf_op jit(solution)/shard_map/ppermute | solution.py:254
  44.6 13.7 %collective-permute-start = (bf16[16,40,384]{2,1,0:T(8,128)(2,1)S(1)}, bf16[16,40,384]{2,1,0:T(8,128)(2,1)S(1)}, u32[]{:S(2)}, u32[]{:S(2)}) collective-permute-start(bf16[16,40,384]{2,1,0:T(8,128)(2,1)S(1)} %all_to_all.10.refs_1_), channel_id=1, source_target_pairs={{0,1},{1,0},{2,3},{3,2},{4,5},{5,4},{6,7},{7,6},{8,9},{9,8},{10,11... | collective-permute-start | bytes 1474568 | tf_op jit(solution)/shard_map/ppermute | solution.py:254
  45.1 13.2 %collective-permute-start.2 = (bf16[16,40,384]{2,1,0:T(8,128)(2,1)S(1)}, bf16[16,40,384]{2,1,0:T(8,128)(2,1)S(1)}, u32[]{:S(2)}, u32[]{:S(2)}) collective-permute-start(bf16[16,40,384]{2,1,0:T(8,128)(2,1)S(1)} %collective-permute-done.1.refs_3_), channel_id=1, source_target_pairs={{0,1},{1,0},{2,3},{3,2},{4,5},{5,4},{6,7},{7,6},{8,9},{9,8},{10,11... | collective-permute-start | bytes 1474568 | tf_op jit(solution)/shard_map/ppermute | solution.py:254
  47.6 6.9 %collective-permute-start.8 = (bf16[8,40,384]{2,1,0:T(8,128)(2,1)S(1)}, bf16[8,40,384]{2,1,0:T(8,128)(2,1)S(1)}, u32[]{:S(2)}, u32[]{:S(2)}) collective-permute-start(bf16[8,40,384]{2,1,0:T(8,128)(2,1)S(1)} %collective-permute-done.7.refs_3_), channel_id=1, source_target_pairs={{0,1},{1,0},{2,3},{3,2},{4,5},{5,4},{6,7},{7,6},{8,9},{9,8},{10,11... | collective-permute-start | bytes 737288 | tf_op jit(solution)/shard_map/ppermute | solution.py:254
  71.0 10.9 %collective-permute-start.16 = (bf16[2,256,384]{2,1,0:T(8,128)(2,1)S(1)}, bf16[2,256,384]{2,1,0:T(8,128)(2,1)S(1)}, u32[]{:S(2)}, u32[]{:S(2)}) collective-permute-start(bf16[2,256,384]{2,1,0:T(8,128)(2,1)S(1)} %get-tuple-element.21), channel_id=1, source_target_pairs={{0,1},{1,0},{2,3},{3,2},{4,5},{5,4},{6,7},{7,6},{8,9},{9,8},{10,11... | collective-permute-start | bytes 1179656 | tf_op jit(solution)/shard_map/ppermute | solution.py:254
  76.8 6.3 %collective-permute-start.9 = (bf16[2,256,384]{2,1,0:T(8,128)(2,1)S(1)}, bf16[2,256,384]{2,1,0:T(8,128)(2,1)S(1)}, u32[]{:S(2)}, u32[]{:S(2)}) collective-permute-start(bf16[2,256,384]{2,1,0:T(8,128)(2,1)S(1)} %get-tuple-element.17), channel_id=1, source_target_pairs={{0,1},{1,0},{2,3},{3,2},{4,5},{5,4},{6,7},{7,6},{8,9},{9,8},{10,11... | collective-permute-start | bytes 1179656 | tf_op jit(solution)/shard_map/ppermute | solution.py:254
  81.3 16.5 %collective-permute-start.23 = (bf16[2,128,384]{2,1,0:T(8,128)(2,1)S(1)}, bf16[2,128,384]{2,1,0:T(8,128)(2,1)S(1)}, u32[]{:S(2)}, u32[]{:S(2)}) collective-permute-start(bf16[2,128,384]{2,1,0:T(8,128)(2,1)S(1)} %get-tuple-element.25), channel_id=1, source_target_pairs={{0,1},{1,0},{2,3},{3,2},{4,5},{5,4},{6,7},{7,6},{8,9},{9,8},{10,11... | collective-permute-start | bytes 589832 | tf_op jit(solution)/shard_map/ppermute | solution.py:254
  82.0 7.8 %collective-permute-start.17 = (bf16[256,384]{1,0:T(8,128)(2,1)S(1)}, bf16[256,384]{1,0:T(8,128)(2,1)S(1)}, u32[]{:S(2)}, u32[]{:S(2)}) collective-permute-start(bf16[256,384]{1,0:T(8,128)(2,1)S(1)} %fusion.12), channel_id=1, source_target_pairs={{0,2},{1,3},{2,0},{3,1},{4,6},{5,7},{6,4},{7,5},{8,10},{9,11},{10,... | collective-permute-start | bytes 589832 | tf_op jit(solution)/shard_map/ppermute | solution.py:254
  83.2 9.9 %collective-permute-start.10 = (bf16[256,384]{1,0:T(8,128)(2,1)S(1)}, bf16[256,384]{1,0:T(8,128)(2,1)S(1)}, u32[]{:S(2)}, u32[]{:S(2)}) collective-permute-start(bf16[256,384]{1,0:T(8,128)(2,1)S(1)} %fusion.10), channel_id=1, source_target_pairs={{0,2},{1,3},{2,0},{3,1},{4,6},{5,7},{6,4},{7,5},{8,10},{9,11},{10,... | collective-permute-start | bytes 589832 | tf_op jit(solution)/shard_map/ppermute | solution.py:254
  89.9 12.1 %collective-permute-start.18 = (bf16[256,384]{1,0:T(8,128)(2,1)S(1)}, bf16[256,384]{1,0:T(8,128)(2,1)S(1)}, u32[]{:S(2)}, u32[]{:S(2)}) collective-permute-start(bf16[256,384]{1,0:T(8,128)(2,1)S(1)} %fusion.5.x0), channel_id=1, source_target_pairs={{0,1},{1,0},{2,3},{3,2},{4,5},{5,4},{6,7},{7,6},{8,9},{9,8},{10,11... | collective-permute-start | bytes 589832 | tf_op jit(solution)/shard_map/ppermute | solution.py:254
  90.0 7.8 %collective-permute-start.19 = (bf16[256,384]{1,0:T(8,128)(2,1)S(1)}, bf16[256,384]{1,0:T(8,128)(2,1)S(1)}, u32[]{:S(2)}, u32[]{:S(2)}) collective-permute-start(bf16[256,384]{1,0:T(8,128)(2,1)S(1)} %fusion.5.x0), channel_id=1, source_target_pairs={{0,2},{1,3},{2,0},{3,1},{4,6},{5,7},{6,4},{7,5},{8,10},{9,11},{10,... | collective-permute-start | bytes 589832 | tf_op jit(solution)/shard_map/ppermute | solution.py:254
  93.2 8.8 %collective-permute-start.12 = (bf16[256,384]{1,0:T(8,128)(2,1)S(1)}, bf16[256,384]{1,0:T(8,128)(2,1)S(1)}, u32[]{:S(2)}, u32[]{:S(2)}) collective-permute-start(bf16[256,384]{1,0:T(8,128)(2,1)S(1)} %fusion.9.x0), channel_id=1, source_target_pairs={{0,2},{1,3},{2,0},{3,1},{4,6},{5,7},{6,4},{7,5},{8,10},{9,11},{10,... | collective-permute-start | bytes 589832 | tf_op jit(solution)/shard_map/ppermute | solution.py:254
  97.8 4.2 %collective-permute-start.20 = (bf16[256,384]{1,0:T(8,128)(2,1)S(1)}, bf16[256,384]{1,0:T(8,128)(2,1)S(1)}, u32[]{:S(2)}, u32[]{:S(2)}) collective-permute-start(bf16[256,384]{1,0:T(8,128)(2,1)S(1)} %collective-permute-done.19.x2), channel_id=1, source_target_pairs={{0,1},{1,0},{2,3},{3,2},{4,5},{5,4},{6,7},{7,6},{8,9},{9,8},{10,11... | collective-permute-start | bytes 589832 | tf_op jit(solution)/shard_map/ppermute | solution.py:254
  97.9 15.1 %collective-permute-start.24 = (bf16[128,384]{1,0:T(8,128)(2,1)S(1)}, bf16[128,384]{1,0:T(8,128)(2,1)S(1)}, u32[]{:S(2)}, u32[]{:S(2)}) collective-permute-start(bf16[128,384]{1,0:T(8,128)(2,1)S(1)} %fusion.16), channel_id=1, source_target_pairs={{0,2},{1,3},{2,0},{3,1},{4,6},{5,7},{6,4},{7,5},{8,10},{9,11},{10,... | collective-permute-start | bytes 294920 | tf_op jit(solution)/shard_map/ppermute | solution.py:254
  99.0 8.8 %collective-permute-start.11 = (bf16[256,384]{1,0:T(8,128)(2,1)S(1)}, bf16[256,384]{1,0:T(8,128)(2,1)S(1)}, u32[]{:S(2)}, u32[]{:S(2)}) collective-permute-start(bf16[256,384]{1,0:T(8,128)(2,1)S(1)} %fusion.9.x0), channel_id=1, source_target_pairs={{0,1},{1,0},{2,3},{3,2},{4,5},{5,4},{6,7},{7,6},{8,9},{9,8},{10,11... | collective-permute-start | bytes 589832 | tf_op jit(solution)/shard_map/ppermute | solution.py:254
  102.0 5.7 %collective-permute-start.13 = (bf16[256,384]{1,0:T(8,128)(2,1)S(1)}, bf16[256,384]{1,0:T(8,128)(2,1)S(1)}, u32[]{:S(2)}, u32[]{:S(2)}) collective-permute-start(bf16[256,384]{1,0:T(8,128)(2,1)S(1)} %collective-permute-done.12.x2), channel_id=1, source_target_pairs={{0,1},{1,0},{2,3},{3,2},{4,5},{5,4},{6,7},{7,6},{8,9},{9,8},{10,11... | collective-permute-start | bytes 589832 | tf_op jit(solution)/shard_map/ppermute | solution.py:254
  107.2 5.8 %collective-permute-start.21 = (bf16[2,256,384]{2,1,0:T(8,128)(2,1)S(1)}, bf16[2,256,384]{2,1,0:T(8,128)(2,1)S(1)}, u32[]{:S(2)}, u32[]{:S(2)}) collective-permute-start(bf16[2,256,384]{2,1,0:T(8,128)(2,1)S(1)} %get-tuple-element.23), channel_id=1, source_target_pairs={{0,1},{1,0},{2,3},{3,2},{4,5},{5,4},{6,7},{7,6},{8,9},{9,8},{10,11... | collective-permute-start | bytes 1179656 | tf_op jit(solution)/shard_map/ppermute | solution.py:254
  112.8 1.8 %collective-permute-start.14 = (bf16[2,256,384]{2,1,0:T(8,128)(2,1)S(1)}, bf16[2,256,384]{2,1,0:T(8,128)(2,1)S(1)}, u32[]{:S(2)}, u32[]{:S(2)}) collective-permute-start(bf16[2,256,384]{2,1,0:T(8,128)(2,1)S(1)} %get-tuple-element.19), channel_id=1, source_target_pairs={{0,1},{1,0},{2,3},{3,2},{4,5},{5,4},{6,7},{7,6},{8,9},{9,8},{10,11... | collective-permute-start | bytes 1179656 | tf_op jit(solution)/shard_map/ppermute | solution.py:254
  113.1 7.8 %collective-permute-start.22 = (bf16[256,384]{1,0:T(8,128)(2,1)S(1)}, bf16[256,384]{1,0:T(8,128)(2,1)S(1)}, u32[]{:S(2)}, u32[]{:S(2)}) collective-permute-start(bf16[256,384]{1,0:T(8,128)(2,1)S(1)} %fusion.13), channel_id=1, source_target_pairs={{0,2},{1,3},{2,0},{3,1},{4,6},{5,7},{6,4},{7,5},{8,10},{9,11},{10,... | collective-permute-start | bytes 589832 | tf_op jit(solution)/shard_map/ppermute | solution.py:254
  114.7 10.0 %collective-permute-start.15 = (bf16[256,384]{1,0:T(8,128)(2,1)S(1)}, bf16[256,384]{1,0:T(8,128)(2,1)S(1)}, u32[]{:S(2)}, u32[]{:S(2)}) collective-permute-start(bf16[256,384]{1,0:T(8,128)(2,1)S(1)} %fusion.11), channel_id=1, source_target_pairs={{0,2},{1,3},{2,0},{3,1},{4,6},{5,7},{6,4},{7,5},{8,10},{9,11},{10,... | collective-permute-start | bytes 589832 | tf_op jit(solution)/shard_map/ppermute | solution.py:254
  (11 other events, 149.4 us)

commit v3 on v2

v3 whole, which is shorter than its diff:
```python
import functools

import jax
import jax.numpy as jnp
from jax import lax
from jax.experimental import pallas as pl
from jax.experimental.pallas import tpu as pltpu
from jax.sharding import PartitionSpec as P

HEAD_DIM = 64
BF = jnp.bfloat16
F32 = jnp.float32
HIDDEN_BIAS = -32768.0
TXT_PAD = 8
VMEM_LIMIT = 28 << 20
VM = pl.BlockSpec(memory_space=pltpu.VMEM)
SM = pl.BlockSpec(memory_space=pltpu.SMEM)
HB = pl.BlockSpec(memory_space=pltpu.HBM)
COST = pl.CostEstimate(flops=1, transcendentals=0, bytes_accessed=1)


def dot(left, right):
    return jnp.dot(left, right, preferred_element_type=F32)


def dot_t(left, right):
    return lax.dot_general(left, right, (((1,), (1,)), ((), ())), preferred_element_type=F32)


def pinned(*arrays):
    return [pltpu.with_memory_space_constraint(array, pltpu.HBM) for array in arrays]


def fetch(sources, targets, sems):
    copies = [
        pltpu.make_async_copy(source, target, sems.at[i])
        for i, (source, target) in enumerate(zip(sources, targets))
    ]
    for copy in copies:
        copy.start()
    return copies


def table_row(table_ref, step, row):
    plane = table_ref[row].astype(F32)
    here = lax.broadcasted_iota(jnp.int32, plane.shape, 0) == step
    return jnp.sum(jnp.where(here, plane, 0.0), axis=0, keepdims=True)


def prep_kernel(step_ref, length_ref, *refs):
    mods_ref, gains_ref, bias_ref = refs[6:9]
    copies = fetch(refs[:6], refs[9:15], refs[15])
    for copy in copies:
        copy.wait()
    itab, ttab, gqi, gki, gqt, gkt = refs[9:15]
    tile = lax.axis_index("tile")
    request = (tile >> 2) * 2 + (tile & 1)
    step, length = step_ref[request], length_ref[request]
    for row in range(6):
        mods_ref[row : row + 1, :] = table_row(itab, step, row)
    for row in range(3):
        mods_ref[8 + row : 9 + row, :] = table_row(ttab, step, row)
    for row, ref in enumerate((gqi, gki, gqt, gkt)):
        gains_ref[row : row + 1, :] = jnp.concatenate([ref[...], ref[...]], axis=1)
    inner = lax.broadcasted_iota(jnp.int32, bias_ref.shape[1:], 0)
    source, slot = inner >> 3, inner & 7
    for side in range(2):
        parity = ((tile >> 1) & 1) ^ side
        sender = (source >> 1) * 4 + parity * 2 + (source & 1)
        seen = (slot < 5) & (sender * 5 + slot < length)
        bias_ref[side] = jnp.where(seen, 0.0, HIDDEN_BIAS).astype(BF)


def prep_call(step_index, text_length, tables, gains):
    width = tables[0].shape[2]
    return pl.pallas_call(
        prep_kernel,
        out_shape=[
            jax.ShapeDtypeStruct((16, width), F32),
            jax.ShapeDtypeStruct((8, 128), F32),
            jax.ShapeDtypeStruct((2, 128, 128), BF),
        ],
        in_specs=[SM, SM] + [HB] * 6,
        out_specs=[VM] * 3,
        scratch_shapes=[pltpu.VMEM(x.shape, x.dtype) for x in (*tables, *gains)]
        + [pltpu.SemaphoreType.DMA((6,))],
        compiler_params=pltpu.CompilerParams(vmem_limit_bytes=VMEM_LIMIT),
        cost_estimate=COST,
        name="prep",
    )(step_index, text_length, *pinned(*tables, *gains))


def norm_rows(raw_ref, acts_ref, start, count, shift, scale, block=32):
    width = raw_ref.shape[1]
    gain = 1.0 + scale

    def body(i, carry):
        rows = pl.ds(pl.multiple_of(start + i * block, block), block)
        values = raw_ref[rows, :].astype(F32)
        centre = jnp.sum(values, axis=-1, keepdims=True) * (1.0 / width)
        moved = values - centre
        spread = jnp.sum(moved * moved, axis=-1, keepdims=True) * (1.0 / width)
        acts_ref[rows, :] = (moved * lax.rsqrt(spread + 1e-06) * gain + shift).astype(BF)
        return carry

    lax.fori_loop(0, count // block, body, 0, unroll=2)


def head_scale(values, group):
    parts = []
    for col in range(0, values.shape[1], 128):
        piece = values[:, col : col + 128]
        squares = piece * piece
        high = squares.astype(BF)
        low = (squares - high.astype(F32)).astype(BF)
        parts.append(dot(jnp.concatenate([high, low], axis=1), group))
    return lax.rsqrt(jnp.concatenate(parts, axis=1) + 1e-06)


def group_matrix():
    row = lax.broadcasted_iota(jnp.int32, (256, 128), 0)
    col = lax.broadcasted_iota(jnp.int32, (256, 128), 1)
    same = ((row & 127) >> 6) == (col >> 6)
    return jnp.where(same, 1.0 / HEAD_DIM, 0.0).astype(BF)


def qkv_kernel(begin, sources, parts, *refs):
    mods, gains, x0, x1, x2, x3, wimg, wtxt = refs[:8]
    outs, (wimg_ref, wtxt_ref, raw_ref, acts_ref, sems) = refs[8:-5], refs[-5:]
    copies = fetch(
        [w.at[i] for w in (wtxt, wimg) for i in parts],
        [
            w.at[:, i * x0.shape[2] : (i + 1) * x0.shape[2]]
            for w in (wtxt_ref, wimg_ref)
            for i in range(len(parts))
        ],
        sems,
    )
    blk = lax.axis_index("blk")
    part = x0.shape[2]
    image_rows = x0.shape[1] - TXT_PAD
    img, txt = sources * image_rows, sources * TXT_PAD
    for j, (ref, first) in enumerate(zip((x0, x1, x2, x3), begin)):
        cols = pl.ds(pl.multiple_of((blk ^ j) * part, part), part)
        raw_ref[:img, cols] = ref[first : first + sources, :image_rows, :].reshape(img, part)
        text = ref[first : first + sources, image_rows:, :].astype(F32).reshape(txt, part)
        raw_ref[img:, cols] = text.astype(BF)
    norm_rows(raw_ref, acts_ref, img, txt, mods[8:9, :], mods[9:10, :])
    norm_rows(raw_ref, acts_ref, 0, img, mods[0:1, :], mods[1:2, :])
    group = group_matrix()
    kv_ref = outs[-1]
    for w_ref, first, last, row, waits in (
        (wtxt_ref, img, img + txt, 2, copies[: len(parts)]),
        (wimg_ref, 0, img, 0, copies[len(parts) :]),
    ):
        for copy in waits:
            copy.wait()
        projected = dot(acts_ref[first:last, :], w_ref[...])
        for i, which in enumerate(parts):
            values = projected[:, i * part : (i + 1) * part]
            if which == 2:
                kv_ref[1, first:last, :] = values.astype(BF)
                continue
            gain = jnp.concatenate([gains[row + which : row + which + 1, :]] * (part // 128), axis=1)
            normed = (values * head_scale(values, group) * gain).astype(BF)
            if which == 1:
                kv_ref[0, first:last, :] = normed
            else:
                outs[0][first:last, :] = normed * BF(HEAD_DIM**-0.5)


def qkv_call(mods, gains, pieces, begin, sources, weights, parts):
    part = pieces[0].shape[2]
    rows, width = sources * pieces[0].shape[1], 4 * part
    outs = [jax.ShapeDtypeStruct((2, rows, part), BF)]
    if 0 in parts:
        outs = [jax.ShapeDtypeStruct((rows, part), BF)] + outs
    weight = pltpu.VMEM((width, len(parts) * part), BF)
    return pl.pallas_call(
        functools.partial(qkv_kernel, begin, sources, parts),
        out_shape=outs,
        in_specs=[VM] * 6 + [HB] * 2,
        out_specs=[VM] * len(outs),
        scratch_shapes=[weight, weight]
        + [pltpu.VMEM((rows, width), BF)] * 2
        + [pltpu.SemaphoreType.DMA((2 * len(parts),))],
        compiler_params=pltpu.CompilerParams(vmem_limit_bytes=VMEM_LIMIT),
        cost_estimate=COST,
        name="qkv",
    )(mods, gains, *pieces, *pinned(*weights))


def head_scores(query, keys, lane, one_lane, head):
    mine = (lane < 64) if head == 0 else (lane >= 64)
    left = jnp.concatenate([jnp.where(mine, query, BF(0.0)), one_lane], axis=1)
    return [dot_t(left, key) for key in keys]


def both_halves(values, lane):
    return jnp.where(lane < 64, values[0], values[1])


def lane_masks(rows):
    lane = lax.broadcasted_iota(jnp.int32, (rows, 128), 1)
    return lane, jnp.where(lane == 0, 1.0, 0.0).astype(BF)


def hiding(bias, img_rows):
    return jnp.concatenate([jnp.zeros((img_rows, 128), BF), bias], axis=0)


def biased(ref, bias, cols):
    return jnp.concatenate([ref[0, :, cols], bias], axis=1)


def summed(ref, cols):
    return jnp.concatenate([ref[1, :, cols], jnp.ones((ref.shape[1], 128), BF)], axis=1)


def own_kernel(bias_ref, q_ref, kv_ref, top_ref, sum_ref, out_ref):
    rows, part = q_ref.shape
    count = rows // 2
    bias = hiding(bias_ref[0], rows - bias_ref.shape[1])
    lane, one_lane = lane_masks(count)
    for col in range(0, part, 128):
        cols = slice(col, col + 128)
        key, value = biased(kv_ref, bias, cols), summed(kv_ref, cols)
        for start in range(0, rows, count):
            span = slice(start, start + count)
            tops, sums, outs = [], [], []
            for head in range(2):
                score = head_scores(q_ref[span, cols], [key], lane, one_lane, head)[0]
                top = jnp.max(score, axis=-1, keepdims=True)
                both = dot(jnp.exp(score - top).astype(BF), value)
                tops.append(top)
                outs.append(both[:, :128])
                sums.append(both[:, 128:])
            top_ref[span, cols] = both_halves(tops, lane)
            sum_ref[span, cols] = both_halves(sums, lane)
            out_ref[span, cols] = both_halves(outs, lane)


def own_call(bias, query, keys):
    shape = jax.ShapeDtypeStruct(query.shape, F32)
    return pl.pallas_call(
        own_kernel,
        out_shape=[shape] * 3,
        in_specs=[VM] * 3,
        out_specs=[VM] * 3,
        compiler_params=pltpu.CompilerParams(vmem_limit_bytes=VMEM_LIMIT),
        cost_estimate=COST,
        name="attend_own",
    )(bias, query, keys)


def attend_kernel(start, counts, gate_rows, *refs):
    groups = len(counts)
    count = sum(counts)
    mods, bias_ref, q_ref, top_ref, sum_ref, out_ref, kv_ref = refs[:7]
    w_refs, sems = refs[7 + 3 * groups : -1], refs[-1]
    copies = fetch(refs[7 : 7 + groups], w_refs, sems)
    part = q_ref.shape[1]
    lane, one_lane = lane_masks(count)
    bias = hiding(bias_ref[1], kv_ref.shape[1] - bias_ref.shape[1])
    span = slice(start, start + count)
    att = []
    for col in range(0, part, 128):
        cols = slice(col, col + 128)
        key, val = biased(kv_ref, bias, cols), summed(kv_ref, cols)
        outs, sums, scales = [], [], []
        for head in range(2):
            score = head_scores(q_ref[span, cols], [key], lane, one_lane, head)[0]
            before = top_ref[span, col + 64 * head : col + 64 * head + 1]
            top = jnp.maximum(before, jnp.max(score, axis=-1, keepdims=True))
            both = dot(jnp.exp(score - top).astype(BF), val)
            outs.append(both[:, :128])
            sums.append(both[:, 128:])
            scales.append(jnp.exp(before - top))
        scale = both_halves(scales, lane)
        total = both_halves(sums, lane) + scale * sum_ref[span, cols]
        att.append(((both_halves(outs, lane) + scale * out_ref[span, cols]) / total).astype(BF))
    att = jnp.concatenate(att, axis=1)
    first = 0
    for i, (rows, row) in enumerate(zip(counts, gate_rows)):
        copies[i].wait()
        outs = refs[7 + groups + 2 * i : 9 + groups + 2 * i]
        project_out(att[first : first + rows], mods[row : row + 1, :], w_refs[i], *outs)
        first += rows


def project_out(left, gate, w_ref, keep_ref, send_ref):
    blk = lax.axis_index("blk")
    part = keep_ref.shape[2]
    width = gate.shape[1]
    for pair in range(2):
        which = (blk >> 1) ^ pair
        value = dot(left, w_ref[:, pl.ds(pl.multiple_of(which * 2 * part, 2 * part), 2 * part)])
        value = value * jnp.where(which == 0, gate[:, : width // 2], gate[:, width // 2 :])
        low, high = value[:, :part].astype(BF), value[:, part:].astype(BF)

        @pl.when((blk & 1) == 0)
        def _():
            keep_ref[pair] = low
            send_ref[pair] = high

        @pl.when((blk & 1) == 1)
        def _():
            keep_ref[pair] = high
            send_ref[pair] = low


def attend_call(mods, bias, query, state, keys, start, counts, gate_rows, weights):
    shapes = []
    for count in counts:
        shapes += [jax.ShapeDtypeStruct((2, count, query.shape[1]), BF)] * 2
    return pl.pallas_call(
        functools.partial(attend_kernel, start, counts, gate_rows),
        out_shape=shapes,
        in_specs=[VM] * 7 + [HB] * len(weights),
        out_specs=[VM] * len(shapes),
        scratch_shapes=[pltpu.VMEM(weight.shape, BF) for weight in weights]
        + [pltpu.SemaphoreType.DMA((len(weights),))],
        compiler_params=pltpu.CompilerParams(vmem_limit_bytes=VMEM_LIMIT),
        cost_estimate=COST,
        name="attend",
    )(mods, bias, query, *state, keys, *pinned(*weights))


def mlp_kernel(mods, mine, near, up_ref, down_ref, keep_ref, send_ref, raw_ref, acts_ref):
    blk = lax.axis_index("blk")
    rows, part = mine.shape[1:]
    span = up_ref.shape[1] // 3
    for j in range(4):
        value = (near if j & 1 else mine)[j >> 1]
        raw_ref[:, pl.ds(pl.multiple_of((blk ^ j) * part, part), part)] = value
    norm_rows(raw_ref, acts_ref, 0, rows, mods[3:4, :], mods[4:5, :])
    for i in range(3):
        cols = slice(i * span, i * span + span)
        hidden = dot(acts_ref[...], up_ref[:, cols])
        raw_ref[:, cols] = jax.nn.gelu(hidden, approximate=True).astype(BF)
    project_out(raw_ref[...], mods[5:6, :], down_ref, keep_ref, send_ref)


def mlp_call(mods, mine, near, up, down):
    rows, part = mine.shape[1:]
    shape = jax.ShapeDtypeStruct((2, rows, part), BF)
    return pl.pallas_call(
        mlp_kernel,
        out_shape=[shape, shape],
        in_specs=[VM] * 5,
        out_specs=[VM, VM],
        scratch_shapes=[pltpu.VMEM((rows, 4 * part), BF)] * 2,
        compiler_params=pltpu.CompilerParams(vmem_limit_bytes=VMEM_LIMIT),
        cost_estimate=COST,
        name="mlp",
    )(mods, mine, near, up, down)


def swap(values, axis, size, bit):
    return lax.ppermute(values, axis, [(i, i ^ bit) for i in range(size)])


def after(value, *others):
    return lax.optimization_barrier((value, *others))[0]


def add(*terms):
    return sum(term.astype(F32) for term in terms).astype(BF)


def small_call(kernel, name, outs, args, scratch=(), spec=VM):
    return pl.pallas_call(
        kernel,
        out_shape=[jax.ShapeDtypeStruct(shape, BF) for shape in outs],
        in_specs=[spec] * len(args),
        out_specs=[VM] * len(outs),
        scratch_shapes=list(scratch),
        compiler_params=pltpu.CompilerParams(vmem_limit_bytes=VMEM_LIMIT),
        cost_estimate=COST,
        name=name,
    )(*args)


def pack_kernel(image, text, out_ref, slots_ref, text_ref, sems):
    requests, image_rows, part = image.shape
    copies = fetch((text, image), (text_ref, out_ref.at[:, :image_rows, :]), sems)
    copies[0].wait()
    slots_ref[...] = jnp.zeros_like(slots_ref)
    for slot in range(text_ref.shape[0]):
        value = text_ref[slot].astype(F32)
        for i in range(part // 128):
            slots_ref[i, pl.ds(slot, requests, stride=TXT_PAD), :] = value[:, i * 128 : i * 128 + 128]
    for i in range(part // 128):
        piece = slots_ref[i].reshape(requests, TXT_PAD, 128).astype(BF)
        out_ref[:, image_rows:, i * 128 : i * 128 + 128] = piece
    copies[1].wait()


def sum_kernel(first, left_ref, right_ref, out_ref):
    for i in range(first, 2):
        out_ref[i - first] = add(left_ref[i], right_ref[i])


def away_kernel(image_ref, came_i, text_ref, came_t, out_ref):
    rows = image_ref.shape[1]
    out_ref[:rows, :] = add(image_ref[1], came_i[1])
    out_ref[rows:, :] = add(text_ref[1], came_t[1])


def core_sum(kept, came, first):
    shape = (2 - first,) + kept.shape[1:]
    return small_call(functools.partial(sum_kernel, first), "core_sum", [shape], [kept, came])[0]


def middle_kernel(begin, own_ref, far_ref, sum_ref, back_ref, out_ref):
    rows, part = out_ref.shape[1:]
    image_rows = own_ref.shape[1] - TXT_PAD
    for i, ref in enumerate((own_ref, far_ref)):
        start = ref[begin : begin + rows // image_rows, :image_rows, :].reshape(rows, part)
        out_ref[i] = add(start, sum_ref[i], back_ref[1 - i])


def first_kernel(own_ref, keep_t, came_t, mid_a, keep_a, came_a, last_a, image_ref, text_ref):
    rows = image_ref.shape[0]
    image_ref[...] = add(mid_a[0], keep_a[0], came_a[0], last_a[:rows, :])
    sources, slots, part = own_ref.shape
    total = keep_t[0].astype(F32) + came_t[0].astype(F32) + last_a[rows:, :].astype(F32)
    text = own_ref[:, slots - TXT_PAD :, :].astype(F32) + total.reshape(sources, TXT_PAD, part)
    text_ref[...] = text.astype(BF)


def final_kernel(image_ref, text_ref, mid_b, keep_b, came_b, last_b, out_ref):
    sources, slots, part = out_ref.shape
    image_rows = slots - TXT_PAD
    half = sources // 2
    out_ref[:half, :image_rows, :] = image_ref[...].reshape(half, image_rows, part)
    value = add(mid_b[0], keep_b[0], came_b[0], last_b[0])
    out_ref[half:, :image_rows, :] = value.reshape(half, image_rows, part)
    out_ref[:, image_rows:, :] = text_ref[...]


def per_device(
    tiles,
    image_tokens,
    text_tokens,
    step_index,
    text_length,
    image_table,
    text_table,
    qkv_image,
    qkv_text,
    attn_out_image,
    attn_out_text,
    query_gain_image,
    key_gain_image,
    query_gain_text,
    key_gain_text,
    up_weight,
    down_weight,
):
    requests, image_rows, part = image_tokens.shape
    text_rows = text_tokens.shape[1]
    groups = [[t for t in range(tiles) if (t >> 1) & 1 == p] for p in (0, 1)]
    tables = [jnp.transpose(table, (1, 0, 2)) for table in (image_table, text_table)]
    weights = [jnp.transpose(weight, (1, 0, 2)) for weight in (qkv_image, qkv_text)]
    gains = [
        gain.reshape(1, HEAD_DIM)
        for gain in (query_gain_image, key_gain_image, query_gain_text, key_gain_text)
    ]

    slots = (requests, image_rows + TXT_PAD, part)
    text_slots = jnp.transpose(text_tokens, (1, 0, 2))
    packed = small_call(
        pack_kernel,
        "pack",
        [slots],
        pinned(image_tokens, text_slots),
        [
            pltpu.VMEM((part // 128, requests * TXT_PAD, 128), F32),
            pltpu.VMEM(text_slots.shape, BF),
            pltpu.SemaphoreType.DMA((2,)),
        ],
        HB,
    )[0]
    own = lax.all_to_all(packed, "tile", 0, 0, axis_index_groups=groups, tiled=True)
    far = swap(own, "blk", 4, 2)
    other = swap(own, "tile", tiles, 2)
    near = swap(own, "blk", 4, 1)
    mods, head_gains, bias = prep_call(after(step_index, own), text_length, tables, gains)

    def tied(*others):
        return after(mods, *others)

    def project(mods, pieces, parts):
        return qkv_call(mods, head_gains, pieces, (0, 0, 0, 0), requests, weights, parts)

    far = after(far, mods)
    other = after(other, far)
    other_far = swap(other, "blk", 4, 2)
    diag = swap(far, "blk", 4, 1)
    query, mine = project(mods, [own, near, far, diag], (1, 2, 0))
    other_near = swap(after(other, query), "blk", 4, 1)
    state = own_call(bias, query, mine)
    other_far = after(other_far, state[0])
    other_diag = swap(other_far, "blk", 4, 1)
    keys = project(tied(state[0]), [other, other_near, other_far, other_diag], (1, 2))[0]

    half = requests // 2
    rows = half * image_rows
    txt_rows = requests * TXT_PAD

    def attend(mods, *groups):
        return attend_call(mods, bias, query, state, keys, *groups)

    def middle(begin, sums, back):
        args = [own, far, sums, back]
        return small_call(functools.partial(middle_kernel, begin), "middle", [(2, rows, part)], args)[0]

    keep_a, send_a = attend(mods, 0, (rows,), (2,), (attn_out_image,))
    came_a = swap(send_a, "blk", 4, 1)
    sum_a = core_sum(keep_a, came_a, 0)
    back_a = swap(sum_a, "blk", 4, 2)
    keep_b, send_b, keep_t, send_t = attend(
        tied(sum_a), rows, (rows, txt_rows), (2, 10), (attn_out_image, attn_out_text)
    )
    came_b = swap(send_b, "blk", 4, 1)
    mid_a = middle(0, sum_a, after(back_a, keep_b))
    near_a = swap(mid_a, "blk", 4, 1)
    sum_b = core_sum(after(keep_b, mid_a), came_b, 0)
    back_b = swap(sum_b, "blk", 4, 2)
    came_t = swap(send_t, "blk", 4, 1)
    came_t = after(came_t, sum_b)
    down_a, send_a = mlp_call(tied(came_t), mid_a, near_a, up_weight, down_weight)
    came_a = swap(send_a, "blk", 4, 1)
    mid_b = middle(half, sum_b, after(back_b, down_a))
    near_b = swap(mid_b, "blk", 4, 1)
    args = [after(down_a, mid_b), came_a, keep_t, came_t]
    away_a = small_call(away_kernel, "away", [(rows + txt_rows, part)], args)[0]
    last_a = swap(away_a, "blk", 4, 2)
    down_b, send_b = mlp_call(tied(away_a), mid_b, near_b, up_weight, down_weight)
    args = [own, keep_t, came_t, mid_a, down_a, came_a, after(last_a, down_b)]
    image_a, text_out = small_call(
        first_kernel, "first", [(rows, part), (requests, TXT_PAD, part)], args
    )
    came_b = swap(after(send_b, image_a), "blk", 4, 1)
    away_b = core_sum(down_b, came_b, 1)
    last_b = swap(away_b, "blk", 4, 2)

    args = [image_a, text_out, mid_b, down_b, came_b, last_b]
    result = small_call(final_kernel, "final", [slots], args)[0]
    result = lax.all_to_all(result, "tile", 0, 0, axis_index_groups=groups, tiled=True)
    return (result[:, :image_rows], result[:, image_rows : image_rows + text_rows])


def solution(mesh):
    in_specs = (
        P(None, "tile", "blk"),
        P(None, "tile", "blk"),
        P(),
        P(),
        P(),
        P(),
        P(None, None, "blk"),
        P(None, None, "blk"),
        P("blk", None),
        P("blk", None),
        P(),
        P(),
        P(),
        P(),
        P(None, "blk"),
        P("blk", None),
    )
    out_specs = (P(None, "tile", "blk"), P(None, "tile", "blk"))
    return jax.shard_map(
        functools.partial(per_device, mesh.shape["tile"]),
        mesh=mesh,
        in_specs=in_specs,
        out_specs=out_specs,
        check_vma=False,
    )
```

time: 142 us -> 119 us (0.84)
  waiting for transfers between devices: 40.8 us -> 31.8 us
  starting transfers between devices: 16.7 us -> 11.8 us
  Pallas kernels: 39.7 us -> 36.4 us
  local copies, waits for them, and re-layouts: 5.67 us -> 2.76 us
  other arithmetic: 2.08 us -> 0.01 us
    ppermute x25 -> x18, waiting for transfers between devices: 40.8 us -> 31.8 us  [swap(): return lax.ppermute(values, axis, [(i, i ^ bit) for i in range(size)])]
    ppermute x25 -> x18, starting transfers between devices: 16.7 us -> 11.8 us  [swap(): return lax.ppermute(values, axis, [(i, i ^ bit) for i in range(size)])]
    pallas_call x8 -> x17, Pallas kernels: 39.7 us -> 36.4 us  [the longest x2 11.2 us: qkv_call(): pl.pallas_call(functools.partial(qkv_kernel, begin, sources, parts), out_...]
    unnamed x38 -> x13, local copies, waits for them, and re-layouts: 4.78 us -> 1.97 us
  transfers between devices with their start and end apart: 25 -> 18, of which waited for: 10 -> 12; matrix products, arithmetic and copies ran while one was open for 1% -> 0% of each run, Pallas kernels for 19% -> 22%
where the time goes in v3:
time: 119 us; the launch traced here: 118 us
  Pallas kernels  36.4 us (31%)
  blocking collectives  34.8 us (29%)
  waiting for transfers between devices  31.8 us (27%)
  starting transfers between devices  11.8 us (10%)
  local copies, waits for them, and re-layouts  2.76 us (2%)
    ppermute x18, waiting for transfers between devices, swap(): return lax.ppermute(values, axis, [(i, i ^ bit) for i in range(size)])  31.8 us
    all_to_all x1, blocking collectives, per_device(): lax.all_to_all(packed, 'tile', 0, 0, axis_index_groups=groups, tiled=True)  20.3 us
    all_to_all x1, blocking collectives, per_device(): lax.all_to_all(result, 'tile', 0, 0, axis_index_groups=groups, tiled=True)  14.5 us
    ppermute x18, starting transfers between devices, swap(): return lax.ppermute(values, axis, [(i, i ^ bit) for i in range(size)])  11.8 us
    pallas_call x2, Pallas kernels, qkv_call(): pl.pallas_call(functools.partial(qkv_kernel, begin, sources, parts), out_...  11.2 us
    pallas_call x2, Pallas kernels, mlp_call(): pl.pallas_call(mlp_kernel, out_shape=[shape, shape], in_specs=[VM] * 5, o...  8.86 us
    pallas_call x2, Pallas kernels, attend_call(): pl.pallas_call(functools.partial(attend_kernel, start, counts, gate_rows)...  8.56 us
    pallas_call x1, Pallas kernels, own_call(): pl.pallas_call(own_kernel, out_shape=[shape] * 3, in_specs=[VM] * 3, out_...  3.74 us
  transfers between devices with their start and end apart: 18, of which 12 were waited for; matrix products, arithmetic and copies ran while one was open for 0% of the time, Pallas kernels for 22%

profile of v3, /device:TPU:0, one launch (start us, length us, event | category | flops | bytes accessed | tf_op | source)
XLA Modules:
  0.0 118.4 jit_solution(3055376968301868442)
XLA Ops:
  0.6 1.1 pack.1
  1.7 20.3 %all_to_all.10.refs_2_.own_ref = bf16[16,40,384]{2,1,0:T(8,128)(2,1)S(1)} all-to-all(bf16[16,40,384]{2,1,0:T(8,128)(2,1)S(1)} %pack.1), channel_id=1, replica_groups={{0,4,16,20,32,36,48,52,64,68,80,84,96,100,112,116},{8,12,24,28,40,44,56..., dimensions={0} | all-to-all | bytes 983040 | tf_op jit(solution)/shard_map/all_to_all | solution.py:485
  21.9 1.0 collective-permute-start.1
  23.0 2.9 %collective-permute-start.3 = (bf16[16,40,384]{2,1,0:T(8,128)(2,1)S(1)}, bf16[16,40,384]{2,1,0:T(8,128)(2,1)S(1)}, u32[]{:S(2)}, u32[]{:S(2)}) collective-permute-start(bf16[16,40,384]{2,1,0:T(8,128)(2,1)S(1)} %all_to_all.10.refs_2_.own_ref), channel_id=1, source_target_pairs={{0,8},{4,12},{8,0},{12,4},{16,24},{20,28},{24,16},{28,20},{32,40},... | collective-permute-start | bytes 1474568 | tf_op jit(solution)/shard_map/ppermute | solution.py:360
  25.9 0.7 copy-done
  26.5 0.7 copy-done.1
  27.2 2.1 %prep.1 = (f32[16,1536]{1,0:T(8,128)S(1)}, f32[8,128]{1,0:T(8,128)S(1)}, bf16[2,128,128]{2,1,0:T(8,128)(2,1)S(1)}) custom-call(s32[16]{0:T(128)S(1)} %copy-done, s32[16]{0:T(128)S(1)} %copy-done.1, bf16[6,28,1536]{2,1,0:T(8,128)(2,1)} %bitcast.17, bf16[3,28,1536]{2,1,0:T(8,128)(2,1)} %bitcast.18, f32[1,64]{1,0:T(1,128)} %bitcast.20, f32[1,64]{1,0:T(1,128)} %bitcast.21, ...), custom_call_target="tpu_custom_call" | custom-call | flops 1 | bytes 1 | tf_op jit(solution)/shard_map/prep/pallas_call | solution.py:76
  29.4 3.9 %collective-permute-done.1.refs_4_.far_ref = bf16[16,40,384]{2,1,0:T(8,128)(2,1)S(1)} collective-permute-done((bf16[16,40,384]{2,1,0:T(8,128)(2,1)S(1)}, bf16[16,40,384]{2,1,0:T(8,128)(2,1)S(1)}, u32[]{:S(2)}, u32[]{:S(2)}) %collective-permute-start.1) | collective-permute-done | bytes 491552 | tf_op jit(solution)/shard_map/ppermute | solution.py:360
  33.2 2.2 %collective-permute-done.3.refs_2_ = bf16[16,40,384]{2,1,0:T(8,128)(2,1)S(1)} collective-permute-done((bf16[16,40,384]{2,1,0:T(8,128)(2,1)S(1)}, bf16[16,40,384]{2,1,0:T(8,128)(2,1)S(1)}, u32[]{:S(2)}, u32[]{:S(2)}) %collective-permute-start.3) | collective-permute-done | bytes 491552 | tf_op jit(solution)/shard_map/ppermute | solution.py:360
  35.5 1.0 collective-permute-start.5
  36.5 6.3 %qkv.2 = (bf16[640,384]{1,0:T(8,128)(2,1)S(1)}, bf16[2,640,384]{2,1,0:T(8,128)(2,1)S(1)}) custom-call(f32[16,1536]{1,0:T(8,128)S(1)} %get-tuple-element.67.refs_0_.mods, f32[8,128]{1,0:T(8,128)S(1)} %get-tuple-element.41.refs_1_, bf16[16,40,384]{2,1,0:T(8,128)(2,1)S(1)} %all_to_all.10.refs_2_.own_ref, bf16[16,40,384]{2,1,0:T(8,128)(2,1)S(1)} %collective-permute-done.refs_3_, ...), custom_call_target="tpu_custom_call" | custom-call | flops 1 | bytes 1 | tf_op jit(solution)/shard_map/qkv/pallas_call | solution.py:179
  42.9 3.7 %attend_own.1 = (f32[640,384]{1,0:T(8,128)S(1)}, f32[640,384]{1,0:T(8,128)S(1)}, f32[640,384]{1,0:T(8,128)S(1)}) custom-call(bf16[2,128,128]{2,1,0:T(8,128)(2,1)S(1)} %get-tuple-element.40.bias_ref.refs_1_, bf16[640,384]{1,0:T(8,128)(2,1)S(1)} %get-tuple-element.43.q_ref.refs_2_, bf16[2,640,384]{2,1,0:T(8,128)(2,1)S(1)} %get-tuple-element.44.kv_ref), custom_call_target="tpu_custom_call" | custom-call | flops 1 | bytes 1 | tf_op jit(solution)/shard_map/attend_own/pallas_call | solution.py:245
  47.4 1.5 %collective-permute-done.6.refs_5_ = bf16[16,40,384]{2,1,0:T(8,128)(2,1)S(1)} collective-permute-done((bf16[16,40,384]{2,1,0:T(8,128)(2,1)S(1)}, bf16[16,40,384]{2,1,0:T(8,128)(2,1)S(1)}, u32[]{:S(2)}, u32[]{:S(2)}) %collective-permute-start.6) | collective-permute-done | bytes 491552 | tf_op jit(solution)/shard_map/ppermute | solution.py:360
  48.9 4.9 %qkv.3.refs_6_ = bf16[2,640,384]{2,1,0:T(8,128)(2,1)S(1)} custom-call(f32[16,1536]{1,0:T(8,128)S(1)} %get-tuple-element.67.refs_0_.mods, f32[8,128]{1,0:T(8,128)S(1)} %get-tuple-element.41.refs_1_, bf16[16,40,384]{2,1,0:T(8,128)(2,1)S(1)} %collective-permute-done.3.refs_2_, bf16[16,40,384]{2,1,0:T(8,128)(2,1)S(1)} %collective-permute-done.4.refs_3_, ...), custom_call_target="tpu_custom_call" | custom-call | flops 1 | bytes 1 | tf_op jit(solution)/shard_map/qkv/pallas_call | solution.py:179
  53.8 4.0 %attend.2 = (bf16[2,256,384]{2,1,0:T(8,128)(2,1)S(1)}, bf16[2,256,384]{2,1,0:T(8,128)(2,1)S(1)}) custom-call(f32[16,1536]{1,0:T(8,128)S(1)} %get-tuple-element.67.refs_0_.mods, bf16[2,128,128]{2,1,0:T(8,128)(2,1)S(1)} %get-tuple-element.40.bias_ref.refs_1_, bf16[640,384]{1,0:T(8,128)(2,1)S(1)} %get-tuple-element.43.q_ref.refs_2_, ...), custom_call_target="tpu_custom_call" | custom-call | flops 1 | bytes 1 | tf_op jit(solution)/shard_map/attend/pallas_call | solution.py:316
  58.3 1.3 %collective-permute-done.7.right_ref = bf16[2,256,384]{2,1,0:T(8,128)(2,1)S(1)} collective-permute-done((bf16[2,256,384]{2,1,0:T(8,128)(2,1)S(1)}, bf16[2,256,384]{2,1,0:T(8,128)(2,1)S(1)}, u32[]{:S(2)}, u32[]{:S(2)}) %collective-permute-start.7) | collective-permute-done | bytes 393248 | tf_op jit(solution)/shard_map/ppermute | solution.py:360
  59.7 1.1 collective-permute-start.9
  60.8 4.6 %attend.3 = (bf16[2,256,384]{2,1,0:T(8,128)(2,1)S(1)}, bf16[2,256,384]{2,1,0:T(8,128)(2,1)S(1)}, bf16[2,128,384]{2,1,0:T(8,128)(2,1)S(1)}, bf16[2,128,384]{2,1,0:T(8,128)(2,1)S(1)}) custom-call(f32[16,1536]{1,0:T(8,128)S(1)} %get-tuple-element.67.refs_0_.mods, bf16[2,128,128]{2,1,0:T(8,128)(2,1)S(1)} %get-tuple-element.40.bias_ref.refs_1_, ...), custom_call_target="tpu_custom_call" | custom-call | flops 1 | bytes 1 | tf_op jit(solution)/shard_map/attend/pallas_call | solution.py:316
  65.6 5.6 %collective-permute-done.9.back_ref = bf16[2,256,384]{2,1,0:T(8,128)(2,1)S(1)} collective-permute-done((bf16[2,256,384]{2,1,0:T(8,128)(2,1)S(1)}, bf16[2,256,384]{2,1,0:T(8,128)(2,1)S(1)}, u32[]{:S(2)}, u32[]{:S(2)}) %collective-permute-start.9) | collective-permute-done | bytes 393248 | tf_op jit(solution)/shard_map/ppermute | solution.py:360
  72.0 1.3 %collective-permute-start.13 = (bf16[2,256,384]{2,1,0:T(8,128)(2,1)S(1)}, bf16[2,256,384]{2,1,0:T(8,128)(2,1)S(1)}, u32[]{:S(2)}, u32[]{:S(2)}) collective-permute-start(bf16[2,256,384]{2,1,0:T(8,128)(2,1)S(1)} %core_sum.4.sum_ref), channel_id=1, source_target_pairs={{0,2},{1,3},{2,0},{3,1},{4,6},{5,7},{6,4},{7,5},{8,10},{9,11},{10,... | collective-permute-start | bytes 1179656 | tf_op jit(solution)/shard_map/ppermute | solution.py:360
  73.5 4.4 %mlp.2 = (bf16[2,256,384]{2,1,0:T(8,128)(2,1)S(1)}, bf16[2,256,384]{2,1,0:T(8,128)(2,1)S(1)}) custom-call(f32[16,1536]{1,0:T(8,128)S(1)} %get-tuple-element.67.refs_0_.mods, bf16[2,256,384]{2,1,0:T(8,128)(2,1)S(1)} %middle.2.mine.mid_a, bf16[2,256,384]{2,1,0:T(8,128)(2,1)S(1)} %collective-permute-done.11.near, bf16[1536,1536]{1,0:T(8,128)(2,1)S(1)} %bitcast.10, ...), custom_call_target="tpu_custom_call" | custom-call | flops 1 | bytes 1 | tf_op jit(solution)/shard_map/mlp/pallas_call | solution.py:347
  78.1 5.3 %collective-permute-done.13.back_ref = bf16[2,256,384]{2,1,0:T(8,128)(2,1)S(1)} collective-permute-done((bf16[2,256,384]{2,1,0:T(8,128)(2,1)S(1)}, bf16[2,256,384]{2,1,0:T(8,128)(2,1)S(1)}, u32[]{:S(2)}, u32[]{:S(2)}) %collective-permute-start.13) | collective-permute-done | bytes 393248 | tf_op jit(solution)/shard_map/ppermute | solution.py:360
  83.8 1.1 collective-permute-start.14
  84.9 0.5 collective-permute-done.15.near
  85.4 4.4 %mlp.3 = (bf16[2,256,384]{2,1,0:T(8,128)(2,1)S(1)}, bf16[2,256,384]{2,1,0:T(8,128)(2,1)S(1)}) custom-call(f32[16,1536]{1,0:T(8,128)S(1)} %get-tuple-element.67.refs_0_.mods, bf16[2,256,384]{2,1,0:T(8,128)(2,1)S(1)} %middle.3.mine.mid_b, bf16[2,256,384]{2,1,0:T(8,128)(2,1)S(1)} %collective-permute-done.15.near, bf16[1536,1536]{1,0:T(8,128)(2,1)S(1)} %bitcast.10, ...), custom_call_target="tpu_custom_call" | custom-call | flops 1 | bytes 1 | tf_op jit(solution)/shard_map/mlp/pallas_call | solution.py:347
  89.8 3.4 %collective-permute-done.14.last_a = bf16[384,384]{1,0:T(8,128)(2,1)S(1)} collective-permute-done((bf16[384,384]{1,0:T(8,128)(2,1)S(1)}, bf16[384,384]{1,0:T(8,128)(2,1)S(1)}, u32[]{:S(2)}, u32[]{:S(2)}) %collective-permute-start.14) | collective-permute-done | bytes 294944 | tf_op jit(solution)/shard_map/ppermute | solution.py:360
  93.5 1.7 %collective-permute-done.16.right_ref.came_b = bf16[2,256,384]{2,1,0:T(8,128)(2,1)S(1)} collective-permute-done((bf16[2,256,384]{2,1,0:T(8,128)(2,1)S(1)}, bf16[2,256,384]{2,1,0:T(8,128)(2,1)S(1)}, u32[]{:S(2)}, u32[]{:S(2)}) %collective-permute-start.16) | collective-permute-done | bytes 393248 | tf_op jit(solution)/shard_map/ppermute | solution.py:360
  95.3 1.1 collective-permute-start.17
  96.4 5.9 %collective-permute-done.17.last_b = bf16[1,256,384]{2,1,0:T(8,128)(2,1)S(1)} collective-permute-done((bf16[1,256,384]{2,1,0:T(8,128)(2,1)S(1)}, bf16[1,256,384]{2,1,0:T(8,128)(2,1)S(1)}, u32[]{:S(2)}, u32[]{:S(2)}) %collective-permute-start.17) | collective-permute-done | bytes 196640 | tf_op jit(solution)/shard_map/ppermute | solution.py:360
  102.4 14.5 %all_to_all.11 = bf16[16,40,384]{2,1,0:T(8,128)(2,1)S(1)} all-to-all(bf16[16,40,384]{2,1,0:T(8,128)(2,1)S(1)} %final.1), channel_id=1, replica_groups={{0,4,16,20,32,36,48,52,64,68,80,84,96,100,112,116},{8,12,24,28,40,44,56..., dimensions={0} | all-to-all | bytes 983040 | tf_op jit(solution)/shard_map/all_to_all | solution.py:551
  116.9 0.6 copy.18
  117.6 0.8 slice.8
  (40 shorter events, 3.5 us)
Async XLA Ops:
  21.9 11.3 %collective-permute-start.1 = (bf16[16,40,384]{2,1,0:T(8,128)(2,1)S(1)}, bf16[16,40,384]{2,1,0:T(8,128)(2,1)S(1)}, u32[]{:S(2)}, u32[]{:S(2)}) collective-permute-start(bf16[16,40,384]{2,1,0:T(8,128)(2,1)S(1)} %all_to_all.10.refs_2_.own_ref), channel_id=1, source_target_pairs={{0,2},{1,3},{2,0},{3,1},{4,6},{5,7},{6,4},{7,5},{8,10},{9,11},{10,... | collective-permute-start | bytes 1474568 | tf_op jit(solution)/shard_map/ppermute | solution.py:360
  23.0 12.5 %collective-permute-start.3 = (bf16[16,40,384]{2,1,0:T(8,128)(2,1)S(1)}, bf16[16,40,384]{2,1,0:T(8,128)(2,1)S(1)}, u32[]{:S(2)}, u32[]{:S(2)}) collective-permute-start(bf16[16,40,384]{2,1,0:T(8,128)(2,1)S(1)} %all_to_all.10.refs_2_.own_ref), channel_id=1, source_target_pairs={{0,8},{4,12},{8,0},{12,4},{16,24},{20,28},{24,16},{28,20},{32,40},... | collective-permute-start | bytes 1474568 | tf_op jit(solution)/shard_map/ppermute | solution.py:360
  25.9 0.7 copy-start
  26.5 0.7 copy-start.1
  29.3 7.2 %collective-permute-start = (bf16[16,40,384]{2,1,0:T(8,128)(2,1)S(1)}, bf16[16,40,384]{2,1,0:T(8,128)(2,1)S(1)}, u32[]{:S(2)}, u32[]{:S(2)}) collective-permute-start(bf16[16,40,384]{2,1,0:T(8,128)(2,1)S(1)} %all_to_all.10.refs_2_.own_ref), channel_id=1, source_target_pairs={{0,1},{1,0},{2,3},{3,2},{4,5},{5,4},{6,7},{7,6},{8,9},{9,8},{10,11... | collective-permute-start | bytes 1474568 | tf_op jit(solution)/shard_map/ppermute | solution.py:360
  33.2 3.3 %collective-permute-start.2 = (bf16[16,40,384]{2,1,0:T(8,128)(2,1)S(1)}, bf16[16,40,384]{2,1,0:T(8,128)(2,1)S(1)}, u32[]{:S(2)}, u32[]{:S(2)}) collective-permute-start(bf16[16,40,384]{2,1,0:T(8,128)(2,1)S(1)} %collective-permute-done.1.refs_4_.far_ref), channel_id=1, source_target_pairs={{0,1},{1,0},{2,3},{3,2},{4,5},{5,4},{6,7},{7,6},{8,9},{9,8},{10,11... | collective-permute-start | bytes 1474568 | tf_op jit(solution)/shard_map/ppermute | solution.py:360
  35.5 11.4 %collective-permute-start.5 = (bf16[16,40,384]{2,1,0:T(8,128)(2,1)S(1)}, bf16[16,40,384]{2,1,0:T(8,128)(2,1)S(1)}, u32[]{:S(2)}, u32[]{:S(2)}) collective-permute-start(bf16[16,40,384]{2,1,0:T(8,128)(2,1)S(1)} %collective-permute-done.3.refs_2_), channel_id=1, source_target_pairs={{0,2},{1,3},{2,0},{3,1},{4,6},{5,7},{6,4},{7,5},{8,10},{9,11},{10,... | collective-permute-start | bytes 1474568 | tf_op jit(solution)/shard_map/ppermute | solution.py:360
  42.8 4.6 %collective-permute-start.4 = (bf16[16,40,384]{2,1,0:T(8,128)(2,1)S(1)}, bf16[16,40,384]{2,1,0:T(8,128)(2,1)S(1)}, u32[]{:S(2)}, u32[]{:S(2)}) collective-permute-start(bf16[16,40,384]{2,1,0:T(8,128)(2,1)S(1)} %collective-permute-done.3.refs_2_), channel_id=1, source_target_pairs={{0,1},{1,0},{2,3},{3,2},{4,5},{5,4},{6,7},{7,6},{8,9},{9,8},{10,11... | collective-permute-start | bytes 1474568 | tf_op jit(solution)/shard_map/ppermute | solution.py:360
  46.9 2.0 %collective-permute-start.6 = (bf16[16,40,384]{2,1,0:T(8,128)(2,1)S(1)}, bf16[16,40,384]{2,1,0:T(8,128)(2,1)S(1)}, u32[]{:S(2)}, u32[]{:S(2)}) collective-permute-start(bf16[16,40,384]{2,1,0:T(8,128)(2,1)S(1)} %collective-permute-done.5.refs_4_), channel_id=1, source_target_pairs={{0,1},{1,0},{2,3},{3,2},{4,5},{5,4},{6,7},{7,6},{8,9},{9,8},{10,11... | collective-permute-start | bytes 1474568 | tf_op jit(solution)/shard_map/ppermute | solution.py:360
  48.9 24.6 %slice-start.2 = ((s8[4718592]{0:T(1024)(128)(4,1)}), s8[4194304]{0:T(1024)(128)(4,1)S(1)}, s32[]{:S(2)}) async-start(s8[4718592]{0:T(1024)(128)(4,1)} %bitcast.11), calls=%async_computation.4 | async-start | bytes 8388608
  53.8 19.6 %slice-start.3 = ((s8[4718592]{0:T(1024)(128)(4,1)}), s8[524288]{0:T(1024)(128)(4,1)S(1)}, s32[]{:S(2)}) async-start(s8[4718592]{0:T(1024)(128)(4,1)} %bitcast.11), calls=%async_computation.5 | async-start | bytes 1048576
  57.8 1.8 %collective-permute-start.7 = (bf16[2,256,384]{2,1,0:T(8,128)(2,1)S(1)}, bf16[2,256,384]{2,1,0:T(8,128)(2,1)S(1)}, u32[]{:S(2)}, u32[]{:S(2)}) collective-permute-start(bf16[2,256,384]{2,1,0:T(8,128)(2,1)S(1)} %get-tuple-element.53), channel_id=1, source_target_pairs={{0,1},{1,0},{2,3},{3,2},{4,5},{5,4},{6,7},{7,6},{8,9},{9,8},{10,11... | collective-permute-start | bytes 1179656 | tf_op jit(solution)/shard_map/ppermute | solution.py:360
  59.6 13.8 %slice-start = ((s8[4718592]{0:T(1024)(128)(4,1)}), s8[4194304]{0:T(1024)(128)(4,1)S(1)}, s32[]{:S(2)}) async-start(s8[4718592]{0:T(1024)(128)(4,1)} %bitcast.9), calls=%async_computation.2 | async-start | bytes 8388608
  59.7 13.7 %slice-start.1 = ((s8[4718592]{0:T(1024)(128)(4,1)}), s8[524288]{0:T(1024)(128)(4,1)S(1)}, s32[]{:S(2)}) async-start(s8[4718592]{0:T(1024)(128)(4,1)} %bitcast.9), calls=%async_computation.3 | async-start | bytes 1048576
  59.7 11.5 %collective-permute-start.9 = (bf16[2,256,384]{2,1,0:T(8,128)(2,1)S(1)}, bf16[2,256,384]{2,1,0:T(8,128)(2,1)S(1)}, u32[]{:S(2)}, u32[]{:S(2)}) collective-permute-start(bf16[2,256,384]{2,1,0:T(8,128)(2,1)S(1)} %core_sum.3.sum_ref), channel_id=1, source_target_pairs={{0,2},{1,3},{2,0},{3,1},{4,6},{5,7},{6,4},{7,5},{8,10},{9,11},{10,... | collective-permute-start | bytes 1179656 | tf_op jit(solution)/shard_map/ppermute | solution.py:360
  65.4 6.5 %collective-permute-start.10 = (bf16[2,256,384]{2,1,0:T(8,128)(2,1)S(1)}, bf16[2,256,384]{2,1,0:T(8,128)(2,1)S(1)}, u32[]{:S(2)}, u32[]{:S(2)}) collective-permute-start(bf16[2,256,384]{2,1,0:T(8,128)(2,1)S(1)} %get-tuple-element.60), channel_id=1, source_target_pairs={{0,1},{1,0},{2,3},{3,2},{4,5},{5,4},{6,7},{7,6},{8,9},{9,8},{10,11... | collective-permute-start | bytes 1179656 | tf_op jit(solution)/shard_map/ppermute | solution.py:360
  71.3 2.1 %collective-permute-start.11 = (bf16[2,256,384]{2,1,0:T(8,128)(2,1)S(1)}, bf16[2,256,384]{2,1,0:T(8,128)(2,1)S(1)}, u32[]{:S(2)}, u32[]{:S(2)}) collective-permute-start(bf16[2,256,384]{2,1,0:T(8,128)(2,1)S(1)} %middle.2.mine.mid_a), channel_id=1, source_target_pairs={{0,1},{1,0},{2,3},{3,2},{4,5},{5,4},{6,7},{7,6},{8,9},{9,8},{10,11... | collective-permute-start | bytes 1179656 | tf_op jit(solution)/shard_map/ppermute | solution.py:360
  71.4 2.0 %collective-permute-start.8 = (bf16[2,128,384]{2,1,0:T(8,128)(2,1)S(1)}, bf16[2,128,384]{2,1,0:T(8,128)(2,1)S(1)}, u32[]{:S(2)}, u32[]{:S(2)}) collective-permute-start(bf16[2,128,384]{2,1,0:T(8,128)(2,1)S(1)} %get-tuple-element.56), channel_id=1, source_target_pairs={{0,1},{1,0},{2,3},{3,2},{4,5},{5,4},{6,7},{7,6},{8,9},{9,8},{10,11... | collective-permute-start | bytes 589832 | tf_op jit(solution)/shard_map/ppermute | solution.py:360
  72.0 11.4 %collective-permute-start.13 = (bf16[2,256,384]{2,1,0:T(8,128)(2,1)S(1)}, bf16[2,256,384]{2,1,0:T(8,128)(2,1)S(1)}, u32[]{:S(2)}, u32[]{:S(2)}) collective-permute-start(bf16[2,256,384]{2,1,0:T(8,128)(2,1)S(1)} %core_sum.4.sum_ref), channel_id=1, source_target_pairs={{0,2},{1,3},{2,0},{3,1},{4,6},{5,7},{6,4},{7,5},{8,10},{9,11},{10,... | collective-permute-start | bytes 1179656 | tf_op jit(solution)/shard_map/ppermute | solution.py:360
  77.9 5.8 %collective-permute-start.12 = (bf16[2,256,384]{2,1,0:T(8,128)(2,1)S(1)}, bf16[2,256,384]{2,1,0:T(8,128)(2,1)S(1)}, u32[]{:S(2)}, u32[]{:S(2)}) collective-permute-start(bf16[2,256,384]{2,1,0:T(8,128)(2,1)S(1)} %get-tuple-element.64), channel_id=1, source_target_pairs={{0,1},{1,0},{2,3},{3,2},{4,5},{5,4},{6,7},{7,6},{8,9},{9,8},{10,11... | collective-permute-start | bytes 1179656 | tf_op jit(solution)/shard_map/ppermute | solution.py:360
  83.6 1.8 %collective-permute-start.15 = (bf16[2,256,384]{2,1,0:T(8,128)(2,1)S(1)}, bf16[2,256,384]{2,1,0:T(8,128)(2,1)S(1)}, u32[]{:S(2)}, u32[]{:S(2)}) collective-permute-start(bf16[2,256,384]{2,1,0:T(8,128)(2,1)S(1)} %middle.3.mine.mid_b), channel_id=1, source_target_pairs={{0,1},{1,0},{2,3},{3,2},{4,5},{5,4},{6,7},{7,6},{8,9},{9,8},{10,11... | collective-permute-start | bytes 1179656 | tf_op jit(solution)/shard_map/ppermute | solution.py:360
  83.8 9.5 %collective-permute-start.14 = (bf16[384,384]{1,0:T(8,128)(2,1)S(1)}, bf16[384,384]{1,0:T(8,128)(2,1)S(1)}, u32[]{:S(2)}, u32[]{:S(2)}) collective-permute-start(bf16[384,384]{1,0:T(8,128)(2,1)S(1)} %away.1), channel_id=1, source_target_pairs={{0,2},{1,3},{2,0},{3,1},{4,6},{5,7},{6,4},{7,5},{8,10},{9,11},{10,... | collective-permute-start | bytes 884744 | tf_op jit(solution)/shard_map/ppermute | solution.py:360
  93.4 1.8 %collective-permute-start.16 = (bf16[2,256,384]{2,1,0:T(8,128)(2,1)S(1)}, bf16[2,256,384]{2,1,0:T(8,128)(2,1)S(1)}, u32[]{:S(2)}, u32[]{:S(2)}) collective-permute-start(bf16[2,256,384]{2,1,0:T(8,128)(2,1)S(1)} %get-tuple-element.73), channel_id=1, source_target_pairs={{0,1},{1,0},{2,3},{3,2},{4,5},{5,4},{6,7},{7,6},{8,9},{9,8},{10,11... | collective-permute-start | bytes 1179656 | tf_op jit(solution)/shard_map/ppermute | solution.py:360
  95.3 7.0 %collective-permute-start.17 = (bf16[1,256,384]{2,1,0:T(8,128)(2,1)S(1)}, bf16[1,256,384]{2,1,0:T(8,128)(2,1)S(1)}, u32[]{:S(2)}, u32[]{:S(2)}) collective-permute-start(bf16[1,256,384]{2,1,0:T(8,128)(2,1)S(1)} %core_sum.5), channel_id=1, source_target_pairs={{0,2},{1,3},{2,0},{3,1},{4,6},{5,7},{6,4},{7,5},{8,10},{9,11},{10,... | collective-permute-start | bytes 589832 | tf_op jit(solution)/shard_map/ppermute | solution.py:360

commit v4 on v3

--- a/solution.py
+++ b/solution.py
@@ -12,6 +12,7 @@
 F32 = jnp.float32
 HIDDEN_BIAS = -32768.0
 TXT_PAD = 8
+PARTS = (1, 2, 0)
 VMEM_LIMIT = 28 << 20
 VM = pl.BlockSpec(memory_space=pltpu.VMEM)
 SM = pl.BlockSpec(memory_space=pltpu.SMEM)
@@ -48,11 +49,17 @@
 
 
 def prep_kernel(step_ref, length_ref, *refs):
-    mods_ref, gains_ref, bias_ref = refs[6:9]
-    copies = fetch(refs[:6], refs[9:15], refs[15])
-    for copy in copies:
+    mods_ref, gains_ref, bias_ref, wimg_ref, wtxt_ref = refs[8:13]
+    part = refs[6].shape[2]
+    sources, targets = list(refs[:6]), list(refs[13:19])
+    for w, w_ref in zip(refs[6:8], (wimg_ref, wtxt_ref)):
+        for i, which in enumerate(PARTS):
+            sources.append(w.at[which])
+            targets.append(w_ref.at[:, i * part : (i + 1) * part])
+    copies = fetch(sources, targets, refs[19])
+    for copy in copies[:6]:
         copy.wait()
-    itab, ttab, gqi, gki, gqt, gkt = refs[9:15]
+    itab, ttab, gqi, gki, gqt, gkt = refs[13:19]
     tile = lax.axis_index("tile")
     request = (tile >> 2) * 2 + (tile & 1)
     step, length = step_ref[request], length_ref[request]
@@ -69,25 +76,30 @@
         sender = (source >> 1) * 4 + parity * 2 + (source & 1)
         seen = (slot < 5) & (sender * 5 + slot < length)
         bias_ref[side] = jnp.where(seen, 0.0, HIDDEN_BIAS).astype(BF)
-
-
-def prep_call(step_index, text_length, tables, gains):
+    for copy in copies[6:]:
+        copy.wait()
+
+
+def prep_call(step_index, text_length, tables, gains, weights):
     width = tables[0].shape[2]
+    wide = jax.ShapeDtypeStruct((width, 3 * weights[0].shape[2]), BF)
     return pl.pallas_call(
         prep_kernel,
         out_shape=[
             jax.ShapeDtypeStruct((16, width), F32),
             jax.ShapeDtypeStruct((8, 128), F32),
             jax.ShapeDtypeStruct((2, 128, 128), BF),
+            wide,
+            wide,
         ],
-        in_specs=[SM, SM] + [HB] * 6,
-        out_specs=[VM] * 3,
+        in_specs=[SM, SM] + [HB] * 8,
+        out_specs=[VM] * 5,
         scratch_shapes=[pltpu.VMEM(x.shape, x.dtype) for x in (*tables, *gains)]
-        + [pltpu.SemaphoreType.DMA((6,))],
+        + [pltpu.SemaphoreType.DMA((12,))],
         compiler_params=pltpu.CompilerParams(vmem_limit_bytes=VMEM_LIMIT),
         cost_estimate=COST,
         name="prep",
-    )(step_index, text_length, *pinned(*tables, *gains))
+    )(step_index, text_length, *pinned(*tables, *gains, *weights))
 
 
 def norm_rows(raw_ref, acts_ref, start, count, shift, scale, block=32):
@@ -103,7 +115,7 @@
         acts_ref[rows, :] = (moved * lax.rsqrt(spread + 1e-06) * gain + shift).astype(BF)
         return carry
 
-    lax.fori_loop(0, count // block, body, 0, unroll=2)
+    lax.fori_loop(0, count // block, body, 0, unroll=4)
 
 
 def head_scale(values, group):
@@ -125,17 +137,8 @@
 
 
 def qkv_kernel(begin, sources, parts, *refs):
-    mods, gains, x0, x1, x2, x3, wimg, wtxt = refs[:8]
-    outs, (wimg_ref, wtxt_ref, raw_ref, acts_ref, sems) = refs[8:-5], refs[-5:]
-    copies = fetch(
-        [w.at[i] for w in (wtxt, wimg) for i in parts],
-        [
-            w.at[:, i * x0.shape[2] : (i + 1) * x0.shape[2]]
-            for w in (wtxt_ref, wimg_ref)
-            for i in range(len(parts))
-        ],
-        sems,
-    )
+    mods, gains, x0, x1, x2, x3, wimg_ref, wtxt_ref = refs[:8]
+    outs, (raw_ref, acts_ref) = refs[8:-2], refs[-2:]
     blk = lax.axis_index("blk")
     part = x0.shape[2]
     image_rows = x0.shape[1] - TXT_PAD
@@ -149,13 +152,8 @@
     norm_rows(raw_ref, acts_ref, 0, img, mods[0:1, :], mods[1:2, :])
     group = group_matrix()
     kv_ref = outs[-1]
-    for w_ref, first, last, row, waits in (
-        (wtxt_ref, img, img + txt, 2, copies[: len(parts)]),
-        (wimg_ref, 0, img, 0, copies[len(parts) :]),
-    ):
-        for copy in waits:
-            copy.wait()
-        projected = dot(acts_ref[first:last, :], w_ref[...])
+    for w_ref, first, last, row in ((wtxt_ref, img, img + txt, 2), (wimg_ref, 0, img, 0)):
+        projected = dot(acts_ref[first:last, :], w_ref[:, : len(parts) * part])
         for i, which in enumerate(parts):
             values = projected[:, i * part : (i + 1) * part]
             if which == 2:
@@ -175,19 +173,16 @@
     outs = [jax.ShapeDtypeStruct((2, rows, part), BF)]
     if 0 in parts:
         outs = [jax.ShapeDtypeStruct((rows, part), BF)] + outs
-    weight = pltpu.VMEM((width, len(parts) * part), BF)
     return pl.pallas_call(
         functools.partial(qkv_kernel, begin, sources, parts),
         out_shape=outs,
-        in_specs=[VM] * 6 + [HB] * 2,
+        in_specs=[VM] * 8,
         out_specs=[VM] * len(outs),
-        scratch_shapes=[weight, weight]
-        + [pltpu.VMEM((rows, width), BF)] * 2
-        + [pltpu.SemaphoreType.DMA((2 * len(parts),))],
+        scratch_shapes=[pltpu.VMEM((rows, width), BF)] * 2,
         compiler_params=pltpu.CompilerParams(vmem_limit_bytes=VMEM_LIMIT),
         cost_estimate=COST,
         name="qkv",
-    )(mods, gains, *pieces, *pinned(*weights))
+    )(mods, gains, *pieces, *weights)
 
 
 def head_scores(query, keys, lane, one_lane, head):
@@ -257,8 +252,7 @@
     groups = len(counts)
     count = sum(counts)
     mods, bias_ref, q_ref, top_ref, sum_ref, out_ref, kv_ref = refs[:7]
-    w_refs, sems = refs[7 + 3 * groups : -1], refs[-1]
-    copies = fetch(refs[7 : 7 + groups], w_refs, sems)
+    w_refs = refs[7 : 7 + groups]
     part = q_ref.shape[1]
     lane, one_lane = lane_masks(count)
     bias = hiding(bias_ref[1], kv_ref.shape[1] - bias_ref.shape[1])
@@ -282,7 +276,6 @@
     att = jnp.concatenate(att, axis=1)
     first = 0
     for i, (rows, row) in enumerate(zip(counts, gate_rows)):
-        copies[i].wait()
         outs = refs[7 + groups + 2 * i : 9 + groups + 2 * i]
         project_out(att[first : first + rows], mods[row : row + 1, :], w_refs[i], *outs)
         first += rows
@@ -316,14 +309,12 @@
     return pl.pallas_call(
         functools.partial(attend_kernel, start, counts, gate_rows),
         out_shape=shapes,
-        in_specs=[VM] * 7 + [HB] * len(weights),
+        in_specs=[VM] * (7 + len(weights)),
         out_specs=[VM] * len(shapes),
-        scratch_shapes=[pltpu.VMEM(weight.shape, BF) for weight in weights]
-        + [pltpu.SemaphoreType.DMA((len(weights),))],
         compiler_params=pltpu.CompilerParams(vmem_limit_bytes=VMEM_LIMIT),
         cost_estimate=COST,
         name="attend",
-    )(mods, bias, query, *state, keys, *pinned(*weights))
+    )(mods, bias, query, *state, keys, *weights)
 
 
 def mlp_kernel(mods, mine, near, up_ref, down_ref, keep_ref, send_ref, raw_ref, acts_ref):
@@ -432,10 +423,10 @@
 def final_kernel(image_ref, text_ref, mid_b, keep_b, came_b, last_b, out_ref):
     sources, slots, part = out_ref.shape
     image_rows = slots - TXT_PAD
-    half = sources // 2
-    out_ref[:half, :image_rows, :] = image_ref[...].reshape(half, image_rows, part)
+    first = image_ref.shape[0] // image_rows
+    out_ref[:first, :image_rows, :] = image_ref[...].reshape(first, image_rows, part)
     value = add(mid_b[0], keep_b[0], came_b[0], last_b[0])
-    out_ref[half:, :image_rows, :] = value.reshape(half, image_rows, part)
+    out_ref[first:, :image_rows, :] = value.reshape(sources - first, image_rows, part)
     out_ref[:, image_rows:, :] = text_ref[...]
 
 
@@ -486,27 +477,27 @@
     far = swap(own, "blk", 4, 2)
     other = swap(own, "tile", tiles, 2)
     near = swap(own, "blk", 4, 1)
-    mods, head_gains, bias = prep_call(after(step_index, own), text_length, tables, gains)
+    mods, head_gains, bias, *wide = prep_call(after(step_index, own), text_length, tables, gains, weights)
 
     def tied(*others):
         return after(mods, *others)
 
     def project(mods, pieces, parts):
-        return qkv_call(mods, head_gains, pieces, (0, 0, 0, 0), requests, weights, parts)
+        return qkv_call(mods, head_gains, pieces, (0, 0, 0, 0), requests, wide, parts)
 
     far = after(far, mods)
     other = after(other, far)
     other_far = swap(other, "blk", 4, 2)
     diag = swap(far, "blk", 4, 1)
-    query, mine = project(mods, [own, near, far, diag], (1, 2, 0))
+    query, mine = project(mods, [own, near, far, diag], PARTS)
     other_near = swap(after(other, query), "blk", 4, 1)
     state = own_call(bias, query, mine)
     other_far = after(other_far, state[0])
     other_diag = swap(other_far, "blk", 4, 1)
-    keys = project(tied(state[0]), [other, other_near, other_far, other_diag], (1, 2))[0]
-
-    half = requests // 2
-    rows = half * image_rows
+    keys = project(tied(state[0]), [other, other_near, other_far, other_diag], PARTS[:2])[0]
+
+    first = requests * 10 // 16
+    rows_a, rows_b = first * image_rows, (requests - first) * image_rows
     txt_rows = requests * TXT_PAD
 
     def attend(mods, *groups):
@@ -514,36 +505,36 @@
 
     def middle(begin, sums, back):
         args = [own, far, sums, back]
-        return small_call(functools.partial(middle_kernel, begin), "middle", [(2, rows, part)], args)[0]
-
-    keep_a, send_a = attend(mods, 0, (rows,), (2,), (attn_out_image,))
+        return small_call(functools.partial(middle_kernel, begin), "middle", [sums.shape], args)[0]
+
+    keep_a, send_a = attend(mods, 0, (rows_a,), (2,), (attn_out_image,))
     came_a = swap(send_a, "blk", 4, 1)
     sum_a = core_sum(keep_a, came_a, 0)
     back_a = swap(sum_a, "blk", 4, 2)
     keep_b, send_b, keep_t, send_t = attend(
-        tied(sum_a), rows, (rows, txt_rows), (2, 10), (attn_out_image, attn_out_text)
+        tied(sum_a), rows_a, (rows_b, txt_rows), (2, 10), (attn_out_image, attn_out_text)
     )
     came_b = swap(send_b, "blk", 4, 1)
-    mid_a = middle(0, sum_a, after(back_a, keep_b))
+    sum_b = core_sum(keep_b, came_b, 0)
+    mid_a = middle(0, sum_a, after(back_a, sum_b))
     near_a = swap(mid_a, "blk", 4, 1)
-    sum_b = core_sum(after(keep_b, mid_a), came_b, 0)
     back_b = swap(sum_b, "blk", 4, 2)
     came_t = swap(send_t, "blk", 4, 1)
     came_t = after(came_t, sum_b)
     down_a, send_a = mlp_call(tied(came_t), mid_a, near_a, up_weight, down_weight)
     came_a = swap(send_a, "blk", 4, 1)
-    mid_b = middle(half, sum_b, after(back_b, down_a))
+    mid_b = middle(first, sum_b, after(back_b, down_a))
     near_b = swap(mid_b, "blk", 4, 1)
-    args = [after(down_a, mid_b), came_a, keep_t, came_t]
-    away_a = small_call(away_kernel, "away", [(rows + txt_rows, part)], args)[0]
+    args = [after(down_a, near_b), came_a, keep_t, came_t]
+    away_a = small_call(away_kernel, "away", [(rows_a + txt_rows, part)], args)[0]
     last_a = swap(away_a, "blk", 4, 2)
     down_b, send_b = mlp_call(tied(away_a), mid_b, near_b, up_weight, down_weight)
     args = [own, keep_t, came_t, mid_a, down_a, came_a, after(last_a, down_b)]
     image_a, text_out = small_call(
-        first_kernel, "first", [(rows, part), (requests, TXT_PAD, part)], args
+        first_kernel, "first", [(rows_a, part), (requests, TXT_PAD, part)], args
     )
-    came_b = swap(after(send_b, image_a), "blk", 4, 1)
-    away_b = core_sum(down_b, came_b, 1)
+    came_b = swap(send_b, "blk", 4, 1)
+    away_b = core_sum(after(down_b, image_a), came_b, 1)
     last_b = swap(away_b, "blk", 4, 2)
 
     args = [image_a, text_out, mid_b, down_b, came_b, last_b]

time: 119 us -> 114 us (0.958)
  Pallas kernels: 36.4 us -> 34.2 us
    pallas_call x2, Pallas kernels: 11.2 us -> 8.95 us  [qkv_call(): pl.pallas_call(functools.partial(qkv_kernel, begin, sources, parts), out_...]
    pallas_call x1, Pallas kernels: 2.09 us -> 4.01 us  [prep_call(): pl.pallas_call(prep_kernel, out_shape=[jax.ShapeDtypeStruct((16, width),...]
    pallas_call x2, Pallas kernels: 8.56 us -> 6.88 us  [attend_call(): pl.pallas_call(functools.partial(attend_kernel, start, counts, gate_rows)...]
where the time goes in v4:
time: 114 us
  Pallas kernels  34.2 us (30%)
  blocking collectives  34.1 us (30%)
  waiting for transfers between devices  31.3 us (27%)
  starting transfers between devices  10.8 us (9%)
  local copies, waits for them, and re-layouts  2.77 us (2%)
    ppermute x18, waiting for transfers between devices, swap(): return lax.ppermute(values, axis, [(i, i ^ bit) for i in range(size)])  31.3 us
    all_to_all x1, blocking collectives, per_device(): lax.all_to_all(packed, 'tile', 0, 0, axis_index_groups=groups, tiled=True)  20.3 us
    all_to_all x1, blocking collectives, per_device(): lax.all_to_all(result, 'tile', 0, 0, axis_index_groups=groups, tiled=True)  13.8 us
    ppermute x18, starting transfers between devices, swap(): return lax.ppermute(values, axis, [(i, i ^ bit) for i in range(size)])  10.8 us
    pallas_call x2, Pallas kernels, qkv_call(): pl.pallas_call(functools.partial(qkv_kernel, begin, sources, parts), out_...  8.95 us
    pallas_call x2, Pallas kernels, mlp_call(): pl.pallas_call(mlp_kernel, out_shape=[shape, shape], in_specs=[VM] * 5, o...  8.66 us
    pallas_call x2, Pallas kernels, attend_call(): pl.pallas_call(functools.partial(attend_kernel, start, counts, gate_rows)...  6.88 us
    pallas_call x1, Pallas kernels, prep_call(): pl.pallas_call(prep_kernel, out_shape=[jax.ShapeDtypeStruct((16, width),...  4.01 us
  transfers between devices with their start and end apart: 18, of which 12 were waited for; matrix products, arithmetic and copies ran while one was open for 0% of the time, Pallas kernels for 22%

profile of v4, /device:TPU:0, one launch (start us, length us, event | category | flops | bytes accessed | tf_op | source)
XLA Modules:
  0.0 114.0 jit_solution(17029461665038207935)
XLA Ops:
  0.6 1.1 pack.1
  1.7 20.3 %all_to_all.10.refs_2_.own_ref = bf16[16,40,384]{2,1,0:T(8,128)(2,1)S(1)} all-to-all(bf16[16,40,384]{2,1,0:T(8,128)(2,1)S(1)} %pack.1), channel_id=1, replica_groups={{0,4,16,20,32,36,48,52,64,68,80,84,96,100,112,116},{8,12,24,28,40,44,56..., dimensions={0} | all-to-all | bytes 983040 | tf_op jit(solution)/shard_map/all_to_all | solution.py:476
  21.9 1.0 collective-permute-start.1
  23.0 2.9 %collective-permute-start.3 = (bf16[16,40,384]{2,1,0:T(8,128)(2,1)S(1)}, bf16[16,40,384]{2,1,0:T(8,128)(2,1)S(1)}, u32[]{:S(2)}, u32[]{:S(2)}) collective-permute-start(bf16[16,40,384]{2,1,0:T(8,128)(2,1)S(1)} %all_to_all.10.refs_2_.own_ref), channel_id=1, source_target_pairs={{0,8},{4,12},{8,0},{12,4},{16,24},{20,28},{24,16},{28,20},{32,40},... | collective-permute-start | bytes 1474568 | tf_op jit(solution)/shard_map/ppermute | solution.py:351
  25.9 0.7 copy-done.2
  26.5 0.7 copy-done.3
  27.2 4.0 %prep.1 = (f32[16,1536]{1,0:T(8,128)S(1)}, f32[8,128]{1,0:T(8,128)S(1)}, bf16[2,128,128]{2,1,0:T(8,128)(2,1)S(1)}, bf16[1536,1152]{1,0:T(8,128)(2,1)S(1)}, bf16[1536,1152]{1,0:T(8,128)(2,1)S(1)}) custom-call(s32[16]{0:T(128)S(1)} %copy-done.2, s32[16]{0:T(128)S(1)} %copy-done.3, bf16[6,28,1536]{2,1,0:T(8,128)(2,1)} %bitcast.15, ...), custom_call_target="tpu_custom_call" | custom-call | flops 1 | bytes 1 | tf_op jit(solution)/shard_map/prep/pallas_call | solution.py:86
  31.3 1.9 %collective-permute-done.1.refs_4_.far_ref = bf16[16,40,384]{2,1,0:T(8,128)(2,1)S(1)} collective-permute-done((bf16[16,40,384]{2,1,0:T(8,128)(2,1)S(1)}, bf16[16,40,384]{2,1,0:T(8,128)(2,1)S(1)}, u32[]{:S(2)}, u32[]{:S(2)}) %collective-permute-start.1) | collective-permute-done | bytes 491552 | tf_op jit(solution)/shard_map/ppermute | solution.py:351
  33.2 2.2 %collective-permute-done.3.refs_2_ = bf16[16,40,384]{2,1,0:T(8,128)(2,1)S(1)} collective-permute-done((bf16[16,40,384]{2,1,0:T(8,128)(2,1)S(1)}, bf16[16,40,384]{2,1,0:T(8,128)(2,1)S(1)}, u32[]{:S(2)}, u32[]{:S(2)}) %collective-permute-start.3) | collective-permute-done | bytes 491552 | tf_op jit(solution)/shard_map/ppermute | solution.py:351
  35.5 1.0 collective-permute-start.5
  36.5 5.1 %qkv.2 = (bf16[640,384]{1,0:T(8,128)(2,1)S(1)}, bf16[2,640,384]{2,1,0:T(8,128)(2,1)S(1)}) custom-call(f32[16,1536]{1,0:T(8,128)S(1)} %get-tuple-element.69.refs_0_.mods, f32[8,128]{1,0:T(8,128)S(1)} %get-tuple-element.42.refs_1_, bf16[16,40,384]{2,1,0:T(8,128)(2,1)S(1)} %all_to_all.10.refs_2_.own_ref, bf16[16,40,384]{2,1,0:T(8,128)(2,1)S(1)} %collective-permute-done.refs_3_, ...), custom_call_target="tpu_custom_call" | custom-call | flops 1 | bytes 1 | tf_op jit(solution)/shard_map/qkv/pallas_call | solution.py:176
  41.7 3.7 %attend_own.1 = (f32[640,384]{1,0:T(8,128)S(1)}, f32[640,384]{1,0:T(8,128)S(1)}, f32[640,384]{1,0:T(8,128)S(1)}) custom-call(bf16[2,128,128]{2,1,0:T(8,128)(2,1)S(1)} %get-tuple-element.41.bias_ref.refs_1_, bf16[640,384]{1,0:T(8,128)(2,1)S(1)} %get-tuple-element.46.q_ref.refs_2_, bf16[2,640,384]{2,1,0:T(8,128)(2,1)S(1)} %get-tuple-element.47.kv_ref), custom_call_target="tpu_custom_call" | custom-call | flops 1 | bytes 1 | tf_op jit(solution)/shard_map/attend_own/pallas_call | solution.py:240
  45.4 1.4 %collective-permute-done.5.refs_4_ = bf16[16,40,384]{2,1,0:T(8,128)(2,1)S(1)} collective-permute-done((bf16[16,40,384]{2,1,0:T(8,128)(2,1)S(1)}, bf16[16,40,384]{2,1,0:T(8,128)(2,1)S(1)}, u32[]{:S(2)}, u32[]{:S(2)}) %collective-permute-start.5) | collective-permute-done | bytes 491552 | tf_op jit(solution)/shard_map/ppermute | solution.py:351
  46.9 1.9 %collective-permute-done.6.refs_5_ = bf16[16,40,384]{2,1,0:T(8,128)(2,1)S(1)} collective-permute-done((bf16[16,40,384]{2,1,0:T(8,128)(2,1)S(1)}, bf16[16,40,384]{2,1,0:T(8,128)(2,1)S(1)}, u32[]{:S(2)}, u32[]{:S(2)}) %collective-permute-start.6) | collective-permute-done | bytes 491552 | tf_op jit(solution)/shard_map/ppermute | solution.py:351
  48.7 3.8 %qkv.3.refs_6_ = bf16[2,640,384]{2,1,0:T(8,128)(2,1)S(1)} custom-call(f32[16,1536]{1,0:T(8,128)S(1)} %get-tuple-element.69.refs_0_.mods, f32[8,128]{1,0:T(8,128)S(1)} %get-tuple-element.42.refs_1_, bf16[16,40,384]{2,1,0:T(8,128)(2,1)S(1)} %collective-permute-done.3.refs_2_, bf16[16,40,384]{2,1,0:T(8,128)(2,1)S(1)} %collective-permute-done.4.refs_3_, ...), custom_call_target="tpu_custom_call" | custom-call | flops 1 | bytes 1 | tf_op jit(solution)/shard_map/qkv/pallas_call | solution.py:176
  52.6 3.3 %attend.2 = (bf16[2,320,384]{2,1,0:T(8,128)(2,1)S(1)}, bf16[2,320,384]{2,1,0:T(8,128)(2,1)S(1)}) custom-call(f32[16,1536]{1,0:T(8,128)S(1)} %get-tuple-element.69.refs_0_.mods, bf16[2,128,128]{2,1,0:T(8,128)(2,1)S(1)} %get-tuple-element.41.bias_ref.refs_1_, bf16[640,384]{1,0:T(8,128)(2,1)S(1)} %get-tuple-element.46.q_ref.refs_2_, ...), custom_call_target="tpu_custom_call" | custom-call | flops 1 | bytes 1 | tf_op jit(solution)/shard_map/attend/pallas_call | solution.py:309
  56.1 1.7 %collective-permute-done.7.right_ref = bf16[2,320,384]{2,1,0:T(8,128)(2,1)S(1)} collective-permute-done((bf16[2,320,384]{2,1,0:T(8,128)(2,1)S(1)}, bf16[2,320,384]{2,1,0:T(8,128)(2,1)S(1)}, u32[]{:S(2)}, u32[]{:S(2)}) %collective-permute-start.7) | collective-permute-done | bytes 491552 | tf_op jit(solution)/shard_map/ppermute | solution.py:351
  58.0 1.1 collective-permute-start.10
  59.1 3.6 %attend.3 = (bf16[2,192,384]{2,1,0:T(8,128)(2,1)S(1)}, bf16[2,192,384]{2,1,0:T(8,128)(2,1)S(1)}, bf16[2,128,384]{2,1,0:T(8,128)(2,1)S(1)}, bf16[2,128,384]{2,1,0:T(8,128)(2,1)S(1)}) custom-call(f32[16,1536]{1,0:T(8,128)S(1)} %get-tuple-element.69.refs_0_.mods, bf16[2,128,128]{2,1,0:T(8,128)(2,1)S(1)} %get-tuple-element.41.bias_ref.refs_1_, ...), custom_call_target="tpu_custom_call" | custom-call | flops 1 | bytes 1 | tf_op jit(solution)/shard_map/attend/pallas_call | solution.py:309
  62.8 1.6 %collective-permute-done.9.right_ref = bf16[2,192,384]{2,1,0:T(8,128)(2,1)S(1)} collective-permute-done((bf16[2,192,384]{2,1,0:T(8,128)(2,1)S(1)}, bf16[2,192,384]{2,1,0:T(8,128)(2,1)S(1)}, u32[]{:S(2)}, u32[]{:S(2)}) %collective-permute-start.9) | collective-permute-done | bytes 294944 | tf_op jit(solution)/shard_map/ppermute | solution.py:351
  64.4 6.9 %collective-permute-done.10.back_ref = bf16[2,320,384]{2,1,0:T(8,128)(2,1)S(1)} collective-permute-done((bf16[2,320,384]{2,1,0:T(8,128)(2,1)S(1)}, bf16[2,320,384]{2,1,0:T(8,128)(2,1)S(1)}, u32[]{:S(2)}, u32[]{:S(2)}) %collective-permute-start.10) | collective-permute-done | bytes 491552 | tf_op jit(solution)/shard_map/ppermute | solution.py:351
  72.1 1.0 collective-permute-start.13
  73.8 5.3 %mlp.2 = (bf16[2,320,384]{2,1,0:T(8,128)(2,1)S(1)}, bf16[2,320,384]{2,1,0:T(8,128)(2,1)S(1)}) custom-call(f32[16,1536]{1,0:T(8,128)S(1)} %get-tuple-element.69.refs_0_.mods, bf16[2,320,384]{2,1,0:T(8,128)(2,1)S(1)} %middle.2.mine.mid_a, bf16[2,320,384]{2,1,0:T(8,128)(2,1)S(1)} %collective-permute-done.11.near, bf16[1536,1536]{1,0:T(8,128)(2,1)S(1)} %bitcast.10, ...), custom_call_target="tpu_custom_call" | custom-call | flops 1 | bytes 1 | tf_op jit(solution)/shard_map/mlp/pallas_call | solution.py:338
  79.3 1.8 %collective-permute-done.13.back_ref = bf16[2,192,384]{2,1,0:T(8,128)(2,1)S(1)} collective-permute-done((bf16[2,192,384]{2,1,0:T(8,128)(2,1)S(1)}, bf16[2,192,384]{2,1,0:T(8,128)(2,1)S(1)}, u32[]{:S(2)}, u32[]{:S(2)}) %collective-permute-start.13) | collective-permute-done | bytes 294944 | tf_op jit(solution)/shard_map/ppermute | solution.py:351
  81.3 1.6 %collective-permute-done.14.near = bf16[2,192,384]{2,1,0:T(8,128)(2,1)S(1)} collective-permute-done((bf16[2,192,384]{2,1,0:T(8,128)(2,1)S(1)}, bf16[2,192,384]{2,1,0:T(8,128)(2,1)S(1)}, u32[]{:S(2)}, u32[]{:S(2)}) %collective-permute-start.14) | collective-permute-done | bytes 294944 | tf_op jit(solution)/shard_map/ppermute | solution.py:351
  83.0 1.1 collective-permute-start.15
  84.1 3.3 %mlp.3 = (bf16[2,192,384]{2,1,0:T(8,128)(2,1)S(1)}, bf16[2,192,384]{2,1,0:T(8,128)(2,1)S(1)}) custom-call(f32[16,1536]{1,0:T(8,128)S(1)} %get-tuple-element.69.refs_0_.mods, bf16[2,192,384]{2,1,0:T(8,128)(2,1)S(1)} %middle.3.mine.mid_b, bf16[2,192,384]{2,1,0:T(8,128)(2,1)S(1)} %collective-permute-done.14.near, bf16[1536,1536]{1,0:T(8,128)(2,1)S(1)} %bitcast.10, ...), custom_call_target="tpu_custom_call" | custom-call | flops 1 | bytes 1 | tf_op jit(solution)/shard_map/mlp/pallas_call | solution.py:338
  87.6 5.6 %collective-permute-done.15.last_a = bf16[448,384]{1,0:T(8,128)(2,1)S(1)} collective-permute-done((bf16[448,384]{1,0:T(8,128)(2,1)S(1)}, bf16[448,384]{1,0:T(8,128)(2,1)S(1)}, u32[]{:S(2)}, u32[]{:S(2)}) %collective-permute-start.15) | collective-permute-done | bytes 344096 | tf_op jit(solution)/shard_map/ppermute | solution.py:351
  93.4 1.1 collective-permute-start.17
  94.5 4.1 %collective-permute-done.17.last_b = bf16[1,192,384]{2,1,0:T(8,128)(2,1)S(1)} collective-permute-done((bf16[1,192,384]{2,1,0:T(8,128)(2,1)S(1)}, bf16[1,192,384]{2,1,0:T(8,128)(2,1)S(1)}, u32[]{:S(2)}, u32[]{:S(2)}) %collective-permute-start.17) | collective-permute-done | bytes 147488 | tf_op jit(solution)/shard_map/ppermute | solution.py:351
  98.7 13.8 %all_to_all.11 = bf16[16,40,384]{2,1,0:T(8,128)(2,1)S(1)} all-to-all(bf16[16,40,384]{2,1,0:T(8,128)(2,1)S(1)} %final.1), channel_id=1, replica_groups={{0,4,16,20,32,36,48,52,64,68,80,84,96,100,112,116},{8,12,24,28,40,44,56..., dimensions={0} | all-to-all | bytes 983040 | tf_op jit(solution)/shard_map/all_to_all | solution.py:542
  113.2 0.8 slice.8
  (44 shorter events, 3.6 us)
Async XLA Ops:
  21.9 11.3 %collective-permute-start.1 = (bf16[16,40,384]{2,1,0:T(8,128)(2,1)S(1)}, bf16[16,40,384]{2,1,0:T(8,128)(2,1)S(1)}, u32[]{:S(2)}, u32[]{:S(2)}) collective-permute-start(bf16[16,40,384]{2,1,0:T(8,128)(2,1)S(1)} %all_to_all.10.refs_2_.own_ref), channel_id=1, source_target_pairs={{0,2},{1,3},{2,0},{3,1},{4,6},{5,7},{6,4},{7,5},{8,10},{9,11},{10,... | collective-permute-start | bytes 1474568 | tf_op jit(solution)/shard_map/ppermute | solution.py:351
  23.0 12.5 %collective-permute-start.3 = (bf16[16,40,384]{2,1,0:T(8,128)(2,1)S(1)}, bf16[16,40,384]{2,1,0:T(8,128)(2,1)S(1)}, u32[]{:S(2)}, u32[]{:S(2)}) collective-permute-start(bf16[16,40,384]{2,1,0:T(8,128)(2,1)S(1)} %all_to_all.10.refs_2_.own_ref), channel_id=1, source_target_pairs={{0,8},{4,12},{8,0},{12,4},{16,24},{20,28},{24,16},{28,20},{32,40},... | collective-permute-start | bytes 1474568 | tf_op jit(solution)/shard_map/ppermute | solution.py:351
  25.9 0.7 copy-start.2
  26.5 0.7 copy-start.3
  31.2 5.3 %collective-permute-start = (bf16[16,40,384]{2,1,0:T(8,128)(2,1)S(1)}, bf16[16,40,384]{2,1,0:T(8,128)(2,1)S(1)}, u32[]{:S(2)}, u32[]{:S(2)}) collective-permute-start(bf16[16,40,384]{2,1,0:T(8,128)(2,1)S(1)} %all_to_all.10.refs_2_.own_ref), channel_id=1, source_target_pairs={{0,1},{1,0},{2,3},{3,2},{4,5},{5,4},{6,7},{7,6},{8,9},{9,8},{10,11... | collective-permute-start | bytes 1474568 | tf_op jit(solution)/shard_map/ppermute | solution.py:351
  33.2 3.3 %collective-permute-start.2 = (bf16[16,40,384]{2,1,0:T(8,128)(2,1)S(1)}, bf16[16,40,384]{2,1,0:T(8,128)(2,1)S(1)}, u32[]{:S(2)}, u32[]{:S(2)}) collective-permute-start(bf16[16,40,384]{2,1,0:T(8,128)(2,1)S(1)} %collective-permute-done.1.refs_4_.far_ref), channel_id=1, source_target_pairs={{0,1},{1,0},{2,3},{3,2},{4,5},{5,4},{6,7},{7,6},{8,9},{9,8},{10,11... | collective-permute-start | bytes 1474568 | tf_op jit(solution)/shard_map/ppermute | solution.py:351
  35.5 11.4 %collective-permute-start.5 = (bf16[16,40,384]{2,1,0:T(8,128)(2,1)S(1)}, bf16[16,40,384]{2,1,0:T(8,128)(2,1)S(1)}, u32[]{:S(2)}, u32[]{:S(2)}) collective-permute-start(bf16[16,40,384]{2,1,0:T(8,128)(2,1)S(1)} %collective-permute-done.3.refs_2_), channel_id=1, source_target_pairs={{0,2},{1,3},{2,0},{3,1},{4,6},{5,7},{6,4},{7,5},{8,10},{9,11},{10,... | collective-permute-start | bytes 1474568 | tf_op jit(solution)/shard_map/ppermute | solution.py:351
  41.6 5.3 %collective-permute-start.4 = (bf16[16,40,384]{2,1,0:T(8,128)(2,1)S(1)}, bf16[16,40,384]{2,1,0:T(8,128)(2,1)S(1)}, u32[]{:S(2)}, u32[]{:S(2)}) collective-permute-start(bf16[16,40,384]{2,1,0:T(8,128)(2,1)S(1)} %collective-permute-done.3.refs_2_), channel_id=1, source_target_pairs={{0,1},{1,0},{2,3},{3,2},{4,5},{5,4},{6,7},{7,6},{8,9},{9,8},{10,11... | collective-permute-start | bytes 1474568 | tf_op jit(solution)/shard_map/ppermute | solution.py:351
  46.9 5.7 %copy-start = (bf16[384,1536]{1,0:T(8,128)(2,1)S(1)}, bf16[384,1536]{1,0:T(8,128)(2,1)}, u32[]{:S(2)}) copy-start(bf16[384,1536]{1,0:T(8,128)(2,1)} %refs_7_.3) | copy-start | bytes 3538948
  46.9 1.9 %collective-permute-start.6 = (bf16[16,40,384]{2,1,0:T(8,128)(2,1)S(1)}, bf16[16,40,384]{2,1,0:T(8,128)(2,1)S(1)}, u32[]{:S(2)}, u32[]{:S(2)}) collective-permute-start(bf16[16,40,384]{2,1,0:T(8,128)(2,1)S(1)} %collective-permute-done.5.refs_4_), channel_id=1, source_target_pairs={{0,1},{1,0},{2,3},{3,2},{4,5},{5,4},{6,7},{7,6},{8,9},{9,8},{10,11... | collective-permute-start | bytes 1474568 | tf_op jit(solution)/shard_map/ppermute | solution.py:351
  48.7 25.0 %slice-start.2 = ((s8[4718592]{0:T(1024)(128)(4,1)}), s8[4194304]{0:T(1024)(128)(4,1)S(1)}, s32[]{:S(2)}) async-start(s8[4718592]{0:T(1024)(128)(4,1)} %bitcast.11), calls=%async_computation.4 | async-start | bytes 8388608
  52.6 6.5 %copy-start.1 = (bf16[384,1536]{1,0:T(8,128)(2,1)S(1)}, bf16[384,1536]{1,0:T(8,128)(2,1)}, u32[]{:S(2)}) copy-start(bf16[384,1536]{1,0:T(8,128)(2,1)} %refs_8_.1) | copy-start | bytes 3538948
  52.6 21.2 %slice-start.3 = ((s8[4718592]{0:T(1024)(128)(4,1)}), s8[524288]{0:T(1024)(128)(4,1)S(1)}, s32[]{:S(2)}) async-start(s8[4718592]{0:T(1024)(128)(4,1)} %bitcast.11), calls=%async_computation.5 | async-start | bytes 1048576
  55.9 1.9 %collective-permute-start.7 = (bf16[2,320,384]{2,1,0:T(8,128)(2,1)S(1)}, bf16[2,320,384]{2,1,0:T(8,128)(2,1)S(1)}, u32[]{:S(2)}, u32[]{:S(2)}) collective-permute-start(bf16[2,320,384]{2,1,0:T(8,128)(2,1)S(1)} %get-tuple-element.56), channel_id=1, source_target_pairs={{0,1},{1,0},{2,3},{3,2},{4,5},{5,4},{6,7},{7,6},{8,9},{9,8},{10,11... | collective-permute-start | bytes 1474568 | tf_op jit(solution)/shard_map/ppermute | solution.py:351
  57.9 15.9 %slice-start = ((s8[4718592]{0:T(1024)(128)(4,1)}), s8[4194304]{0:T(1024)(128)(4,1)S(1)}, s32[]{:S(2)}) async-start(s8[4718592]{0:T(1024)(128)(4,1)} %bitcast.9), calls=%async_computation.2 | async-start | bytes 8388608
  58.0 15.8 %slice-start.1 = ((s8[4718592]{0:T(1024)(128)(4,1)}), s8[524288]{0:T(1024)(128)(4,1)S(1)}, s32[]{:S(2)}) async-start(s8[4718592]{0:T(1024)(128)(4,1)} %bitcast.9), calls=%async_computation.3 | async-start | bytes 1048576
  58.0 13.3 %collective-permute-start.10 = (bf16[2,320,384]{2,1,0:T(8,128)(2,1)S(1)}, bf16[2,320,384]{2,1,0:T(8,128)(2,1)S(1)}, u32[]{:S(2)}, u32[]{:S(2)}) collective-permute-start(bf16[2,320,384]{2,1,0:T(8,128)(2,1)S(1)} %core_sum.3.sum_ref), channel_id=1, source_target_pairs={{0,2},{1,3},{2,0},{3,1},{4,6},{5,7},{6,4},{7,5},{8,10},{9,11},{10,... | collective-permute-start | bytes 1474568 | tf_op jit(solution)/shard_map/ppermute | solution.py:351
  62.7 1.7 %collective-permute-start.9 = (bf16[2,192,384]{2,1,0:T(8,128)(2,1)S(1)}, bf16[2,192,384]{2,1,0:T(8,128)(2,1)S(1)}, u32[]{:S(2)}, u32[]{:S(2)}) collective-permute-start(bf16[2,192,384]{2,1,0:T(8,128)(2,1)S(1)} %get-tuple-element.61), channel_id=1, source_target_pairs={{0,1},{1,0},{2,3},{3,2},{4,5},{5,4},{6,7},{7,6},{8,9},{9,8},{10,11... | collective-permute-start | bytes 884744 | tf_op jit(solution)/shard_map/ppermute | solution.py:351
  71.5 2.2 %collective-permute-start.11 = (bf16[2,320,384]{2,1,0:T(8,128)(2,1)S(1)}, bf16[2,320,384]{2,1,0:T(8,128)(2,1)S(1)}, u32[]{:S(2)}, u32[]{:S(2)}) collective-permute-start(bf16[2,320,384]{2,1,0:T(8,128)(2,1)S(1)} %middle.2.mine.mid_a), channel_id=1, source_target_pairs={{0,1},{1,0},{2,3},{3,2},{4,5},{5,4},{6,7},{7,6},{8,9},{9,8},{10,11... | collective-permute-start | bytes 1474568 | tf_op jit(solution)/shard_map/ppermute | solution.py:351
  71.6 2.1 %collective-permute-start.8 = (bf16[2,128,384]{2,1,0:T(8,128)(2,1)S(1)}, bf16[2,128,384]{2,1,0:T(8,128)(2,1)S(1)}, u32[]{:S(2)}, u32[]{:S(2)}) collective-permute-start(bf16[2,128,384]{2,1,0:T(8,128)(2,1)S(1)} %get-tuple-element.59), channel_id=1, source_target_pairs={{0,1},{1,0},{2,3},{3,2},{4,5},{5,4},{6,7},{7,6},{8,9},{9,8},{10,11... | collective-permute-start | bytes 589832 | tf_op jit(solution)/shard_map/ppermute | solution.py:351
  72.1 9.0 %collective-permute-start.13 = (bf16[2,192,384]{2,1,0:T(8,128)(2,1)S(1)}, bf16[2,192,384]{2,1,0:T(8,128)(2,1)S(1)}, u32[]{:S(2)}, u32[]{:S(2)}) collective-permute-start(bf16[2,192,384]{2,1,0:T(8,128)(2,1)S(1)} %core_sum.4.sum_ref), channel_id=1, source_target_pairs={{0,2},{1,3},{2,0},{3,1},{4,6},{5,7},{6,4},{7,5},{8,10},{9,11},{10,... | collective-permute-start | bytes 884744 | tf_op jit(solution)/shard_map/ppermute | solution.py:351
  79.1 3.8 %collective-permute-start.12 = (bf16[2,320,384]{2,1,0:T(8,128)(2,1)S(1)}, bf16[2,320,384]{2,1,0:T(8,128)(2,1)S(1)}, u32[]{:S(2)}, u32[]{:S(2)}) collective-permute-start(bf16[2,320,384]{2,1,0:T(8,128)(2,1)S(1)} %get-tuple-element.66), channel_id=1, source_target_pairs={{0,1},{1,0},{2,3},{3,2},{4,5},{5,4},{6,7},{7,6},{8,9},{9,8},{10,11... | collective-permute-start | bytes 1474568 | tf_op jit(solution)/shard_map/ppermute | solution.py:351
  81.2 1.7 %collective-permute-start.14 = (bf16[2,192,384]{2,1,0:T(8,128)(2,1)S(1)}, bf16[2,192,384]{2,1,0:T(8,128)(2,1)S(1)}, u32[]{:S(2)}, u32[]{:S(2)}) collective-permute-start(bf16[2,192,384]{2,1,0:T(8,128)(2,1)S(1)} %middle.3.mine.mid_b), channel_id=1, source_target_pairs={{0,1},{1,0},{2,3},{3,2},{4,5},{5,4},{6,7},{7,6},{8,9},{9,8},{10,11... | collective-permute-start | bytes 884744 | tf_op jit(solution)/shard_map/ppermute | solution.py:351
  83.0 10.2 %collective-permute-start.15 = (bf16[448,384]{1,0:T(8,128)(2,1)S(1)}, bf16[448,384]{1,0:T(8,128)(2,1)S(1)}, u32[]{:S(2)}, u32[]{:S(2)}) collective-permute-start(bf16[448,384]{1,0:T(8,128)(2,1)S(1)} %away.1), channel_id=1, source_target_pairs={{0,2},{1,3},{2,0},{3,1},{4,6},{5,7},{6,4},{7,5},{8,10},{9,11},{10,... | collective-permute-start | bytes 1032200 | tf_op jit(solution)/shard_map/ppermute | solution.py:351
  87.5 5.9 %collective-permute-start.16 = (bf16[2,192,384]{2,1,0:T(8,128)(2,1)S(1)}, bf16[2,192,384]{2,1,0:T(8,128)(2,1)S(1)}, u32[]{:S(2)}, u32[]{:S(2)}) collective-permute-start(bf16[2,192,384]{2,1,0:T(8,128)(2,1)S(1)} %get-tuple-element.74), channel_id=1, source_target_pairs={{0,1},{1,0},{2,3},{3,2},{4,5},{5,4},{6,7},{7,6},{8,9},{9,8},{10,11... | collective-permute-start | bytes 884744 | tf_op jit(solution)/shard_map/ppermute | solution.py:351
  93.4 5.2 %collective-permute-start.17 = (bf16[1,192,384]{2,1,0:T(8,128)(2,1)S(1)}, bf16[1,192,384]{2,1,0:T(8,128)(2,1)S(1)}, u32[]{:S(2)}, u32[]{:S(2)}) collective-permute-start(bf16[1,192,384]{2,1,0:T(8,128)(2,1)S(1)} %core_sum.5), channel_id=1, source_target_pairs={{0,2},{1,3},{2,0},{3,1},{4,6},{5,7},{6,4},{7,5},{8,10},{9,11},{10,... | collective-permute-start | bytes 442376 | tf_op jit(solution)/shard_map/ppermute | solution.py:351

commit v5 on v4

--- a/solution.py
+++ b/solution.py
@@ -115,7 +115,7 @@
         acts_ref[rows, :] = (moved * lax.rsqrt(spread + 1e-06) * gain + shift).astype(BF)
         return carry
 
-    lax.fori_loop(0, count // block, body, 0, unroll=4)
+    lax.fori_loop(0, count // block, body, 0, unroll=True)
 
 
 def head_scale(values, group):
@@ -277,11 +277,13 @@
     first = 0
     for i, (rows, row) in enumerate(zip(counts, gate_rows)):
         outs = refs[7 + groups + 2 * i : 9 + groups + 2 * i]
-        project_out(att[first : first + rows], mods[row : row + 1, :], w_refs[i], *outs)
+        keep_ref, send_ref = outs
+        sends = (send_ref.at[0], send_ref.at[1])
+        project_out(att[first : first + rows], mods[row : row + 1, :], w_refs[i], keep_ref, sends)
         first += rows
 
 
-def project_out(left, gate, w_ref, keep_ref, send_ref):
+def project_out(left, gate, w_ref, keep_ref, sends):
     blk = lax.axis_index("blk")
     part = keep_ref.shape[2]
     width = gate.shape[1]
@@ -294,12 +296,12 @@
         @pl.when((blk & 1) == 0)
         def _():
             keep_ref[pair] = low
-            send_ref[pair] = high
+            sends[pair][...] = high
 
         @pl.when((blk & 1) == 1)
         def _():
             keep_ref[pair] = high
-            send_ref[pair] = low
+            sends[pair][...] = low
 
 
 def attend_call(mods, bias, query, state, keys, start, counts, gate_rows, weights):
@@ -317,34 +319,35 @@
     )(mods, bias, query, *state, keys, *weights)
 
 
-def mlp_kernel(mods, mine, near, up_ref, down_ref, keep_ref, send_ref, raw_ref, acts_ref):
+def mlp_kernel(mods, m0, m1, n0, n1, up_ref, down_ref, keep_ref, s0, s1, raw_ref, acts_ref):
     blk = lax.axis_index("blk")
-    rows, part = mine.shape[1:]
+    rows, part = m0.shape
     span = up_ref.shape[1] // 3
     for j in range(4):
-        value = (near if j & 1 else mine)[j >> 1]
+        value = (m0, n0, m1, n1)[j][...]
         raw_ref[:, pl.ds(pl.multiple_of((blk ^ j) * part, part), part)] = value
     norm_rows(raw_ref, acts_ref, 0, rows, mods[3:4, :], mods[4:5, :])
     for i in range(3):
         cols = slice(i * span, i * span + span)
         hidden = dot(acts_ref[...], up_ref[:, cols])
         raw_ref[:, cols] = jax.nn.gelu(hidden, approximate=True).astype(BF)
-    project_out(raw_ref[...], mods[5:6, :], down_ref, keep_ref, send_ref)
+    project_out(raw_ref[...], mods[5:6, :], down_ref, keep_ref, (s0, s1))
 
 
 def mlp_call(mods, mine, near, up, down):
-    rows, part = mine.shape[1:]
-    shape = jax.ShapeDtypeStruct((2, rows, part), BF)
+    rows, part = mine[0].shape
+    kept = jax.ShapeDtypeStruct((2, rows, part), BF)
+    sent = jax.ShapeDtypeStruct((rows, part), BF)
     return pl.pallas_call(
         mlp_kernel,
-        out_shape=[shape, shape],
-        in_specs=[VM] * 5,
-        out_specs=[VM, VM],
+        out_shape=[kept, sent, sent],
+        in_specs=[VM] * 7,
+        out_specs=[VM] * 3,
         scratch_shapes=[pltpu.VMEM((rows, 4 * part), BF)] * 2,
         compiler_params=pltpu.CompilerParams(vmem_limit_bytes=VMEM_LIMIT),
         cost_estimate=COST,
         name="mlp",
-    )(mods, mine, near, up, down)
+    )(mods, *mine, *near, up, down)
 
 
 def swap(values, axis, size, bit):
@@ -387,35 +390,40 @@
     copies[1].wait()
 
 
-def sum_kernel(first, left_ref, right_ref, out_ref):
-    for i in range(first, 2):
-        out_ref[i - first] = add(left_ref[i], right_ref[i])
-
-
-def away_kernel(image_ref, came_i, text_ref, came_t, out_ref):
+def sum_kernel(left_ref, right_ref, out_ref):
+    for i in range(2):
+        out_ref[i] = add(left_ref[i], right_ref[i])
+
+
+def joint_kernel(left_ref, right_ref, text_ref, came_t, image_ref, out_ref):
     rows = image_ref.shape[1]
-    out_ref[:rows, :] = add(image_ref[1], came_i[1])
-    out_ref[rows:, :] = add(text_ref[1], came_t[1])
-
-
-def core_sum(kept, came, first):
-    shape = (2 - first,) + kept.shape[1:]
-    return small_call(functools.partial(sum_kernel, first), "core_sum", [shape], [kept, came])[0]
-
-
-def middle_kernel(begin, own_ref, far_ref, sum_ref, back_ref, out_ref):
-    rows, part = out_ref.shape[1:]
+    text = add(text_ref[1], came_t[1])
+    half = text.shape[0] // 2
+    for i in range(2):
+        value = add(left_ref[i], right_ref[i])
+        image_ref[i] = value
+        out_ref[i, :rows, :] = value
+        out_ref[i, rows:, :] = text[i * half : i * half + half]
+
+
+def middle_kernel(begin, own_ref, far_ref, sum_ref, back_ref, *outs):
+    rows, part = sum_ref.shape[1:]
     image_rows = own_ref.shape[1] - TXT_PAD
-    for i, ref in enumerate((own_ref, far_ref)):
+    for i, (ref, out_ref) in enumerate(zip((own_ref, far_ref), outs)):
         start = ref[begin : begin + rows // image_rows, :image_rows, :].reshape(rows, part)
-        out_ref[i] = add(start, sum_ref[i], back_ref[1 - i])
-
-
-def first_kernel(own_ref, keep_t, came_t, mid_a, keep_a, came_a, last_a, image_ref, text_ref):
-    rows = image_ref.shape[0]
-    image_ref[...] = add(mid_a[0], keep_a[0], came_a[0], last_a[:rows, :])
+        out_ref[...] = add(start, sum_ref[i], back_ref[1 - i, :rows, :])
+
+
+def away_kernel(keep_ref, came_ref, out_ref):
+    out_ref[...] = add(keep_ref[1], came_ref[...])
+
+
+def first_kernel(own_ref, keep_t, came_t, back_b, mid_a, keep_a, came_a, last_a, image_ref, text_ref):
+    image_ref[...] = add(mid_a[...], keep_a[0], came_a[...], last_a[...])
     sources, slots, part = own_ref.shape
-    total = keep_t[0].astype(F32) + came_t[0].astype(F32) + last_a[rows:, :].astype(F32)
+    rows = back_b.shape[1] - keep_t.shape[1] // 2
+    back = jnp.concatenate([back_b[0, rows:, :], back_b[1, rows:, :]], axis=0)
+    total = keep_t[0].astype(F32) + came_t[0].astype(F32) + back.astype(F32)
     text = own_ref[:, slots - TXT_PAD :, :].astype(F32) + total.reshape(sources, TXT_PAD, part)
     text_ref[...] = text.astype(BF)
 
@@ -425,7 +433,7 @@
     image_rows = slots - TXT_PAD
     first = image_ref.shape[0] // image_rows
     out_ref[:first, :image_rows, :] = image_ref[...].reshape(first, image_rows, part)
-    value = add(mid_b[0], keep_b[0], came_b[0], last_b[0])
+    value = add(mid_b[...], keep_b[0], came_b[...], last_b[...])
     out_ref[first:, :image_rows, :] = value.reshape(sources - first, image_rows, part)
     out_ref[:, image_rows:, :] = text_ref[...]
 
@@ -476,7 +484,7 @@
     own = lax.all_to_all(packed, "tile", 0, 0, axis_index_groups=groups, tiled=True)
     far = swap(own, "blk", 4, 2)
     other = swap(own, "tile", tiles, 2)
-    near = swap(own, "blk", 4, 1)
+    own_near = swap(own, "blk", 4, 1)
     mods, head_gains, bias, *wide = prep_call(after(step_index, own), text_length, tables, gains, weights)
 
     def tied(*others):
@@ -489,7 +497,7 @@
     other = after(other, far)
     other_far = swap(other, "blk", 4, 2)
     diag = swap(far, "blk", 4, 1)
-    query, mine = project(mods, [own, near, far, diag], PARTS)
+    query, mine = project(mods, [own, own_near, far, diag], PARTS)
     other_near = swap(after(other, query), "blk", 4, 1)
     state = own_call(bias, query, mine)
     other_far = after(other_far, state[0])
@@ -504,40 +512,47 @@
         return attend_call(mods, bias, query, state, keys, *groups)
 
     def middle(begin, sums, back):
-        args = [own, far, sums, back]
-        return small_call(functools.partial(middle_kernel, begin), "middle", [sums.shape], args)[0]
+        kernel = functools.partial(middle_kernel, begin)
+        return small_call(kernel, "middle", [sums.shape[1:]] * 2, [own, far, sums, back])
+
+    def near(value):
+        return swap(value, "blk", 4, 1)
+
+    def across(value):
+        return swap(value, "blk", 4, 2)
+
+    def away(kept, came):
+        return small_call(away_kernel, "away", [came.shape], [kept, came])[0]
 
     keep_a, send_a = attend(mods, 0, (rows_a,), (2,), (attn_out_image,))
-    came_a = swap(send_a, "blk", 4, 1)
-    sum_a = core_sum(keep_a, came_a, 0)
-    back_a = swap(sum_a, "blk", 4, 2)
+    sum_a = small_call(sum_kernel, "core_sum", [keep_a.shape], [keep_a, near(send_a)])[0]
+    back_a = across(sum_a)
     keep_b, send_b, keep_t, send_t = attend(
         tied(sum_a), rows_a, (rows_b, txt_rows), (2, 10), (attn_out_image, attn_out_text)
     )
-    came_b = swap(send_b, "blk", 4, 1)
-    sum_b = core_sum(keep_b, came_b, 0)
+    came_t = near(send_t)
+    shapes = [keep_b.shape, (2, rows_b + txt_rows // 2, part)]
+    sum_b, joint = small_call(joint_kernel, "joint", shapes, [keep_b, near(send_b), keep_t, came_t])
+    back_b = across(joint)
     mid_a = middle(0, sum_a, after(back_a, sum_b))
-    near_a = swap(mid_a, "blk", 4, 1)
-    back_b = swap(sum_b, "blk", 4, 2)
-    came_t = swap(send_t, "blk", 4, 1)
-    came_t = after(came_t, sum_b)
-    down_a, send_a = mlp_call(tied(came_t), mid_a, near_a, up_weight, down_weight)
-    came_a = swap(send_a, "blk", 4, 1)
+    near_a = [near(value) for value in mid_a]
+
+    down_a, *send_a = mlp_call(mods, mid_a, near_a, up_weight, down_weight)
+    came_a = [near(value) for value in send_a]
     mid_b = middle(first, sum_b, after(back_b, down_a))
-    near_b = swap(mid_b, "blk", 4, 1)
-    args = [after(down_a, near_b), came_a, keep_t, came_t]
-    away_a = small_call(away_kernel, "away", [(rows_a + txt_rows, part)], args)[0]
-    last_a = swap(away_a, "blk", 4, 2)
-    down_b, send_b = mlp_call(tied(away_a), mid_b, near_b, up_weight, down_weight)
-    args = [own, keep_t, came_t, mid_a, down_a, came_a, after(last_a, down_b)]
+    near_b = [near(value) for value in mid_b]
+    away_a = away(after(down_a, *near_b), came_a[1])
+    last_a = across(away_a)
+    down_b, *send_b = mlp_call(tied(away_a), mid_b, near_b, up_weight, down_weight)
+    args = [own, keep_t, came_t, back_b, mid_a[0], down_a, came_a[0], after(last_a, down_b)]
     image_a, text_out = small_call(
         first_kernel, "first", [(rows_a, part), (requests, TXT_PAD, part)], args
     )
-    came_b = swap(send_b, "blk", 4, 1)
-    away_b = core_sum(after(down_b, image_a), came_b, 1)
-    last_b = swap(away_b, "blk", 4, 2)
-
-    args = [image_a, text_out, mid_b, down_b, came_b, last_b]
+    came_b = [near(value) for value in send_b]
+    away_b = away(after(down_b, image_a), came_b[1])
+    last_b = across(away_b)
+
+    args = [image_a, text_out, mid_b[0], down_b, came_b[0], last_b]
     result = small_call(final_kernel, "final", [slots], args)[0]
     result = lax.all_to_all(result, "tile", 0, 0, axis_index_groups=groups, tiled=True)
     return (result[:, :image_rows], result[:, image_rows : image_rows + text_rows])

time: 114 us -> 110 us (0.965)
  Pallas kernels: 34.2 us -> 31.3 us
  waiting for transfers between devices: 31.3 us -> 28.5 us
  starting transfers between devices: 10.8 us -> 12.4 us
    ppermute x18 -> x22, waiting for transfers between devices: 31.3 us -> 28.5 us  [swap(): return lax.ppermute(values, axis, [(i, i ^ bit) for i in range(size)])]
    pallas_call x2, Pallas kernels: 8.95 us -> 7.21 us  [qkv_call(): pl.pallas_call(functools.partial(qkv_kernel, begin, sources, parts), out_...]
    ppermute x18 -> x22, starting transfers between devices: 10.8 us -> 12.4 us  [swap(): return lax.ppermute(values, axis, [(i, i ^ bit) for i in range(size)])]
    pallas_call x2, Pallas kernels: 8.66 us -> 7.49 us  [mlp_call(): pl.pallas_call(mlp_kernel, out_shape=[kept, sent, sent], in_specs=[VM] *...]
  transfers between devices with their start and end apart: 18 -> 22, of which waited for: 12 -> 14; matrix products, arithmetic and copies ran while one was open for 0% -> 0% of each run, Pallas kernels for 22% -> 22%
where the time goes in v5:
time: 110 us
  blocking collectives  34.1 us (31%)
  Pallas kernels  31.3 us (28%)
  waiting for transfers between devices  28.5 us (26%)
  starting transfers between devices  12.4 us (11%)
  local copies, waits for them, and re-layouts  2.77 us (3%)
    ppermute x22, waiting for transfers between devices, swap(): return lax.ppermute(values, axis, [(i, i ^ bit) for i in range(size)])  28.5 us
    all_to_all x1, blocking collectives, per_device(): lax.all_to_all(packed, 'tile', 0, 0, axis_index_groups=groups, tiled=True)  20.3 us
    all_to_all x1, blocking collectives, per_device(): lax.all_to_all(result, 'tile', 0, 0, axis_index_groups=groups, tiled=True)  13.8 us
    ppermute x22, starting transfers between devices, swap(): return lax.ppermute(values, axis, [(i, i ^ bit) for i in range(size)])  12.4 us
    pallas_call x2, Pallas kernels, mlp_call(): pl.pallas_call(mlp_kernel, out_shape=[kept, sent, sent], in_specs=[VM] *...  7.49 us
    pallas_call x2, Pallas kernels, qkv_call(): pl.pallas_call(functools.partial(qkv_kernel, begin, sources, parts), out_...  7.21 us
    pallas_call x2, Pallas kernels, attend_call(): pl.pallas_call(functools.partial(attend_kernel, start, counts, gate_rows)...  6.89 us
    pallas_call x1, Pallas kernels, prep_call(): pl.pallas_call(prep_kernel, out_shape=[jax.ShapeDtypeStruct((16, width),...  4.01 us
  transfers between devices with their start and end apart: 22, of which 14 were waited for; matrix products, arithmetic and copies ran while one was open for 0% of the time, Pallas kernels for 22%

profile of v5, /device:TPU:0, one launch (start us, length us, event | category | flops | bytes accessed | tf_op | source)
XLA Modules:
  0.0 109.9 jit_solution(12642737799858633684)
XLA Ops:
  0.6 1.1 pack.1
  1.7 20.3 %all_to_all.10.refs_2_.own_ref = bf16[16,40,384]{2,1,0:T(8,128)(2,1)S(1)} all-to-all(bf16[16,40,384]{2,1,0:T(8,128)(2,1)S(1)} %pack.1), channel_id=1, replica_groups={{0,4,16,20,32,36,48,52,64,68,80,84,96,100,112,116},{8,12,24,28,40,44,56..., dimensions={0} | all-to-all | bytes 983040 | tf_op jit(solution)/shard_map/all_to_all | solution.py:484
  21.9 1.0 collective-permute-start.1
  23.0 2.9 %collective-permute-start.3 = (bf16[16,40,384]{2,1,0:T(8,128)(2,1)S(1)}, bf16[16,40,384]{2,1,0:T(8,128)(2,1)S(1)}, u32[]{:S(2)}, u32[]{:S(2)}) collective-permute-start(bf16[16,40,384]{2,1,0:T(8,128)(2,1)S(1)} %all_to_all.10.refs_2_.own_ref), channel_id=1, source_target_pairs={{0,8},{4,12},{8,0},{12,4},{16,24},{20,28},{24,16},{28,20},{32,40},... | collective-permute-start | bytes 1474568 | tf_op jit(solution)/shard_map/ppermute | solution.py:354
  25.9 0.7 copy-done.2
  26.5 0.7 copy-done.3
  27.2 4.0 %prep.1 = (f32[16,1536]{1,0:T(8,128)S(1)}, f32[8,128]{1,0:T(8,128)S(1)}, bf16[2,128,128]{2,1,0:T(8,128)(2,1)S(1)}, bf16[1536,1152]{1,0:T(8,128)(2,1)S(1)}, bf16[1536,1152]{1,0:T(8,128)(2,1)S(1)}) custom-call(s32[16]{0:T(128)S(1)} %copy-done.2, s32[16]{0:T(128)S(1)} %copy-done.3, bf16[6,28,1536]{2,1,0:T(8,128)(2,1)} %bitcast.15, ...), custom_call_target="tpu_custom_call" | custom-call | flops 1 | bytes 1 | tf_op jit(solution)/shard_map/prep/pallas_call | solution.py:86
  31.3 1.9 %collective-permute-done.1.refs_4_.far_ref = bf16[16,40,384]{2,1,0:T(8,128)(2,1)S(1)} collective-permute-done((bf16[16,40,384]{2,1,0:T(8,128)(2,1)S(1)}, bf16[16,40,384]{2,1,0:T(8,128)(2,1)S(1)}, u32[]{:S(2)}, u32[]{:S(2)}) %collective-permute-start.1) | collective-permute-done | bytes 491552 | tf_op jit(solution)/shard_map/ppermute | solution.py:354
  33.2 2.2 %collective-permute-done.3.refs_2_ = bf16[16,40,384]{2,1,0:T(8,128)(2,1)S(1)} collective-permute-done((bf16[16,40,384]{2,1,0:T(8,128)(2,1)S(1)}, bf16[16,40,384]{2,1,0:T(8,128)(2,1)S(1)}, u32[]{:S(2)}, u32[]{:S(2)}) %collective-permute-start.3) | collective-permute-done | bytes 491552 | tf_op jit(solution)/shard_map/ppermute | solution.py:354
  35.5 1.0 collective-permute-start.5
  36.5 4.3 %qkv.2 = (bf16[640,384]{1,0:T(8,128)(2,1)S(1)}, bf16[2,640,384]{2,1,0:T(8,128)(2,1)S(1)}) custom-call(f32[16,1536]{1,0:T(8,128)S(1)} %get-tuple-element.80.refs_0_.mods, f32[8,128]{1,0:T(8,128)S(1)} %get-tuple-element.48.refs_1_, bf16[16,40,384]{2,1,0:T(8,128)(2,1)S(1)} %all_to_all.10.refs_2_.own_ref, bf16[16,40,384]{2,1,0:T(8,128)(2,1)S(1)} %collective-permute-done.refs_3_, ...), custom_call_target="tpu_custom_call" | custom-call | flops 1 | bytes 1 | tf_op jit(solution)/shard_map/qkv/pallas_call | solution.py:176
  40.8 3.7 %attend_own.1 = (f32[640,384]{1,0:T(8,128)S(1)}, f32[640,384]{1,0:T(8,128)S(1)}, f32[640,384]{1,0:T(8,128)S(1)}) custom-call(bf16[2,128,128]{2,1,0:T(8,128)(2,1)S(1)} %get-tuple-element.47.bias_ref.refs_1_, bf16[640,384]{1,0:T(8,128)(2,1)S(1)} %get-tuple-element.52.q_ref.refs_2_, bf16[2,640,384]{2,1,0:T(8,128)(2,1)S(1)} %get-tuple-element.53.kv_ref), custom_call_target="tpu_custom_call" | custom-call | flops 1 | bytes 1 | tf_op jit(solution)/shard_map/attend_own/pallas_call | solution.py:240
  44.6 2.3 %collective-permute-done.5.refs_4_ = bf16[16,40,384]{2,1,0:T(8,128)(2,1)S(1)} collective-permute-done((bf16[16,40,384]{2,1,0:T(8,128)(2,1)S(1)}, bf16[16,40,384]{2,1,0:T(8,128)(2,1)S(1)}, u32[]{:S(2)}, u32[]{:S(2)}) %collective-permute-start.5) | collective-permute-done | bytes 491552 | tf_op jit(solution)/shard_map/ppermute | solution.py:354
  46.9 1.9 %collective-permute-done.6.refs_5_ = bf16[16,40,384]{2,1,0:T(8,128)(2,1)S(1)} collective-permute-done((bf16[16,40,384]{2,1,0:T(8,128)(2,1)S(1)}, bf16[16,40,384]{2,1,0:T(8,128)(2,1)S(1)}, u32[]{:S(2)}, u32[]{:S(2)}) %collective-permute-start.6) | collective-permute-done | bytes 491552 | tf_op jit(solution)/shard_map/ppermute | solution.py:354
  48.7 3.0 %qkv.3.refs_6_ = bf16[2,640,384]{2,1,0:T(8,128)(2,1)S(1)} custom-call(f32[16,1536]{1,0:T(8,128)S(1)} %get-tuple-element.80.refs_0_.mods, f32[8,128]{1,0:T(8,128)S(1)} %get-tuple-element.48.refs_1_, bf16[16,40,384]{2,1,0:T(8,128)(2,1)S(1)} %collective-permute-done.3.refs_2_, bf16[16,40,384]{2,1,0:T(8,128)(2,1)S(1)} %collective-permute-done.4.refs_3_, ...), custom_call_target="tpu_custom_call" | custom-call | flops 1 | bytes 1 | tf_op jit(solution)/shard_map/qkv/pallas_call | solution.py:176
  51.7 3.3 %attend.2 = (bf16[2,320,384]{2,1,0:T(8,128)(2,1)S(1)}, bf16[2,320,384]{2,1,0:T(8,128)(2,1)S(1)}) custom-call(f32[16,1536]{1,0:T(8,128)S(1)} %get-tuple-element.80.refs_0_.mods, bf16[2,128,128]{2,1,0:T(8,128)(2,1)S(1)} %get-tuple-element.47.bias_ref.refs_1_, bf16[640,384]{1,0:T(8,128)(2,1)S(1)} %get-tuple-element.52.q_ref.refs_2_, ...), custom_call_target="tpu_custom_call" | custom-call | flops 1 | bytes 1 | tf_op jit(solution)/shard_map/attend/pallas_call | solution.py:311
  55.2 1.7 %collective-permute-done.7.right_ref = bf16[2,320,384]{2,1,0:T(8,128)(2,1)S(1)} collective-permute-done((bf16[2,320,384]{2,1,0:T(8,128)(2,1)S(1)}, bf16[2,320,384]{2,1,0:T(8,128)(2,1)S(1)}, u32[]{:S(2)}, u32[]{:S(2)}) %collective-permute-start.7) | collective-permute-done | bytes 491552 | tf_op jit(solution)/shard_map/ppermute | solution.py:354
  57.1 1.1 %collective-permute-start.11 = (bf16[2,320,384]{2,1,0:T(8,128)(2,1)S(1)}, bf16[2,320,384]{2,1,0:T(8,128)(2,1)S(1)}, u32[]{:S(2)}, u32[]{:S(2)}) collective-permute-start(bf16[2,320,384]{2,1,0:T(8,128)(2,1)S(1)} %core_sum.1.sum_ref), channel_id=1, source_target_pairs={{0,2},{1,3},{2,0},{3,1},{4,6},{5,7},{6,4},{7,5},{8,10},{9,11},{10,... | collective-permute-start | bytes 1474568 | tf_op jit(solution)/shard_map/ppermute | solution.py:354
  58.2 3.6 %attend.3 = (bf16[2,192,384]{2,1,0:T(8,128)(2,1)S(1)}, bf16[2,192,384]{2,1,0:T(8,128)(2,1)S(1)}, bf16[2,128,384]{2,1,0:T(8,128)(2,1)S(1)}, bf16[2,128,384]{2,1,0:T(8,128)(2,1)S(1)}) custom-call(f32[16,1536]{1,0:T(8,128)S(1)} %get-tuple-element.80.refs_0_.mods, bf16[2,128,128]{2,1,0:T(8,128)(2,1)S(1)} %get-tuple-element.47.bias_ref.refs_1_, ...), custom_call_target="tpu_custom_call" | custom-call | flops 1 | bytes 1 | tf_op jit(solution)/shard_map/attend/pallas_call | solution.py:311
  62.4 1.4 %collective-permute-done.8.came_t = bf16[2,128,384]{2,1,0:T(8,128)(2,1)S(1)} collective-permute-done((bf16[2,128,384]{2,1,0:T(8,128)(2,1)S(1)}, bf16[2,128,384]{2,1,0:T(8,128)(2,1)S(1)}, u32[]{:S(2)}, u32[]{:S(2)}) %collective-permute-start.8) | collective-permute-done | bytes 196640 | tf_op jit(solution)/shard_map/ppermute | solution.py:354
  63.9 1.1 collective-permute-start.10
  65.0 6.3 %collective-permute-done.11.back_ref = bf16[2,320,384]{2,1,0:T(8,128)(2,1)S(1)} collective-permute-done((bf16[2,320,384]{2,1,0:T(8,128)(2,1)S(1)}, bf16[2,320,384]{2,1,0:T(8,128)(2,1)S(1)}, u32[]{:S(2)}, u32[]{:S(2)}) %collective-permute-start.11) | collective-permute-done | bytes 491552 | tf_op jit(solution)/shard_map/ppermute | solution.py:354
  72.0 1.0 collective-permute-done.13.n1
  73.4 4.6 %mlp.2 = (bf16[2,320,384]{2,1,0:T(8,128)(2,1)S(1)}, bf16[320,384]{1,0:T(8,128)(2,1)S(1)}, bf16[320,384]{1,0:T(8,128)(2,1)S(1)}) custom-call(f32[16,1536]{1,0:T(8,128)S(1)} %get-tuple-element.80.refs_0_.mods, bf16[320,384]{1,0:T(8,128)(2,1)S(1)} %get-tuple-element.71.m0.mid_a, bf16[320,384]{1,0:T(8,128)(2,1)S(1)} %get-tuple-element.72.m1, ...), custom_call_target="tpu_custom_call" | custom-call | flops 1 | bytes 1 | tf_op jit(solution)/shard_map/mlp/pallas_call | solution.py:341
  79.6 0.9 collective-permute-done.16.n1
  80.7 1.1 %collective-permute-start.18 = (bf16[320,384]{1,0:T(8,128)(2,1)S(1)}, bf16[320,384]{1,0:T(8,128)(2,1)S(1)}, u32[]{:S(2)}, u32[]{:S(2)}) collective-permute-start(bf16[320,384]{1,0:T(8,128)(2,1)S(1)} %away.2), channel_id=1, source_target_pairs={{0,2},{1,3},{2,0},{3,1},{4,6},{5,7},{6,4},{7,5},{8,10},{9,11},{10,... | collective-permute-start | bytes 737288 | tf_op jit(solution)/shard_map/ppermute | solution.py:354
  81.9 2.9 %mlp.3 = (bf16[2,192,384]{2,1,0:T(8,128)(2,1)S(1)}, bf16[192,384]{1,0:T(8,128)(2,1)S(1)}, bf16[192,384]{1,0:T(8,128)(2,1)S(1)}) custom-call(f32[16,1536]{1,0:T(8,128)S(1)} %get-tuple-element.80.refs_0_.mods, bf16[192,384]{1,0:T(8,128)(2,1)S(1)} %get-tuple-element.76.m0.mid_b, bf16[192,384]{1,0:T(8,128)(2,1)S(1)} %get-tuple-element.77.m1, ...), custom_call_target="tpu_custom_call" | custom-call | flops 1 | bytes 1 | tf_op jit(solution)/shard_map/mlp/pallas_call | solution.py:341
  85.4 3.6 %collective-permute-done.18.last_a = bf16[320,384]{1,0:T(8,128)(2,1)S(1)} collective-permute-done((bf16[320,384]{1,0:T(8,128)(2,1)S(1)}, bf16[320,384]{1,0:T(8,128)(2,1)S(1)}, u32[]{:S(2)}, u32[]{:S(2)}) %collective-permute-start.18) | collective-permute-done | bytes 245792 | tf_op jit(solution)/shard_map/ppermute | solution.py:354
  89.2 1.1 %collective-permute-start.21 = (bf16[192,384]{1,0:T(8,128)(2,1)S(1)}, bf16[192,384]{1,0:T(8,128)(2,1)S(1)}, u32[]{:S(2)}, u32[]{:S(2)}) collective-permute-start(bf16[192,384]{1,0:T(8,128)(2,1)S(1)} %away.3), channel_id=1, source_target_pairs={{0,2},{1,3},{2,0},{3,1},{4,6},{5,7},{6,4},{7,5},{8,10},{9,11},{10,... | collective-permute-start | bytes 442376 | tf_op jit(solution)/shard_map/ppermute | solution.py:354
  90.3 4.2 %collective-permute-done.21.last_b = bf16[192,384]{1,0:T(8,128)(2,1)S(1)} collective-permute-done((bf16[192,384]{1,0:T(8,128)(2,1)S(1)}, bf16[192,384]{1,0:T(8,128)(2,1)S(1)}, u32[]{:S(2)}, u32[]{:S(2)}) %collective-permute-start.21) | collective-permute-done | bytes 147488 | tf_op jit(solution)/shard_map/ppermute | solution.py:354
  94.6 13.8 %all_to_all.11 = bf16[16,40,384]{2,1,0:T(8,128)(2,1)S(1)} all-to-all(bf16[16,40,384]{2,1,0:T(8,128)(2,1)S(1)} %final.1), channel_id=1, replica_groups={{0,4,16,20,32,36,48,52,64,68,80,84,96,100,112,116},{8,12,24,28,40,44,56..., dimensions={0} | all-to-all | bytes 983040 | tf_op jit(solution)/shard_map/all_to_all | solution.py:557
  109.1 0.8 slice.8
  (52 shorter events, 5.8 us)
Async XLA Ops:
  21.9 11.3 %collective-permute-start.1 = (bf16[16,40,384]{2,1,0:T(8,128)(2,1)S(1)}, bf16[16,40,384]{2,1,0:T(8,128)(2,1)S(1)}, u32[]{:S(2)}, u32[]{:S(2)}) collective-permute-start(bf16[16,40,384]{2,1,0:T(8,128)(2,1)S(1)} %all_to_all.10.refs_2_.own_ref), channel_id=1, source_target_pairs={{0,2},{1,3},{2,0},{3,1},{4,6},{5,7},{6,4},{7,5},{8,10},{9,11},{10,... | collective-permute-start | bytes 1474568 | tf_op jit(solution)/shard_map/ppermute | solution.py:354
  23.0 12.5 %collective-permute-start.3 = (bf16[16,40,384]{2,1,0:T(8,128)(2,1)S(1)}, bf16[16,40,384]{2,1,0:T(8,128)(2,1)S(1)}, u32[]{:S(2)}, u32[]{:S(2)}) collective-permute-start(bf16[16,40,384]{2,1,0:T(8,128)(2,1)S(1)} %all_to_all.10.refs_2_.own_ref), channel_id=1, source_target_pairs={{0,8},{4,12},{8,0},{12,4},{16,24},{20,28},{24,16},{28,20},{32,40},... | collective-permute-start | bytes 1474568 | tf_op jit(solution)/shard_map/ppermute | solution.py:354
  25.9 0.7 copy-start.2
  26.5 0.7 copy-start.3
  31.2 5.3 %collective-permute-start = (bf16[16,40,384]{2,1,0:T(8,128)(2,1)S(1)}, bf16[16,40,384]{2,1,0:T(8,128)(2,1)S(1)}, u32[]{:S(2)}, u32[]{:S(2)}) collective-permute-start(bf16[16,40,384]{2,1,0:T(8,128)(2,1)S(1)} %all_to_all.10.refs_2_.own_ref), channel_id=1, source_target_pairs={{0,1},{1,0},{2,3},{3,2},{4,5},{5,4},{6,7},{7,6},{8,9},{9,8},{10,11... | collective-permute-start | bytes 1474568 | tf_op jit(solution)/shard_map/ppermute | solution.py:354
  33.2 3.3 %collective-permute-start.2 = (bf16[16,40,384]{2,1,0:T(8,128)(2,1)S(1)}, bf16[16,40,384]{2,1,0:T(8,128)(2,1)S(1)}, u32[]{:S(2)}, u32[]{:S(2)}) collective-permute-start(bf16[16,40,384]{2,1,0:T(8,128)(2,1)S(1)} %collective-permute-done.1.refs_4_.far_ref), channel_id=1, source_target_pairs={{0,1},{1,0},{2,3},{3,2},{4,5},{5,4},{6,7},{7,6},{8,9},{9,8},{10,11... | collective-permute-start | bytes 1474568 | tf_op jit(solution)/shard_map/ppermute | solution.py:354
  35.5 11.4 %collective-permute-start.5 = (bf16[16,40,384]{2,1,0:T(8,128)(2,1)S(1)}, bf16[16,40,384]{2,1,0:T(8,128)(2,1)S(1)}, u32[]{:S(2)}, u32[]{:S(2)}) collective-permute-start(bf16[16,40,384]{2,1,0:T(8,128)(2,1)S(1)} %collective-permute-done.3.refs_2_), channel_id=1, source_target_pairs={{0,2},{1,3},{2,0},{3,1},{4,6},{5,7},{6,4},{7,5},{8,10},{9,11},{10,... | collective-permute-start | bytes 1474568 | tf_op jit(solution)/shard_map/ppermute | solution.py:354
  40.7 6.1 %collective-permute-start.4 = (bf16[16,40,384]{2,1,0:T(8,128)(2,1)S(1)}, bf16[16,40,384]{2,1,0:T(8,128)(2,1)S(1)}, u32[]{:S(2)}, u32[]{:S(2)}) collective-permute-start(bf16[16,40,384]{2,1,0:T(8,128)(2,1)S(1)} %collective-permute-done.3.refs_2_), channel_id=1, source_target_pairs={{0,1},{1,0},{2,3},{3,2},{4,5},{5,4},{6,7},{7,6},{8,9},{9,8},{10,11... | collective-permute-start | bytes 1474568 | tf_op jit(solution)/shard_map/ppermute | solution.py:354
  46.9 4.8 %copy-start = (bf16[384,1536]{1,0:T(8,128)(2,1)S(1)}, bf16[384,1536]{1,0:T(8,128)(2,1)}, u32[]{:S(2)}) copy-start(bf16[384,1536]{1,0:T(8,128)(2,1)} %refs_7_.3) | copy-start | bytes 3538948
  46.9 1.9 %collective-permute-start.6 = (bf16[16,40,384]{2,1,0:T(8,128)(2,1)S(1)}, bf16[16,40,384]{2,1,0:T(8,128)(2,1)S(1)}, u32[]{:S(2)}, u32[]{:S(2)}) collective-permute-start(bf16[16,40,384]{2,1,0:T(8,128)(2,1)S(1)} %collective-permute-done.5.refs_4_), channel_id=1, source_target_pairs={{0,1},{1,0},{2,3},{3,2},{4,5},{5,4},{6,7},{7,6},{8,9},{9,8},{10,11... | collective-permute-start | bytes 1474568 | tf_op jit(solution)/shard_map/ppermute | solution.py:354
  48.7 24.7 %slice-start.2 = ((s8[4718592]{0:T(1024)(128)(4,1)}), s8[4194304]{0:T(1024)(128)(4,1)S(1)}, s32[]{:S(2)}) async-start(s8[4718592]{0:T(1024)(128)(4,1)} %bitcast.11), calls=%async_computation.4 | async-start | bytes 8388608
  51.7 6.5 %copy-start.1 = (bf16[384,1536]{1,0:T(8,128)(2,1)S(1)}, bf16[384,1536]{1,0:T(8,128)(2,1)}, u32[]{:S(2)}) copy-start(bf16[384,1536]{1,0:T(8,128)(2,1)} %refs_8_.1) | copy-start | bytes 3538948
  51.7 21.7 %slice-start.3 = ((s8[4718592]{0:T(1024)(128)(4,1)}), s8[524288]{0:T(1024)(128)(4,1)S(1)}, s32[]{:S(2)}) async-start(s8[4718592]{0:T(1024)(128)(4,1)} %bitcast.11), calls=%async_computation.5 | async-start | bytes 1048576
  55.0 1.9 %collective-permute-start.7 = (bf16[2,320,384]{2,1,0:T(8,128)(2,1)S(1)}, bf16[2,320,384]{2,1,0:T(8,128)(2,1)S(1)}, u32[]{:S(2)}, u32[]{:S(2)}) collective-permute-start(bf16[2,320,384]{2,1,0:T(8,128)(2,1)S(1)} %get-tuple-element.62), channel_id=1, source_target_pairs={{0,1},{1,0},{2,3},{3,2},{4,5},{5,4},{6,7},{7,6},{8,9},{9,8},{10,11... | collective-permute-start | bytes 1474568 | tf_op jit(solution)/shard_map/ppermute | solution.py:354
  57.0 16.4 %slice-start = ((s8[4718592]{0:T(1024)(128)(4,1)}), s8[4194304]{0:T(1024)(128)(4,1)S(1)}, s32[]{:S(2)}) async-start(s8[4718592]{0:T(1024)(128)(4,1)} %bitcast.9), calls=%async_computation.2 | async-start | bytes 8388608
  57.1 16.3 %slice-start.1 = ((s8[4718592]{0:T(1024)(128)(4,1)}), s8[524288]{0:T(1024)(128)(4,1)S(1)}, s32[]{:S(2)}) async-start(s8[4718592]{0:T(1024)(128)(4,1)} %bitcast.9), calls=%async_computation.3 | async-start | bytes 1048576
  57.1 14.1 %collective-permute-start.11 = (bf16[2,320,384]{2,1,0:T(8,128)(2,1)S(1)}, bf16[2,320,384]{2,1,0:T(8,128)(2,1)S(1)}, u32[]{:S(2)}, u32[]{:S(2)}) collective-permute-start(bf16[2,320,384]{2,1,0:T(8,128)(2,1)S(1)} %core_sum.1.sum_ref), channel_id=1, source_target_pairs={{0,2},{1,3},{2,0},{3,1},{4,6},{5,7},{6,4},{7,5},{8,10},{9,11},{10,... | collective-permute-start | bytes 1474568 | tf_op jit(solution)/shard_map/ppermute | solution.py:354
  61.8 1.9 %collective-permute-start.9 = (bf16[2,192,384]{2,1,0:T(8,128)(2,1)S(1)}, bf16[2,192,384]{2,1,0:T(8,128)(2,1)S(1)}, u32[]{:S(2)}, u32[]{:S(2)}) collective-permute-start(bf16[2,192,384]{2,1,0:T(8,128)(2,1)S(1)} %get-tuple-element.67), channel_id=1, source_target_pairs={{0,1},{1,0},{2,3},{3,2},{4,5},{5,4},{6,7},{7,6},{8,9},{9,8},{10,11... | collective-permute-start | bytes 884744 | tf_op jit(solution)/shard_map/ppermute | solution.py:354
  61.9 1.9 %collective-permute-start.8 = (bf16[2,128,384]{2,1,0:T(8,128)(2,1)S(1)}, bf16[2,128,384]{2,1,0:T(8,128)(2,1)S(1)}, u32[]{:S(2)}, u32[]{:S(2)}) collective-permute-start(bf16[2,128,384]{2,1,0:T(8,128)(2,1)S(1)} %get-tuple-element.65), channel_id=1, source_target_pairs={{0,1},{1,0},{2,3},{3,2},{4,5},{5,4},{6,7},{7,6},{8,9},{9,8},{10,11... | collective-permute-start | bytes 589832 | tf_op jit(solution)/shard_map/ppermute | solution.py:354
  63.9 15.0 %collective-permute-start.10 = (bf16[2,256,384]{2,1,0:T(8,128)(2,1)S(1)}, bf16[2,256,384]{2,1,0:T(8,128)(2,1)S(1)}, u32[]{:S(2)}, u32[]{:S(2)}) collective-permute-start(bf16[2,256,384]{2,1,0:T(8,128)(2,1)S(1)} %get-tuple-element.68), channel_id=1, source_target_pairs={{0,2},{1,3},{2,0},{3,1},{4,6},{5,7},{6,4},{7,5},{8,10},{9,11},{10,... | collective-permute-start | bytes 1179656 | tf_op jit(solution)/shard_map/ppermute | solution.py:354
  71.5 1.6 %collective-permute-start.13 = (bf16[320,384]{1,0:T(8,128)(2,1)S(1)}, bf16[320,384]{1,0:T(8,128)(2,1)S(1)}, u32[]{:S(2)}, u32[]{:S(2)}) collective-permute-start(bf16[320,384]{1,0:T(8,128)(2,1)S(1)} %get-tuple-element.72.m1), channel_id=1, source_target_pairs={{0,1},{1,0},{2,3},{3,2},{4,5},{5,4},{6,7},{7,6},{8,9},{9,8},{10,11... | collective-permute-start | bytes 737288 | tf_op jit(solution)/shard_map/ppermute | solution.py:354
  71.5 1.9 %collective-permute-start.12 = (bf16[320,384]{1,0:T(8,128)(2,1)S(1)}, bf16[320,384]{1,0:T(8,128)(2,1)S(1)}, u32[]{:S(2)}, u32[]{:S(2)}) collective-permute-start(bf16[320,384]{1,0:T(8,128)(2,1)S(1)} %get-tuple-element.71.m0.mid_a), channel_id=1, source_target_pairs={{0,1},{1,0},{2,3},{3,2},{4,5},{5,4},{6,7},{7,6},{8,9},{9,8},{10,11... | collective-permute-start | bytes 737288 | tf_op jit(solution)/shard_map/ppermute | solution.py:354
  78.1 2.6 %collective-permute-start.17 = (bf16[320,384]{1,0:T(8,128)(2,1)S(1)}, bf16[320,384]{1,0:T(8,128)(2,1)S(1)}, u32[]{:S(2)}, u32[]{:S(2)}) collective-permute-start(bf16[320,384]{1,0:T(8,128)(2,1)S(1)} %get-tuple-element.79), channel_id=1, source_target_pairs={{0,1},{1,0},{2,3},{3,2},{4,5},{5,4},{6,7},{7,6},{8,9},{9,8},{10,11... | collective-permute-start | bytes 737288 | tf_op jit(solution)/shard_map/ppermute | solution.py:354
  79.0 1.5 %collective-permute-start.16 = (bf16[192,384]{1,0:T(8,128)(2,1)S(1)}, bf16[192,384]{1,0:T(8,128)(2,1)S(1)}, u32[]{:S(2)}, u32[]{:S(2)}) collective-permute-start(bf16[192,384]{1,0:T(8,128)(2,1)S(1)} %get-tuple-element.77.m1), channel_id=1, source_target_pairs={{0,1},{1,0},{2,3},{3,2},{4,5},{5,4},{6,7},{7,6},{8,9},{9,8},{10,11... | collective-permute-start | bytes 442376 | tf_op jit(solution)/shard_map/ppermute | solution.py:354
  79.1 1.6 %collective-permute-start.15 = (bf16[192,384]{1,0:T(8,128)(2,1)S(1)}, bf16[192,384]{1,0:T(8,128)(2,1)S(1)}, u32[]{:S(2)}, u32[]{:S(2)}) collective-permute-start(bf16[192,384]{1,0:T(8,128)(2,1)S(1)} %get-tuple-element.76.m0.mid_b), channel_id=1, source_target_pairs={{0,1},{1,0},{2,3},{3,2},{4,5},{5,4},{6,7},{7,6},{8,9},{9,8},{10,11... | collective-permute-start | bytes 442376 | tf_op jit(solution)/shard_map/ppermute | solution.py:354
  80.7 8.2 %collective-permute-start.18 = (bf16[320,384]{1,0:T(8,128)(2,1)S(1)}, bf16[320,384]{1,0:T(8,128)(2,1)S(1)}, u32[]{:S(2)}, u32[]{:S(2)}) collective-permute-start(bf16[320,384]{1,0:T(8,128)(2,1)S(1)} %away.2), channel_id=1, source_target_pairs={{0,2},{1,3},{2,0},{3,1},{4,6},{5,7},{6,4},{7,5},{8,10},{9,11},{10,... | collective-permute-start | bytes 737288 | tf_op jit(solution)/shard_map/ppermute | solution.py:354
  81.9 7.1 %collective-permute-start.14 = (bf16[320,384]{1,0:T(8,128)(2,1)S(1)}, bf16[320,384]{1,0:T(8,128)(2,1)S(1)}, u32[]{:S(2)}, u32[]{:S(2)}) collective-permute-start(bf16[320,384]{1,0:T(8,128)(2,1)S(1)} %get-tuple-element.74), channel_id=1, source_target_pairs={{0,1},{1,0},{2,3},{3,2},{4,5},{5,4},{6,7},{7,6},{8,9},{9,8},{10,11... | collective-permute-start | bytes 737288 | tf_op jit(solution)/shard_map/ppermute | solution.py:354
  84.7 4.4 %collective-permute-start.20 = (bf16[192,384]{1,0:T(8,128)(2,1)S(1)}, bf16[192,384]{1,0:T(8,128)(2,1)S(1)}, u32[]{:S(2)}, u32[]{:S(2)}) collective-permute-start(bf16[192,384]{1,0:T(8,128)(2,1)S(1)} %get-tuple-element.87), channel_id=1, source_target_pairs={{0,1},{1,0},{2,3},{3,2},{4,5},{5,4},{6,7},{7,6},{8,9},{9,8},{10,11... | collective-permute-start | bytes 442376 | tf_op jit(solution)/shard_map/ppermute | solution.py:354
  85.3 5.0 %collective-permute-start.19 = (bf16[192,384]{1,0:T(8,128)(2,1)S(1)}, bf16[192,384]{1,0:T(8,128)(2,1)S(1)}, u32[]{:S(2)}, u32[]{:S(2)}) collective-permute-start(bf16[192,384]{1,0:T(8,128)(2,1)S(1)} %get-tuple-element.85), channel_id=1, source_target_pairs={{0,1},{1,0},{2,3},{3,2},{4,5},{5,4},{6,7},{7,6},{8,9},{9,8},{10,11... | collective-permute-start | bytes 442376 | tf_op jit(solution)/shard_map/ppermute | solution.py:354
  89.2 5.3 %collective-permute-start.21 = (bf16[192,384]{1,0:T(8,128)(2,1)S(1)}, bf16[192,384]{1,0:T(8,128)(2,1)S(1)}, u32[]{:S(2)}, u32[]{:S(2)}) collective-permute-start(bf16[192,384]{1,0:T(8,128)(2,1)S(1)} %away.3), channel_id=1, source_target_pairs={{0,2},{1,3},{2,0},{3,1},{4,6},{5,7},{6,4},{7,5},{8,10},{9,11},{10,... | collective-permute-start | bytes 442376 | tf_op jit(solution)/shard_map/ppermute | solution.py:354

commit v6 on v5

--- a/solution.py
+++ b/solution.py
@@ -385,7 +385,7 @@
         for i in range(part // 128):
             slots_ref[i, pl.ds(slot, requests, stride=TXT_PAD), :] = value[:, i * 128 : i * 128 + 128]
     for i in range(part // 128):
-        piece = slots_ref[i].reshape(requests, TXT_PAD, 128).astype(BF)
+        piece = slots_ref[i, : requests * TXT_PAD, :].reshape(requests, TXT_PAD, 128).astype(BF)
         out_ref[:, image_rows:, i * 128 : i * 128 + 128] = piece
     copies[1].wait()
 
@@ -416,6 +416,23 @@
 
 def away_kernel(keep_ref, came_ref, out_ref):
     out_ref[...] = add(keep_ref[1], came_ref[...])
+
+
+def unpack_kernel(rows_ref, image_ref, text_ref, slots_ref, order_ref, sems):
+    sources, slots, part = rows_ref.shape
+    image_rows = slots - TXT_PAD
+    image_copy = pltpu.make_async_copy(rows_ref.at[:, :image_rows, :], image_ref, sems.at[0])
+    image_copy.start()
+    for i in range(part // 128):
+        cols = slice(i * 128, i * 128 + 128)
+        value = rows_ref[:, image_rows:, cols].astype(F32)
+        slots_ref[i, : sources * TXT_PAD, :] = value.reshape(sources * TXT_PAD, 128)
+        for slot in range(order_ref.shape[0]):
+            order_ref[slot, :, cols] = slots_ref[i, pl.ds(slot, sources, stride=TXT_PAD), :].astype(BF)
+    text_copy = pltpu.make_async_copy(order_ref, text_ref, sems.at[1])
+    text_copy.start()
+    image_copy.wait()
+    text_copy.wait()
 
 
 def first_kernel(own_ref, keep_t, came_t, back_b, mid_a, keep_a, came_a, last_a, image_ref, text_ref):
@@ -475,7 +492,7 @@
         [slots],
         pinned(image_tokens, text_slots),
         [
-            pltpu.VMEM((part // 128, requests * TXT_PAD, 128), F32),
+            pltpu.VMEM((part // 128, (requests + 1) * TXT_PAD, 128), F32),
             pltpu.VMEM(text_slots.shape, BF),
             pltpu.SemaphoreType.DMA((2,)),
         ],
@@ -555,7 +572,22 @@
     args = [image_a, text_out, mid_b[0], down_b, came_b[0], last_b]
     result = small_call(final_kernel, "final", [slots], args)[0]
     result = lax.all_to_all(result, "tile", 0, 0, axis_index_groups=groups, tiled=True)
-    return (result[:, :image_rows], result[:, image_rows : image_rows + text_rows])
+    shapes = [image_tokens.shape, text_slots.shape]
+    image_out, text_out = pl.pallas_call(
+        unpack_kernel,
+        out_shape=[jax.ShapeDtypeStruct(shape, BF) for shape in shapes],
+        in_specs=[VM],
+        out_specs=[HB] * 2,
+        scratch_shapes=[
+            pltpu.VMEM((part // 128, (requests + 1) * TXT_PAD, 128), F32),
+            pltpu.VMEM(text_slots.shape, BF),
+            pltpu.SemaphoreType.DMA((2,)),
+        ],
+        compiler_params=pltpu.CompilerParams(vmem_limit_bytes=VMEM_LIMIT),
+        cost_estimate=COST,
+        name="unpack",
+    )(result)
+    return (image_out, jnp.transpose(text_out, (1, 0, 2)))
 
 
 def solution(mesh):

time: 110 us -> 110 us (level)
  local copies, waits for them, and re-layouts: 2.77 us -> 1.34 us
where the time goes in v6:
time: 110 us; the launch traced here: 109 us
  blocking collectives  34.1 us (31%)
  Pallas kernels  32 us (29%)
  waiting for transfers between devices  28.5 us (26%)
  starting transfers between devices  12.4 us (11%)
  local copies, waits for them, and re-layouts  1.34 us (1%)
    ppermute x22, waiting for transfers between devices, swap(): return lax.ppermute(values, axis, [(i, i ^ bit) for i in range(size)])  28.5 us
    all_to_all x1, blocking collectives, per_device(): lax.all_to_all(packed, 'tile', 0, 0, axis_index_groups=groups, tiled=True)  20.3 us
    all_to_all x1, blocking collectives, per_device(): lax.all_to_all(result, 'tile', 0, 0, axis_index_groups=groups, tiled=True)  13.8 us
    ppermute x22, starting transfers between devices, swap(): return lax.ppermute(values, axis, [(i, i ^ bit) for i in range(size)])  12.4 us
    pallas_call x2, Pallas kernels, mlp_call(): pl.pallas_call(mlp_kernel, out_shape=[kept, sent, sent], in_specs=[VM] *...  7.49 us
    pallas_call x2, Pallas kernels, qkv_call(): pl.pallas_call(functools.partial(qkv_kernel, begin, sources, parts), out_...  7.21 us
    pallas_call x2, Pallas kernels, attend_call(): pl.pallas_call(functools.partial(attend_kernel, start, counts, gate_rows)...  6.89 us
    pallas_call x1, Pallas kernels, prep_call(): pl.pallas_call(prep_kernel, out_shape=[jax.ShapeDtypeStruct((16, width),...  4.01 us
  transfers between devices with their start and end apart: 22, of which 14 were waited for; matrix products, arithmetic and copies ran while one was open for 0% of the time, Pallas kernels for 22%

profile of v6, /device:TPU:0, one launch (start us, length us, event | category | flops | bytes accessed | tf_op | source)
XLA Modules:
  0.0 109.4 jit_solution(9087086995705095065)
XLA Ops:
  0.6 1.1 pack.1
  1.7 20.3 %all_to_all.10.refs_2_.own_ref = bf16[16,40,384]{2,1,0:T(8,128)(2,1)S(1)} all-to-all(bf16[16,40,384]{2,1,0:T(8,128)(2,1)S(1)} %pack.1), channel_id=1, replica_groups={{0,4,16,20,32,36,48,52,64,68,80,84,96,100,112,116},{8,12,24,28,40,44,56..., dimensions={0} | all-to-all | bytes 983040 | tf_op jit(solution)/shard_map/all_to_all | solution.py:501
  21.9 1.0 collective-permute-start.1
  23.0 2.9 %collective-permute-start.3 = (bf16[16,40,384]{2,1,0:T(8,128)(2,1)S(1)}, bf16[16,40,384]{2,1,0:T(8,128)(2,1)S(1)}, u32[]{:S(2)}, u32[]{:S(2)}) collective-permute-start(bf16[16,40,384]{2,1,0:T(8,128)(2,1)S(1)} %all_to_all.10.refs_2_.own_ref), channel_id=1, source_target_pairs={{0,8},{4,12},{8,0},{12,4},{16,24},{20,28},{24,16},{28,20},{32,40},... | collective-permute-start | bytes 1474568 | tf_op jit(solution)/shard_map/ppermute | solution.py:354
  25.9 0.7 copy-done.2
  26.5 0.7 copy-done.3
  27.2 4.0 %prep.1 = (f32[16,1536]{1,0:T(8,128)S(1)}, f32[8,128]{1,0:T(8,128)S(1)}, bf16[2,128,128]{2,1,0:T(8,128)(2,1)S(1)}, bf16[1536,1152]{1,0:T(8,128)(2,1)S(1)}, bf16[1536,1152]{1,0:T(8,128)(2,1)S(1)}) custom-call(s32[16]{0:T(128)S(1)} %copy-done.2, s32[16]{0:T(128)S(1)} %copy-done.3, bf16[6,28,1536]{2,1,0:T(8,128)(2,1)} %bitcast.16, ...), custom_call_target="tpu_custom_call" | custom-call | flops 1 | bytes 1 | tf_op jit(solution)/shard_map/prep/pallas_call | solution.py:86
  31.3 1.9 %collective-permute-done.1.refs_4_.far_ref = bf16[16,40,384]{2,1,0:T(8,128)(2,1)S(1)} collective-permute-done((bf16[16,40,384]{2,1,0:T(8,128)(2,1)S(1)}, bf16[16,40,384]{2,1,0:T(8,128)(2,1)S(1)}, u32[]{:S(2)}, u32[]{:S(2)}) %collective-permute-start.1) | collective-permute-done | bytes 491552 | tf_op jit(solution)/shard_map/ppermute | solution.py:354
  33.2 2.2 %collective-permute-done.3.refs_2_ = bf16[16,40,384]{2,1,0:T(8,128)(2,1)S(1)} collective-permute-done((bf16[16,40,384]{2,1,0:T(8,128)(2,1)S(1)}, bf16[16,40,384]{2,1,0:T(8,128)(2,1)S(1)}, u32[]{:S(2)}, u32[]{:S(2)}) %collective-permute-start.3) | collective-permute-done | bytes 491552 | tf_op jit(solution)/shard_map/ppermute | solution.py:354
  35.5 1.0 collective-permute-start.5
  36.5 4.3 %qkv.2 = (bf16[640,384]{1,0:T(8,128)(2,1)S(1)}, bf16[2,640,384]{2,1,0:T(8,128)(2,1)S(1)}) custom-call(f32[16,1536]{1,0:T(8,128)S(1)} %get-tuple-element.82.refs_0_.mods, f32[8,128]{1,0:T(8,128)S(1)} %get-tuple-element.50.refs_1_, bf16[16,40,384]{2,1,0:T(8,128)(2,1)S(1)} %all_to_all.10.refs_2_.own_ref, bf16[16,40,384]{2,1,0:T(8,128)(2,1)S(1)} %collective-permute-done.refs_3_, ...), custom_call_target="tpu_custom_call" | custom-call | flops 1 | bytes 1 | tf_op jit(solution)/shard_map/qkv/pallas_call | solution.py:176
  40.8 3.7 %attend_own.1 = (f32[640,384]{1,0:T(8,128)S(1)}, f32[640,384]{1,0:T(8,128)S(1)}, f32[640,384]{1,0:T(8,128)S(1)}) custom-call(bf16[2,128,128]{2,1,0:T(8,128)(2,1)S(1)} %get-tuple-element.49.bias_ref.refs_1_, bf16[640,384]{1,0:T(8,128)(2,1)S(1)} %get-tuple-element.54.q_ref.refs_2_, bf16[2,640,384]{2,1,0:T(8,128)(2,1)S(1)} %get-tuple-element.55.kv_ref), custom_call_target="tpu_custom_call" | custom-call | flops 1 | bytes 1 | tf_op jit(solution)/shard_map/attend_own/pallas_call | solution.py:240
  44.6 2.3 %collective-permute-done.5.refs_4_ = bf16[16,40,384]{2,1,0:T(8,128)(2,1)S(1)} collective-permute-done((bf16[16,40,384]{2,1,0:T(8,128)(2,1)S(1)}, bf16[16,40,384]{2,1,0:T(8,128)(2,1)S(1)}, u32[]{:S(2)}, u32[]{:S(2)}) %collective-permute-start.5) | collective-permute-done | bytes 491552 | tf_op jit(solution)/shard_map/ppermute | solution.py:354
  46.9 1.9 %collective-permute-done.6.refs_5_ = bf16[16,40,384]{2,1,0:T(8,128)(2,1)S(1)} collective-permute-done((bf16[16,40,384]{2,1,0:T(8,128)(2,1)S(1)}, bf16[16,40,384]{2,1,0:T(8,128)(2,1)S(1)}, u32[]{:S(2)}, u32[]{:S(2)}) %collective-permute-start.6) | collective-permute-done | bytes 491552 | tf_op jit(solution)/shard_map/ppermute | solution.py:354
  48.7 3.0 %qkv.3.refs_6_ = bf16[2,640,384]{2,1,0:T(8,128)(2,1)S(1)} custom-call(f32[16,1536]{1,0:T(8,128)S(1)} %get-tuple-element.82.refs_0_.mods, f32[8,128]{1,0:T(8,128)S(1)} %get-tuple-element.50.refs_1_, bf16[16,40,384]{2,1,0:T(8,128)(2,1)S(1)} %collective-permute-done.3.refs_2_, bf16[16,40,384]{2,1,0:T(8,128)(2,1)S(1)} %collective-permute-done.4.refs_3_, ...), custom_call_target="tpu_custom_call" | custom-call | flops 1 | bytes 1 | tf_op jit(solution)/shard_map/qkv/pallas_call | solution.py:176
  51.7 3.3 %attend.2 = (bf16[2,320,384]{2,1,0:T(8,128)(2,1)S(1)}, bf16[2,320,384]{2,1,0:T(8,128)(2,1)S(1)}) custom-call(f32[16,1536]{1,0:T(8,128)S(1)} %get-tuple-element.82.refs_0_.mods, bf16[2,128,128]{2,1,0:T(8,128)(2,1)S(1)} %get-tuple-element.49.bias_ref.refs_1_, bf16[640,384]{1,0:T(8,128)(2,1)S(1)} %get-tuple-element.54.q_ref.refs_2_, ...), custom_call_target="tpu_custom_call" | custom-call | flops 1 | bytes 1 | tf_op jit(solution)/shard_map/attend/pallas_call | solution.py:311
  55.2 1.7 %collective-permute-done.7.right_ref = bf16[2,320,384]{2,1,0:T(8,128)(2,1)S(1)} collective-permute-done((bf16[2,320,384]{2,1,0:T(8,128)(2,1)S(1)}, bf16[2,320,384]{2,1,0:T(8,128)(2,1)S(1)}, u32[]{:S(2)}, u32[]{:S(2)}) %collective-permute-start.7) | collective-permute-done | bytes 491552 | tf_op jit(solution)/shard_map/ppermute | solution.py:354
  57.1 1.1 %collective-permute-start.11 = (bf16[2,320,384]{2,1,0:T(8,128)(2,1)S(1)}, bf16[2,320,384]{2,1,0:T(8,128)(2,1)S(1)}, u32[]{:S(2)}, u32[]{:S(2)}) collective-permute-start(bf16[2,320,384]{2,1,0:T(8,128)(2,1)S(1)} %core_sum.1.sum_ref), channel_id=1, source_target_pairs={{0,2},{1,3},{2,0},{3,1},{4,6},{5,7},{6,4},{7,5},{8,10},{9,11},{10,... | collective-permute-start | bytes 1474568 | tf_op jit(solution)/shard_map/ppermute | solution.py:354
  58.2 3.6 %attend.3 = (bf16[2,192,384]{2,1,0:T(8,128)(2,1)S(1)}, bf16[2,192,384]{2,1,0:T(8,128)(2,1)S(1)}, bf16[2,128,384]{2,1,0:T(8,128)(2,1)S(1)}, bf16[2,128,384]{2,1,0:T(8,128)(2,1)S(1)}) custom-call(f32[16,1536]{1,0:T(8,128)S(1)} %get-tuple-element.82.refs_0_.mods, bf16[2,128,128]{2,1,0:T(8,128)(2,1)S(1)} %get-tuple-element.49.bias_ref.refs_1_, ...), custom_call_target="tpu_custom_call" | custom-call | flops 1 | bytes 1 | tf_op jit(solution)/shard_map/attend/pallas_call | solution.py:311
  62.4 1.4 %collective-permute-done.8.came_t = bf16[2,128,384]{2,1,0:T(8,128)(2,1)S(1)} collective-permute-done((bf16[2,128,384]{2,1,0:T(8,128)(2,1)S(1)}, bf16[2,128,384]{2,1,0:T(8,128)(2,1)S(1)}, u32[]{:S(2)}, u32[]{:S(2)}) %collective-permute-start.8) | collective-permute-done | bytes 196640 | tf_op jit(solution)/shard_map/ppermute | solution.py:354
  63.9 1.1 collective-permute-start.10
  65.0 6.3 %collective-permute-done.11.back_ref = bf16[2,320,384]{2,1,0:T(8,128)(2,1)S(1)} collective-permute-done((bf16[2,320,384]{2,1,0:T(8,128)(2,1)S(1)}, bf16[2,320,384]{2,1,0:T(8,128)(2,1)S(1)}, u32[]{:S(2)}, u32[]{:S(2)}) %collective-permute-start.11) | collective-permute-done | bytes 491552 | tf_op jit(solution)/shard_map/ppermute | solution.py:354
  72.0 1.0 collective-permute-done.13.n1
  73.4 4.6 %mlp.2 = (bf16[2,320,384]{2,1,0:T(8,128)(2,1)S(1)}, bf16[320,384]{1,0:T(8,128)(2,1)S(1)}, bf16[320,384]{1,0:T(8,128)(2,1)S(1)}) custom-call(f32[16,1536]{1,0:T(8,128)S(1)} %get-tuple-element.82.refs_0_.mods, bf16[320,384]{1,0:T(8,128)(2,1)S(1)} %get-tuple-element.73.m0.mid_a, bf16[320,384]{1,0:T(8,128)(2,1)S(1)} %get-tuple-element.74.m1, ...), custom_call_target="tpu_custom_call" | custom-call | flops 1 | bytes 1 | tf_op jit(solution)/shard_map/mlp/pallas_call | solution.py:341
  79.6 0.9 collective-permute-done.16.n1
  80.7 1.1 %collective-permute-start.18 = (bf16[320,384]{1,0:T(8,128)(2,1)S(1)}, bf16[320,384]{1,0:T(8,128)(2,1)S(1)}, u32[]{:S(2)}, u32[]{:S(2)}) collective-permute-start(bf16[320,384]{1,0:T(8,128)(2,1)S(1)} %away.2), channel_id=1, source_target_pairs={{0,2},{1,3},{2,0},{3,1},{4,6},{5,7},{6,4},{7,5},{8,10},{9,11},{10,... | collective-permute-start | bytes 737288 | tf_op jit(solution)/shard_map/ppermute | solution.py:354
  81.9 2.9 %mlp.3 = (bf16[2,192,384]{2,1,0:T(8,128)(2,1)S(1)}, bf16[192,384]{1,0:T(8,128)(2,1)S(1)}, bf16[192,384]{1,0:T(8,128)(2,1)S(1)}) custom-call(f32[16,1536]{1,0:T(8,128)S(1)} %get-tuple-element.82.refs_0_.mods, bf16[192,384]{1,0:T(8,128)(2,1)S(1)} %get-tuple-element.78.m0.mid_b, bf16[192,384]{1,0:T(8,128)(2,1)S(1)} %get-tuple-element.79.m1, ...), custom_call_target="tpu_custom_call" | custom-call | flops 1 | bytes 1 | tf_op jit(solution)/shard_map/mlp/pallas_call | solution.py:341
  85.4 3.6 %collective-permute-done.18.last_a = bf16[320,384]{1,0:T(8,128)(2,1)S(1)} collective-permute-done((bf16[320,384]{1,0:T(8,128)(2,1)S(1)}, bf16[320,384]{1,0:T(8,128)(2,1)S(1)}, u32[]{:S(2)}, u32[]{:S(2)}) %collective-permute-start.18) | collective-permute-done | bytes 245792 | tf_op jit(solution)/shard_map/ppermute | solution.py:354
  89.2 1.1 %collective-permute-start.21 = (bf16[192,384]{1,0:T(8,128)(2,1)S(1)}, bf16[192,384]{1,0:T(8,128)(2,1)S(1)}, u32[]{:S(2)}, u32[]{:S(2)}) collective-permute-start(bf16[192,384]{1,0:T(8,128)(2,1)S(1)} %away.3), channel_id=1, source_target_pairs={{0,2},{1,3},{2,0},{3,1},{4,6},{5,7},{6,4},{7,5},{8,10},{9,11},{10,... | collective-permute-start | bytes 442376 | tf_op jit(solution)/shard_map/ppermute | solution.py:354
  90.3 4.2 %collective-permute-done.21.last_b = bf16[192,384]{1,0:T(8,128)(2,1)S(1)} collective-permute-done((bf16[192,384]{1,0:T(8,128)(2,1)S(1)}, bf16[192,384]{1,0:T(8,128)(2,1)S(1)}, u32[]{:S(2)}, u32[]{:S(2)}) %collective-permute-start.21) | collective-permute-done | bytes 147488 | tf_op jit(solution)/shard_map/ppermute | solution.py:354
  94.6 13.8 %all_to_all.11.rows_ref = bf16[16,40,384]{2,1,0:T(8,128)(2,1)S(1)} all-to-all(bf16[16,40,384]{2,1,0:T(8,128)(2,1)S(1)} %final.1), channel_id=1, replica_groups={{0,4,16,20,32,36,48,52,64,68,80,84,96,100,112,116},{8,12,24,28,40,44,56..., dimensions={0} | all-to-all | bytes 983040 | tf_op jit(solution)/shard_map/all_to_all | solution.py:574
  108.5 0.8 unpack.1
  (50 shorter events, 5.1 us)
Async XLA Ops:
  21.9 11.3 %collective-permute-start.1 = (bf16[16,40,384]{2,1,0:T(8,128)(2,1)S(1)}, bf16[16,40,384]{2,1,0:T(8,128)(2,1)S(1)}, u32[]{:S(2)}, u32[]{:S(2)}) collective-permute-start(bf16[16,40,384]{2,1,0:T(8,128)(2,1)S(1)} %all_to_all.10.refs_2_.own_ref), channel_id=1, source_target_pairs={{0,2},{1,3},{2,0},{3,1},{4,6},{5,7},{6,4},{7,5},{8,10},{9,11},{10,... | collective-permute-start | bytes 1474568 | tf_op jit(solution)/shard_map/ppermute | solution.py:354
  23.0 12.5 %collective-permute-start.3 = (bf16[16,40,384]{2,1,0:T(8,128)(2,1)S(1)}, bf16[16,40,384]{2,1,0:T(8,128)(2,1)S(1)}, u32[]{:S(2)}, u32[]{:S(2)}) collective-permute-start(bf16[16,40,384]{2,1,0:T(8,128)(2,1)S(1)} %all_to_all.10.refs_2_.own_ref), channel_id=1, source_target_pairs={{0,8},{4,12},{8,0},{12,4},{16,24},{20,28},{24,16},{28,20},{32,40},... | collective-permute-start | bytes 1474568 | tf_op jit(solution)/shard_map/ppermute | solution.py:354
  25.9 0.7 copy-start.2
  26.5 0.7 copy-start.3
  31.2 5.3 %collective-permute-start = (bf16[16,40,384]{2,1,0:T(8,128)(2,1)S(1)}, bf16[16,40,384]{2,1,0:T(8,128)(2,1)S(1)}, u32[]{:S(2)}, u32[]{:S(2)}) collective-permute-start(bf16[16,40,384]{2,1,0:T(8,128)(2,1)S(1)} %all_to_all.10.refs_2_.own_ref), channel_id=1, source_target_pairs={{0,1},{1,0},{2,3},{3,2},{4,5},{5,4},{6,7},{7,6},{8,9},{9,8},{10,11... | collective-permute-start | bytes 1474568 | tf_op jit(solution)/shard_map/ppermute | solution.py:354
  33.2 3.3 %collective-permute-start.2 = (bf16[16,40,384]{2,1,0:T(8,128)(2,1)S(1)}, bf16[16,40,384]{2,1,0:T(8,128)(2,1)S(1)}, u32[]{:S(2)}, u32[]{:S(2)}) collective-permute-start(bf16[16,40,384]{2,1,0:T(8,128)(2,1)S(1)} %collective-permute-done.1.refs_4_.far_ref), channel_id=1, source_target_pairs={{0,1},{1,0},{2,3},{3,2},{4,5},{5,4},{6,7},{7,6},{8,9},{9,8},{10,11... | collective-permute-start | bytes 1474568 | tf_op jit(solution)/shard_map/ppermute | solution.py:354
  35.5 11.4 %collective-permute-start.5 = (bf16[16,40,384]{2,1,0:T(8,128)(2,1)S(1)}, bf16[16,40,384]{2,1,0:T(8,128)(2,1)S(1)}, u32[]{:S(2)}, u32[]{:S(2)}) collective-permute-start(bf16[16,40,384]{2,1,0:T(8,128)(2,1)S(1)} %collective-permute-done.3.refs_2_), channel_id=1, source_target_pairs={{0,2},{1,3},{2,0},{3,1},{4,6},{5,7},{6,4},{7,5},{8,10},{9,11},{10,... | collective-permute-start | bytes 1474568 | tf_op jit(solution)/shard_map/ppermute | solution.py:354
  40.7 6.1 %collective-permute-start.4 = (bf16[16,40,384]{2,1,0:T(8,128)(2,1)S(1)}, bf16[16,40,384]{2,1,0:T(8,128)(2,1)S(1)}, u32[]{:S(2)}, u32[]{:S(2)}) collective-permute-start(bf16[16,40,384]{2,1,0:T(8,128)(2,1)S(1)} %collective-permute-done.3.refs_2_), channel_id=1, source_target_pairs={{0,1},{1,0},{2,3},{3,2},{4,5},{5,4},{6,7},{7,6},{8,9},{9,8},{10,11... | collective-permute-start | bytes 1474568 | tf_op jit(solution)/shard_map/ppermute | solution.py:354
  46.9 4.8 %copy-start = (bf16[384,1536]{1,0:T(8,128)(2,1)S(1)}, bf16[384,1536]{1,0:T(8,128)(2,1)}, u32[]{:S(2)}) copy-start(bf16[384,1536]{1,0:T(8,128)(2,1)} %refs_7_.3) | copy-start | bytes 3538948
  46.9 1.9 %collective-permute-start.6 = (bf16[16,40,384]{2,1,0:T(8,128)(2,1)S(1)}, bf16[16,40,384]{2,1,0:T(8,128)(2,1)S(1)}, u32[]{:S(2)}, u32[]{:S(2)}) collective-permute-start(bf16[16,40,384]{2,1,0:T(8,128)(2,1)S(1)} %collective-permute-done.5.refs_4_), channel_id=1, source_target_pairs={{0,1},{1,0},{2,3},{3,2},{4,5},{5,4},{6,7},{7,6},{8,9},{9,8},{10,11... | collective-permute-start | bytes 1474568 | tf_op jit(solution)/shard_map/ppermute | solution.py:354
  48.7 24.7 %slice-start.2 = ((s8[4718592]{0:T(1024)(128)(4,1)}), s8[4194304]{0:T(1024)(128)(4,1)S(1)}, s32[]{:S(2)}) async-start(s8[4718592]{0:T(1024)(128)(4,1)} %bitcast.12), calls=%async_computation.4 | async-start | bytes 8388608
  51.7 6.5 %copy-start.1 = (bf16[384,1536]{1,0:T(8,128)(2,1)S(1)}, bf16[384,1536]{1,0:T(8,128)(2,1)}, u32[]{:S(2)}) copy-start(bf16[384,1536]{1,0:T(8,128)(2,1)} %refs_8_.1) | copy-start | bytes 3538948
  51.7 21.7 %slice-start.3 = ((s8[4718592]{0:T(1024)(128)(4,1)}), s8[524288]{0:T(1024)(128)(4,1)S(1)}, s32[]{:S(2)}) async-start(s8[4718592]{0:T(1024)(128)(4,1)} %bitcast.12), calls=%async_computation.5 | async-start | bytes 1048576
  55.0 1.9 %collective-permute-start.7 = (bf16[2,320,384]{2,1,0:T(8,128)(2,1)S(1)}, bf16[2,320,384]{2,1,0:T(8,128)(2,1)S(1)}, u32[]{:S(2)}, u32[]{:S(2)}) collective-permute-start(bf16[2,320,384]{2,1,0:T(8,128)(2,1)S(1)} %get-tuple-element.64), channel_id=1, source_target_pairs={{0,1},{1,0},{2,3},{3,2},{4,5},{5,4},{6,7},{7,6},{8,9},{9,8},{10,11... | collective-permute-start | bytes 1474568 | tf_op jit(solution)/shard_map/ppermute | solution.py:354
  57.0 16.4 %slice-start = ((s8[4718592]{0:T(1024)(128)(4,1)}), s8[4194304]{0:T(1024)(128)(4,1)S(1)}, s32[]{:S(2)}) async-start(s8[4718592]{0:T(1024)(128)(4,1)} %bitcast.10), calls=%async_computation.2 | async-start | bytes 8388608
  57.1 16.3 %slice-start.1 = ((s8[4718592]{0:T(1024)(128)(4,1)}), s8[524288]{0:T(1024)(128)(4,1)S(1)}, s32[]{:S(2)}) async-start(s8[4718592]{0:T(1024)(128)(4,1)} %bitcast.10), calls=%async_computation.3 | async-start | bytes 1048576
  57.1 14.1 %collective-permute-start.11 = (bf16[2,320,384]{2,1,0:T(8,128)(2,1)S(1)}, bf16[2,320,384]{2,1,0:T(8,128)(2,1)S(1)}, u32[]{:S(2)}, u32[]{:S(2)}) collective-permute-start(bf16[2,320,384]{2,1,0:T(8,128)(2,1)S(1)} %core_sum.1.sum_ref), channel_id=1, source_target_pairs={{0,2},{1,3},{2,0},{3,1},{4,6},{5,7},{6,4},{7,5},{8,10},{9,11},{10,... | collective-permute-start | bytes 1474568 | tf_op jit(solution)/shard_map/ppermute | solution.py:354
  61.8 1.9 %collective-permute-start.9 = (bf16[2,192,384]{2,1,0:T(8,128)(2,1)S(1)}, bf16[2,192,384]{2,1,0:T(8,128)(2,1)S(1)}, u32[]{:S(2)}, u32[]{:S(2)}) collective-permute-start(bf16[2,192,384]{2,1,0:T(8,128)(2,1)S(1)} %get-tuple-element.69), channel_id=1, source_target_pairs={{0,1},{1,0},{2,3},{3,2},{4,5},{5,4},{6,7},{7,6},{8,9},{9,8},{10,11... | collective-permute-start | bytes 884744 | tf_op jit(solution)/shard_map/ppermute | solution.py:354
  61.9 1.9 %collective-permute-start.8 = (bf16[2,128,384]{2,1,0:T(8,128)(2,1)S(1)}, bf16[2,128,384]{2,1,0:T(8,128)(2,1)S(1)}, u32[]{:S(2)}, u32[]{:S(2)}) collective-permute-start(bf16[2,128,384]{2,1,0:T(8,128)(2,1)S(1)} %get-tuple-element.67), channel_id=1, source_target_pairs={{0,1},{1,0},{2,3},{3,2},{4,5},{5,4},{6,7},{7,6},{8,9},{9,8},{10,11... | collective-permute-start | bytes 589832 | tf_op jit(solution)/shard_map/ppermute | solution.py:354
  63.9 15.0 %collective-permute-start.10 = (bf16[2,256,384]{2,1,0:T(8,128)(2,1)S(1)}, bf16[2,256,384]{2,1,0:T(8,128)(2,1)S(1)}, u32[]{:S(2)}, u32[]{:S(2)}) collective-permute-start(bf16[2,256,384]{2,1,0:T(8,128)(2,1)S(1)} %get-tuple-element.70), channel_id=1, source_target_pairs={{0,2},{1,3},{2,0},{3,1},{4,6},{5,7},{6,4},{7,5},{8,10},{9,11},{10,... | collective-permute-start | bytes 1179656 | tf_op jit(solution)/shard_map/ppermute | solution.py:354
  71.5 1.6 %collective-permute-start.13 = (bf16[320,384]{1,0:T(8,128)(2,1)S(1)}, bf16[320,384]{1,0:T(8,128)(2,1)S(1)}, u32[]{:S(2)}, u32[]{:S(2)}) collective-permute-start(bf16[320,384]{1,0:T(8,128)(2,1)S(1)} %get-tuple-element.74.m1), channel_id=1, source_target_pairs={{0,1},{1,0},{2,3},{3,2},{4,5},{5,4},{6,7},{7,6},{8,9},{9,8},{10,11... | collective-permute-start | bytes 737288 | tf_op jit(solution)/shard_map/ppermute | solution.py:354
  71.5 1.9 %collective-permute-start.12 = (bf16[320,384]{1,0:T(8,128)(2,1)S(1)}, bf16[320,384]{1,0:T(8,128)(2,1)S(1)}, u32[]{:S(2)}, u32[]{:S(2)}) collective-permute-start(bf16[320,384]{1,0:T(8,128)(2,1)S(1)} %get-tuple-element.73.m0.mid_a), channel_id=1, source_target_pairs={{0,1},{1,0},{2,3},{3,2},{4,5},{5,4},{6,7},{7,6},{8,9},{9,8},{10,11... | collective-permute-start | bytes 737288 | tf_op jit(solution)/shard_map/ppermute | solution.py:354
  78.1 2.6 %collective-permute-start.17 = (bf16[320,384]{1,0:T(8,128)(2,1)S(1)}, bf16[320,384]{1,0:T(8,128)(2,1)S(1)}, u32[]{:S(2)}, u32[]{:S(2)}) collective-permute-start(bf16[320,384]{1,0:T(8,128)(2,1)S(1)} %get-tuple-element.81), channel_id=1, source_target_pairs={{0,1},{1,0},{2,3},{3,2},{4,5},{5,4},{6,7},{7,6},{8,9},{9,8},{10,11... | collective-permute-start | bytes 737288 | tf_op jit(solution)/shard_map/ppermute | solution.py:354
  79.0 1.5 %collective-permute-start.16 = (bf16[192,384]{1,0:T(8,128)(2,1)S(1)}, bf16[192,384]{1,0:T(8,128)(2,1)S(1)}, u32[]{:S(2)}, u32[]{:S(2)}) collective-permute-start(bf16[192,384]{1,0:T(8,128)(2,1)S(1)} %get-tuple-element.79.m1), channel_id=1, source_target_pairs={{0,1},{1,0},{2,3},{3,2},{4,5},{5,4},{6,7},{7,6},{8,9},{9,8},{10,11... | collective-permute-start | bytes 442376 | tf_op jit(solution)/shard_map/ppermute | solution.py:354
  79.1 1.6 %collective-permute-start.15 = (bf16[192,384]{1,0:T(8,128)(2,1)S(1)}, bf16[192,384]{1,0:T(8,128)(2,1)S(1)}, u32[]{:S(2)}, u32[]{:S(2)}) collective-permute-start(bf16[192,384]{1,0:T(8,128)(2,1)S(1)} %get-tuple-element.78.m0.mid_b), channel_id=1, source_target_pairs={{0,1},{1,0},{2,3},{3,2},{4,5},{5,4},{6,7},{7,6},{8,9},{9,8},{10,11... | collective-permute-start | bytes 442376 | tf_op jit(solution)/shard_map/ppermute | solution.py:354
  80.7 8.2 %collective-permute-start.18 = (bf16[320,384]{1,0:T(8,128)(2,1)S(1)}, bf16[320,384]{1,0:T(8,128)(2,1)S(1)}, u32[]{:S(2)}, u32[]{:S(2)}) collective-permute-start(bf16[320,384]{1,0:T(8,128)(2,1)S(1)} %away.2), channel_id=1, source_target_pairs={{0,2},{1,3},{2,0},{3,1},{4,6},{5,7},{6,4},{7,5},{8,10},{9,11},{10,... | collective-permute-start | bytes 737288 | tf_op jit(solution)/shard_map/ppermute | solution.py:354
  81.9 7.1 %collective-permute-start.14 = (bf16[320,384]{1,0:T(8,128)(2,1)S(1)}, bf16[320,384]{1,0:T(8,128)(2,1)S(1)}, u32[]{:S(2)}, u32[]{:S(2)}) collective-permute-start(bf16[320,384]{1,0:T(8,128)(2,1)S(1)} %get-tuple-element.76), channel_id=1, source_target_pairs={{0,1},{1,0},{2,3},{3,2},{4,5},{5,4},{6,7},{7,6},{8,9},{9,8},{10,11... | collective-permute-start | bytes 737288 | tf_op jit(solution)/shard_map/ppermute | solution.py:354
  84.7 4.4 %collective-permute-start.20 = (bf16[192,384]{1,0:T(8,128)(2,1)S(1)}, bf16[192,384]{1,0:T(8,128)(2,1)S(1)}, u32[]{:S(2)}, u32[]{:S(2)}) collective-permute-start(bf16[192,384]{1,0:T(8,128)(2,1)S(1)} %get-tuple-element.89), channel_id=1, source_target_pairs={{0,1},{1,0},{2,3},{3,2},{4,5},{5,4},{6,7},{7,6},{8,9},{9,8},{10,11... | collective-permute-start | bytes 442376 | tf_op jit(solution)/shard_map/ppermute | solution.py:354
  85.3 5.0 %collective-permute-start.19 = (bf16[192,384]{1,0:T(8,128)(2,1)S(1)}, bf16[192,384]{1,0:T(8,128)(2,1)S(1)}, u32[]{:S(2)}, u32[]{:S(2)}) collective-permute-start(bf16[192,384]{1,0:T(8,128)(2,1)S(1)} %get-tuple-element.87), channel_id=1, source_target_pairs={{0,1},{1,0},{2,3},{3,2},{4,5},{5,4},{6,7},{7,6},{8,9},{9,8},{10,11... | collective-permute-start | bytes 442376 | tf_op jit(solution)/shard_map/ppermute | solution.py:354
  89.2 5.3 %collective-permute-start.21 = (bf16[192,384]{1,0:T(8,128)(2,1)S(1)}, bf16[192,384]{1,0:T(8,128)(2,1)S(1)}, u32[]{:S(2)}, u32[]{:S(2)}) collective-permute-start(bf16[192,384]{1,0:T(8,128)(2,1)S(1)} %away.3), channel_id=1, source_target_pairs={{0,2},{1,3},{2,0},{3,1},{4,6},{5,7},{6,4},{7,5},{8,10},{9,11},{10,... | collective-permute-start | bytes 442376 | tf_op jit(solution)/shard_map/ppermute | solution.py:354

commit v7 on v6

--- a/solution.py
+++ b/solution.py
@@ -10,6 +10,7 @@
 HEAD_DIM = 64
 BF = jnp.bfloat16
 F32 = jnp.float32
+QUERY_SCALE = HEAD_DIM**-0.5 * 1.4426950408889634
 HIDDEN_BIAS = -32768.0
 TXT_PAD = 8
 PARTS = (1, 2, 0)
@@ -160,11 +161,11 @@
                 kv_ref[1, first:last, :] = values.astype(BF)
                 continue
             gain = jnp.concatenate([gains[row + which : row + which + 1, :]] * (part // 128), axis=1)
-            normed = (values * head_scale(values, group) * gain).astype(BF)
+            normed = values * head_scale(values, group) * gain
             if which == 1:
-                kv_ref[0, first:last, :] = normed
+                kv_ref[0, first:last, :] = normed.astype(BF)
             else:
-                outs[0][first:last, :] = normed * BF(HEAD_DIM**-0.5)
+                outs[0][first:last, :] = (normed * QUERY_SCALE).astype(BF)
 
 
 def qkv_call(mods, gains, pieces, begin, sources, weights, parts):
@@ -226,7 +227,7 @@
             for head in range(2):
                 score = head_scores(q_ref[span, cols], [key], lane, one_lane, head)[0]
                 top = jnp.max(score, axis=-1, keepdims=True)
-                both = dot(jnp.exp(score - top).astype(BF), value)
+                both = dot(jnp.exp2(score - top).astype(BF), value)
                 tops.append(top)
                 outs.append(both[:, :128])
                 sums.append(both[:, 128:])
@@ -266,10 +267,10 @@
             score = head_scores(q_ref[span, cols], [key], lane, one_lane, head)[0]
             before = top_ref[span, col + 64 * head : col + 64 * head + 1]
             top = jnp.maximum(before, jnp.max(score, axis=-1, keepdims=True))
-            both = dot(jnp.exp(score - top).astype(BF), val)
+            both = dot(jnp.exp2(score - top).astype(BF), val)
             outs.append(both[:, :128])
             sums.append(both[:, 128:])
-            scales.append(jnp.exp(before - top))
+            scales.append(jnp.exp2(before - top))
         scale = both_halves(scales, lane)
         total = both_halves(sums, lane) + scale * sum_ref[span, cols]
         att.append(((both_halves(outs, lane) + scale * out_ref[span, cols]) / total).astype(BF))

time: 110 us -> 110 us (level)
  no operation moved by 1% of the time
where the time goes in v7:
time: 110 us; the launch traced here: 109 us
  blocking collectives  34.1 us (31%)
  Pallas kernels  31.9 us (29%)
  waiting for transfers between devices  28.6 us (26%)
  starting transfers between devices  12.4 us (11%)
  local copies, waits for them, and re-layouts  1.34 us (1%)
    ppermute x22, waiting for transfers between devices, swap(): return lax.ppermute(values, axis, [(i, i ^ bit) for i in range(size)])  28.6 us
    all_to_all x1, blocking collectives, per_device(): lax.all_to_all(packed, 'tile', 0, 0, axis_index_groups=groups, tiled=True)  20.3 us
    all_to_all x1, blocking collectives, per_device(): lax.all_to_all(result, 'tile', 0, 0, axis_index_groups=groups, tiled=True)  13.8 us
    ppermute x22, starting transfers between devices, swap(): return lax.ppermute(values, axis, [(i, i ^ bit) for i in range(size)])  12.4 us
    pallas_call x2, Pallas kernels, mlp_call(): pl.pallas_call(mlp_kernel, out_shape=[kept, sent, sent], in_specs=[VM] *...  7.49 us
    pallas_call x2, Pallas kernels, qkv_call(): pl.pallas_call(functools.partial(qkv_kernel, begin, sources, parts), out_...  7.22 us
    pallas_call x2, Pallas kernels, attend_call(): pl.pallas_call(functools.partial(attend_kernel, start, counts, gate_rows)...  6.76 us
    pallas_call x1, Pallas kernels, prep_call(): pl.pallas_call(prep_kernel, out_shape=[jax.ShapeDtypeStruct((16, width),...  4.01 us
  transfers between devices with their start and end apart: 22, of which 14 were waited for; matrix products, arithmetic and copies ran while one was open for 0% of the time, Pallas kernels for 22%

profile of v7, /device:TPU:0, one launch (start us, length us, event | category | flops | bytes accessed | tf_op | source)
XLA Modules:
  0.0 109.3 jit_solution(10277771932555879912)
XLA Ops:
  0.6 1.1 pack.1
  1.7 20.3 %all_to_all.10.refs_2_.own_ref = bf16[16,40,384]{2,1,0:T(8,128)(2,1)S(1)} all-to-all(bf16[16,40,384]{2,1,0:T(8,128)(2,1)S(1)} %pack.1), channel_id=1, replica_groups={{0,4,16,20,32,36,48,52,64,68,80,84,96,100,112,116},{8,12,24,28,40,44,56..., dimensions={0} | all-to-all | bytes 983040 | tf_op jit(solution)/shard_map/all_to_all | solution.py:502
  21.9 1.0 collective-permute-start.1
  23.0 2.9 %collective-permute-start.3 = (bf16[16,40,384]{2,1,0:T(8,128)(2,1)S(1)}, bf16[16,40,384]{2,1,0:T(8,128)(2,1)S(1)}, u32[]{:S(2)}, u32[]{:S(2)}) collective-permute-start(bf16[16,40,384]{2,1,0:T(8,128)(2,1)S(1)} %all_to_all.10.refs_2_.own_ref), channel_id=1, source_target_pairs={{0,8},{4,12},{8,0},{12,4},{16,24},{20,28},{24,16},{28,20},{32,40},... | collective-permute-start | bytes 1474568 | tf_op jit(solution)/shard_map/ppermute | solution.py:355
  25.9 0.7 copy-done.2
  26.5 0.7 copy-done.3
  27.2 4.0 %prep.1 = (f32[16,1536]{1,0:T(8,128)S(1)}, f32[8,128]{1,0:T(8,128)S(1)}, bf16[2,128,128]{2,1,0:T(8,128)(2,1)S(1)}, bf16[1536,1152]{1,0:T(8,128)(2,1)S(1)}, bf16[1536,1152]{1,0:T(8,128)(2,1)S(1)}) custom-call(s32[16]{0:T(128)S(1)} %copy-done.2, s32[16]{0:T(128)S(1)} %copy-done.3, bf16[6,28,1536]{2,1,0:T(8,128)(2,1)} %bitcast.16, ...), custom_call_target="tpu_custom_call" | custom-call | flops 1 | bytes 1 | tf_op jit(solution)/shard_map/prep/pallas_call | solution.py:87
  31.3 1.9 %collective-permute-done.1.refs_4_.far_ref = bf16[16,40,384]{2,1,0:T(8,128)(2,1)S(1)} collective-permute-done((bf16[16,40,384]{2,1,0:T(8,128)(2,1)S(1)}, bf16[16,40,384]{2,1,0:T(8,128)(2,1)S(1)}, u32[]{:S(2)}, u32[]{:S(2)}) %collective-permute-start.1) | collective-permute-done | bytes 491552 | tf_op jit(solution)/shard_map/ppermute | solution.py:355
  33.2 2.2 %collective-permute-done.3.refs_2_ = bf16[16,40,384]{2,1,0:T(8,128)(2,1)S(1)} collective-permute-done((bf16[16,40,384]{2,1,0:T(8,128)(2,1)S(1)}, bf16[16,40,384]{2,1,0:T(8,128)(2,1)S(1)}, u32[]{:S(2)}, u32[]{:S(2)}) %collective-permute-start.3) | collective-permute-done | bytes 491552 | tf_op jit(solution)/shard_map/ppermute | solution.py:355
  35.5 1.0 collective-permute-start.5
  36.5 4.3 %qkv.2 = (bf16[640,384]{1,0:T(8,128)(2,1)S(1)}, bf16[2,640,384]{2,1,0:T(8,128)(2,1)S(1)}) custom-call(f32[16,1536]{1,0:T(8,128)S(1)} %get-tuple-element.82.refs_0_.mods, f32[8,128]{1,0:T(8,128)S(1)} %get-tuple-element.50.refs_1_, bf16[16,40,384]{2,1,0:T(8,128)(2,1)S(1)} %all_to_all.10.refs_2_.own_ref, bf16[16,40,384]{2,1,0:T(8,128)(2,1)S(1)} %collective-permute-done.refs_3_, ...), custom_call_target="tpu_custom_call" | custom-call | flops 1 | bytes 1 | tf_op jit(solution)/shard_map/qkv/pallas_call | solution.py:177
  40.8 3.7 %attend_own.1 = (f32[640,384]{1,0:T(8,128)S(1)}, f32[640,384]{1,0:T(8,128)S(1)}, f32[640,384]{1,0:T(8,128)S(1)}) custom-call(bf16[2,128,128]{2,1,0:T(8,128)(2,1)S(1)} %get-tuple-element.49.bias_ref.refs_1_, bf16[640,384]{1,0:T(8,128)(2,1)S(1)} %get-tuple-element.54.q_ref.refs_2_, bf16[2,640,384]{2,1,0:T(8,128)(2,1)S(1)} %get-tuple-element.55.kv_ref), custom_call_target="tpu_custom_call" | custom-call | flops 1 | bytes 1 | tf_op jit(solution)/shard_map/attend_own/pallas_call | solution.py:241
  44.5 2.3 %collective-permute-done.5.refs_4_ = bf16[16,40,384]{2,1,0:T(8,128)(2,1)S(1)} collective-permute-done((bf16[16,40,384]{2,1,0:T(8,128)(2,1)S(1)}, bf16[16,40,384]{2,1,0:T(8,128)(2,1)S(1)}, u32[]{:S(2)}, u32[]{:S(2)}) %collective-permute-start.5) | collective-permute-done | bytes 491552 | tf_op jit(solution)/shard_map/ppermute | solution.py:355
  46.9 1.9 %collective-permute-done.6.refs_5_ = bf16[16,40,384]{2,1,0:T(8,128)(2,1)S(1)} collective-permute-done((bf16[16,40,384]{2,1,0:T(8,128)(2,1)S(1)}, bf16[16,40,384]{2,1,0:T(8,128)(2,1)S(1)}, u32[]{:S(2)}, u32[]{:S(2)}) %collective-permute-start.6) | collective-permute-done | bytes 491552 | tf_op jit(solution)/shard_map/ppermute | solution.py:355
  48.7 3.0 %qkv.3.refs_6_ = bf16[2,640,384]{2,1,0:T(8,128)(2,1)S(1)} custom-call(f32[16,1536]{1,0:T(8,128)S(1)} %get-tuple-element.82.refs_0_.mods, f32[8,128]{1,0:T(8,128)S(1)} %get-tuple-element.50.refs_1_, bf16[16,40,384]{2,1,0:T(8,128)(2,1)S(1)} %collective-permute-done.3.refs_2_, bf16[16,40,384]{2,1,0:T(8,128)(2,1)S(1)} %collective-permute-done.4.refs_3_, ...), custom_call_target="tpu_custom_call" | custom-call | flops 1 | bytes 1 | tf_op jit(solution)/shard_map/qkv/pallas_call | solution.py:177
  51.7 3.2 %attend.2 = (bf16[2,320,384]{2,1,0:T(8,128)(2,1)S(1)}, bf16[2,320,384]{2,1,0:T(8,128)(2,1)S(1)}) custom-call(f32[16,1536]{1,0:T(8,128)S(1)} %get-tuple-element.82.refs_0_.mods, bf16[2,128,128]{2,1,0:T(8,128)(2,1)S(1)} %get-tuple-element.49.bias_ref.refs_1_, bf16[640,384]{1,0:T(8,128)(2,1)S(1)} %get-tuple-element.54.q_ref.refs_2_, ...), custom_call_target="tpu_custom_call" | custom-call | flops 1 | bytes 1 | tf_op jit(solution)/shard_map/attend/pallas_call | solution.py:312
  55.2 1.7 %collective-permute-done.7.right_ref = bf16[2,320,384]{2,1,0:T(8,128)(2,1)S(1)} collective-permute-done((bf16[2,320,384]{2,1,0:T(8,128)(2,1)S(1)}, bf16[2,320,384]{2,1,0:T(8,128)(2,1)S(1)}, u32[]{:S(2)}, u32[]{:S(2)}) %collective-permute-start.7) | collective-permute-done | bytes 491552 | tf_op jit(solution)/shard_map/ppermute | solution.py:355
  57.0 1.1 %collective-permute-start.11 = (bf16[2,320,384]{2,1,0:T(8,128)(2,1)S(1)}, bf16[2,320,384]{2,1,0:T(8,128)(2,1)S(1)}, u32[]{:S(2)}, u32[]{:S(2)}) collective-permute-start(bf16[2,320,384]{2,1,0:T(8,128)(2,1)S(1)} %core_sum.1.sum_ref), channel_id=1, source_target_pairs={{0,2},{1,3},{2,0},{3,1},{4,6},{5,7},{6,4},{7,5},{8,10},{9,11},{10,... | collective-permute-start | bytes 1474568 | tf_op jit(solution)/shard_map/ppermute | solution.py:355
  58.1 3.5 %attend.3 = (bf16[2,192,384]{2,1,0:T(8,128)(2,1)S(1)}, bf16[2,192,384]{2,1,0:T(8,128)(2,1)S(1)}, bf16[2,128,384]{2,1,0:T(8,128)(2,1)S(1)}, bf16[2,128,384]{2,1,0:T(8,128)(2,1)S(1)}) custom-call(f32[16,1536]{1,0:T(8,128)S(1)} %get-tuple-element.82.refs_0_.mods, bf16[2,128,128]{2,1,0:T(8,128)(2,1)S(1)} %get-tuple-element.49.bias_ref.refs_1_, ...), custom_call_target="tpu_custom_call" | custom-call | flops 1 | bytes 1 | tf_op jit(solution)/shard_map/attend/pallas_call | solution.py:312
  62.3 1.4 %collective-permute-done.8.came_t = bf16[2,128,384]{2,1,0:T(8,128)(2,1)S(1)} collective-permute-done((bf16[2,128,384]{2,1,0:T(8,128)(2,1)S(1)}, bf16[2,128,384]{2,1,0:T(8,128)(2,1)S(1)}, u32[]{:S(2)}, u32[]{:S(2)}) %collective-permute-start.8) | collective-permute-done | bytes 196640 | tf_op jit(solution)/shard_map/ppermute | solution.py:355
  63.7 1.1 %collective-permute-start.10 = (bf16[2,256,384]{2,1,0:T(8,128)(2,1)S(1)}, bf16[2,256,384]{2,1,0:T(8,128)(2,1)S(1)}, u32[]{:S(2)}, u32[]{:S(2)}) collective-permute-start(bf16[2,256,384]{2,1,0:T(8,128)(2,1)S(1)} %get-tuple-element.70), channel_id=1, source_target_pairs={{0,2},{1,3},{2,0},{3,1},{4,6},{5,7},{6,4},{7,5},{8,10},{9,11},{10,... | collective-permute-start | bytes 1179656 | tf_op jit(solution)/shard_map/ppermute | solution.py:355
  64.8 6.3 %collective-permute-done.11.back_ref = bf16[2,320,384]{2,1,0:T(8,128)(2,1)S(1)} collective-permute-done((bf16[2,320,384]{2,1,0:T(8,128)(2,1)S(1)}, bf16[2,320,384]{2,1,0:T(8,128)(2,1)S(1)}, u32[]{:S(2)}, u32[]{:S(2)}) %collective-permute-start.11) | collective-permute-done | bytes 491552 | tf_op jit(solution)/shard_map/ppermute | solution.py:355
  72.0 1.0 collective-permute-done.13.n1
  73.3 4.6 %mlp.2 = (bf16[2,320,384]{2,1,0:T(8,128)(2,1)S(1)}, bf16[320,384]{1,0:T(8,128)(2,1)S(1)}, bf16[320,384]{1,0:T(8,128)(2,1)S(1)}) custom-call(f32[16,1536]{1,0:T(8,128)S(1)} %get-tuple-element.82.refs_0_.mods, bf16[320,384]{1,0:T(8,128)(2,1)S(1)} %get-tuple-element.73.m0.mid_a, bf16[320,384]{1,0:T(8,128)(2,1)S(1)} %get-tuple-element.74.m1, ...), custom_call_target="tpu_custom_call" | custom-call | flops 1 | bytes 1 | tf_op jit(solution)/shard_map/mlp/pallas_call | solution.py:342
  79.5 0.9 collective-permute-done.16.n1
  80.6 1.1 %collective-permute-start.18 = (bf16[320,384]{1,0:T(8,128)(2,1)S(1)}, bf16[320,384]{1,0:T(8,128)(2,1)S(1)}, u32[]{:S(2)}, u32[]{:S(2)}) collective-permute-start(bf16[320,384]{1,0:T(8,128)(2,1)S(1)} %away.2), channel_id=1, source_target_pairs={{0,2},{1,3},{2,0},{3,1},{4,6},{5,7},{6,4},{7,5},{8,10},{9,11},{10,... | collective-permute-start | bytes 737288 | tf_op jit(solution)/shard_map/ppermute | solution.py:355
  81.8 2.9 %mlp.3 = (bf16[2,192,384]{2,1,0:T(8,128)(2,1)S(1)}, bf16[192,384]{1,0:T(8,128)(2,1)S(1)}, bf16[192,384]{1,0:T(8,128)(2,1)S(1)}) custom-call(f32[16,1536]{1,0:T(8,128)S(1)} %get-tuple-element.82.refs_0_.mods, bf16[192,384]{1,0:T(8,128)(2,1)S(1)} %get-tuple-element.78.m0.mid_b, bf16[192,384]{1,0:T(8,128)(2,1)S(1)} %get-tuple-element.79.m1, ...), custom_call_target="tpu_custom_call" | custom-call | flops 1 | bytes 1 | tf_op jit(solution)/shard_map/mlp/pallas_call | solution.py:342
  85.3 3.6 %collective-permute-done.18.last_a = bf16[320,384]{1,0:T(8,128)(2,1)S(1)} collective-permute-done((bf16[320,384]{1,0:T(8,128)(2,1)S(1)}, bf16[320,384]{1,0:T(8,128)(2,1)S(1)}, u32[]{:S(2)}, u32[]{:S(2)}) %collective-permute-start.18) | collective-permute-done | bytes 245792 | tf_op jit(solution)/shard_map/ppermute | solution.py:355
  89.1 1.1 %collective-permute-start.21 = (bf16[192,384]{1,0:T(8,128)(2,1)S(1)}, bf16[192,384]{1,0:T(8,128)(2,1)S(1)}, u32[]{:S(2)}, u32[]{:S(2)}) collective-permute-start(bf16[192,384]{1,0:T(8,128)(2,1)S(1)} %away.3), channel_id=1, source_target_pairs={{0,2},{1,3},{2,0},{3,1},{4,6},{5,7},{6,4},{7,5},{8,10},{9,11},{10,... | collective-permute-start | bytes 442376 | tf_op jit(solution)/shard_map/ppermute | solution.py:355
  90.2 4.2 %collective-permute-done.21.last_b = bf16[192,384]{1,0:T(8,128)(2,1)S(1)} collective-permute-done((bf16[192,384]{1,0:T(8,128)(2,1)S(1)}, bf16[192,384]{1,0:T(8,128)(2,1)S(1)}, u32[]{:S(2)}, u32[]{:S(2)}) %collective-permute-start.21) | collective-permute-done | bytes 147488 | tf_op jit(solution)/shard_map/ppermute | solution.py:355
  94.6 13.8 %all_to_all.11.rows_ref = bf16[16,40,384]{2,1,0:T(8,128)(2,1)S(1)} all-to-all(bf16[16,40,384]{2,1,0:T(8,128)(2,1)S(1)} %final.1), channel_id=1, replica_groups={{0,4,16,20,32,36,48,52,64,68,80,84,96,100,112,116},{8,12,24,28,40,44,56..., dimensions={0} | all-to-all | bytes 983040 | tf_op jit(solution)/shard_map/all_to_all | solution.py:575
  108.4 0.8 unpack.1
  (50 shorter events, 5.1 us)
Async XLA Ops:
  21.9 11.3 %collective-permute-start.1 = (bf16[16,40,384]{2,1,0:T(8,128)(2,1)S(1)}, bf16[16,40,384]{2,1,0:T(8,128)(2,1)S(1)}, u32[]{:S(2)}, u32[]{:S(2)}) collective-permute-start(bf16[16,40,384]{2,1,0:T(8,128)(2,1)S(1)} %all_to_all.10.refs_2_.own_ref), channel_id=1, source_target_pairs={{0,2},{1,3},{2,0},{3,1},{4,6},{5,7},{6,4},{7,5},{8,10},{9,11},{10,... | collective-permute-start | bytes 1474568 | tf_op jit(solution)/shard_map/ppermute | solution.py:355
  23.0 12.5 %collective-permute-start.3 = (bf16[16,40,384]{2,1,0:T(8,128)(2,1)S(1)}, bf16[16,40,384]{2,1,0:T(8,128)(2,1)S(1)}, u32[]{:S(2)}, u32[]{:S(2)}) collective-permute-start(bf16[16,40,384]{2,1,0:T(8,128)(2,1)S(1)} %all_to_all.10.refs_2_.own_ref), channel_id=1, source_target_pairs={{0,8},{4,12},{8,0},{12,4},{16,24},{20,28},{24,16},{28,20},{32,40},... | collective-permute-start | bytes 1474568 | tf_op jit(solution)/shard_map/ppermute | solution.py:355
  25.9 0.7 copy-start.2
  26.5 0.7 copy-start.3
  31.2 5.3 %collective-permute-start = (bf16[16,40,384]{2,1,0:T(8,128)(2,1)S(1)}, bf16[16,40,384]{2,1,0:T(8,128)(2,1)S(1)}, u32[]{:S(2)}, u32[]{:S(2)}) collective-permute-start(bf16[16,40,384]{2,1,0:T(8,128)(2,1)S(1)} %all_to_all.10.refs_2_.own_ref), channel_id=1, source_target_pairs={{0,1},{1,0},{2,3},{3,2},{4,5},{5,4},{6,7},{7,6},{8,9},{9,8},{10,11... | collective-permute-start | bytes 1474568 | tf_op jit(solution)/shard_map/ppermute | solution.py:355
  33.2 3.3 %collective-permute-start.2 = (bf16[16,40,384]{2,1,0:T(8,128)(2,1)S(1)}, bf16[16,40,384]{2,1,0:T(8,128)(2,1)S(1)}, u32[]{:S(2)}, u32[]{:S(2)}) collective-permute-start(bf16[16,40,384]{2,1,0:T(8,128)(2,1)S(1)} %collective-permute-done.1.refs_4_.far_ref), channel_id=1, source_target_pairs={{0,1},{1,0},{2,3},{3,2},{4,5},{5,4},{6,7},{7,6},{8,9},{9,8},{10,11... | collective-permute-start | bytes 1474568 | tf_op jit(solution)/shard_map/ppermute | solution.py:355
  35.5 11.4 %collective-permute-start.5 = (bf16[16,40,384]{2,1,0:T(8,128)(2,1)S(1)}, bf16[16,40,384]{2,1,0:T(8,128)(2,1)S(1)}, u32[]{:S(2)}, u32[]{:S(2)}) collective-permute-start(bf16[16,40,384]{2,1,0:T(8,128)(2,1)S(1)} %collective-permute-done.3.refs_2_), channel_id=1, source_target_pairs={{0,2},{1,3},{2,0},{3,1},{4,6},{5,7},{6,4},{7,5},{8,10},{9,11},{10,... | collective-permute-start | bytes 1474568 | tf_op jit(solution)/shard_map/ppermute | solution.py:355
  40.7 6.1 %collective-permute-start.4 = (bf16[16,40,384]{2,1,0:T(8,128)(2,1)S(1)}, bf16[16,40,384]{2,1,0:T(8,128)(2,1)S(1)}, u32[]{:S(2)}, u32[]{:S(2)}) collective-permute-start(bf16[16,40,384]{2,1,0:T(8,128)(2,1)S(1)} %collective-permute-done.3.refs_2_), channel_id=1, source_target_pairs={{0,1},{1,0},{2,3},{3,2},{4,5},{5,4},{6,7},{7,6},{8,9},{9,8},{10,11... | collective-permute-start | bytes 1474568 | tf_op jit(solution)/shard_map/ppermute | solution.py:355
  46.9 4.8 %copy-start = (bf16[384,1536]{1,0:T(8,128)(2,1)S(1)}, bf16[384,1536]{1,0:T(8,128)(2,1)}, u32[]{:S(2)}) copy-start(bf16[384,1536]{1,0:T(8,128)(2,1)} %refs_7_.3) | copy-start | bytes 3538948
  46.9 1.9 %collective-permute-start.6 = (bf16[16,40,384]{2,1,0:T(8,128)(2,1)S(1)}, bf16[16,40,384]{2,1,0:T(8,128)(2,1)S(1)}, u32[]{:S(2)}, u32[]{:S(2)}) collective-permute-start(bf16[16,40,384]{2,1,0:T(8,128)(2,1)S(1)} %collective-permute-done.5.refs_4_), channel_id=1, source_target_pairs={{0,1},{1,0},{2,3},{3,2},{4,5},{5,4},{6,7},{7,6},{8,9},{9,8},{10,11... | collective-permute-start | bytes 1474568 | tf_op jit(solution)/shard_map/ppermute | solution.py:355
  48.7 24.6 %slice-start.2 = ((s8[4718592]{0:T(1024)(128)(4,1)}), s8[4194304]{0:T(1024)(128)(4,1)S(1)}, s32[]{:S(2)}) async-start(s8[4718592]{0:T(1024)(128)(4,1)} %bitcast.12), calls=%async_computation.4 | async-start | bytes 8388608
  51.7 6.4 %copy-start.1 = (bf16[384,1536]{1,0:T(8,128)(2,1)S(1)}, bf16[384,1536]{1,0:T(8,128)(2,1)}, u32[]{:S(2)}) copy-start(bf16[384,1536]{1,0:T(8,128)(2,1)} %refs_8_.1) | copy-start | bytes 3538948
  51.7 21.6 %slice-start.3 = ((s8[4718592]{0:T(1024)(128)(4,1)}), s8[524288]{0:T(1024)(128)(4,1)S(1)}, s32[]{:S(2)}) async-start(s8[4718592]{0:T(1024)(128)(4,1)} %bitcast.12), calls=%async_computation.5 | async-start | bytes 1048576
  54.9 1.9 %collective-permute-start.7 = (bf16[2,320,384]{2,1,0:T(8,128)(2,1)S(1)}, bf16[2,320,384]{2,1,0:T(8,128)(2,1)S(1)}, u32[]{:S(2)}, u32[]{:S(2)}) collective-permute-start(bf16[2,320,384]{2,1,0:T(8,128)(2,1)S(1)} %get-tuple-element.64), channel_id=1, source_target_pairs={{0,1},{1,0},{2,3},{3,2},{4,5},{5,4},{6,7},{7,6},{8,9},{9,8},{10,11... | collective-permute-start | bytes 1474568 | tf_op jit(solution)/shard_map/ppermute | solution.py:355
  56.9 16.4 %slice-start = ((s8[4718592]{0:T(1024)(128)(4,1)}), s8[4194304]{0:T(1024)(128)(4,1)S(1)}, s32[]{:S(2)}) async-start(s8[4718592]{0:T(1024)(128)(4,1)} %bitcast.10), calls=%async_computation.2 | async-start | bytes 8388608
  57.0 16.3 %slice-start.1 = ((s8[4718592]{0:T(1024)(128)(4,1)}), s8[524288]{0:T(1024)(128)(4,1)S(1)}, s32[]{:S(2)}) async-start(s8[4718592]{0:T(1024)(128)(4,1)} %bitcast.10), calls=%async_computation.3 | async-start | bytes 1048576
  57.0 14.1 %collective-permute-start.11 = (bf16[2,320,384]{2,1,0:T(8,128)(2,1)S(1)}, bf16[2,320,384]{2,1,0:T(8,128)(2,1)S(1)}, u32[]{:S(2)}, u32[]{:S(2)}) collective-permute-start(bf16[2,320,384]{2,1,0:T(8,128)(2,1)S(1)} %core_sum.1.sum_ref), channel_id=1, source_target_pairs={{0,2},{1,3},{2,0},{3,1},{4,6},{5,7},{6,4},{7,5},{8,10},{9,11},{10,... | collective-permute-start | bytes 1474568 | tf_op jit(solution)/shard_map/ppermute | solution.py:355
  61.7 1.9 %collective-permute-start.9 = (bf16[2,192,384]{2,1,0:T(8,128)(2,1)S(1)}, bf16[2,192,384]{2,1,0:T(8,128)(2,1)S(1)}, u32[]{:S(2)}, u32[]{:S(2)}) collective-permute-start(bf16[2,192,384]{2,1,0:T(8,128)(2,1)S(1)} %get-tuple-element.69), channel_id=1, source_target_pairs={{0,1},{1,0},{2,3},{3,2},{4,5},{5,4},{6,7},{7,6},{8,9},{9,8},{10,11... | collective-permute-start | bytes 884744 | tf_op jit(solution)/shard_map/ppermute | solution.py:355
  61.8 1.9 %collective-permute-start.8 = (bf16[2,128,384]{2,1,0:T(8,128)(2,1)S(1)}, bf16[2,128,384]{2,1,0:T(8,128)(2,1)S(1)}, u32[]{:S(2)}, u32[]{:S(2)}) collective-permute-start(bf16[2,128,384]{2,1,0:T(8,128)(2,1)S(1)} %get-tuple-element.67), channel_id=1, source_target_pairs={{0,1},{1,0},{2,3},{3,2},{4,5},{5,4},{6,7},{7,6},{8,9},{9,8},{10,11... | collective-permute-start | bytes 589832 | tf_op jit(solution)/shard_map/ppermute | solution.py:355
  63.7 15.1 %collective-permute-start.10 = (bf16[2,256,384]{2,1,0:T(8,128)(2,1)S(1)}, bf16[2,256,384]{2,1,0:T(8,128)(2,1)S(1)}, u32[]{:S(2)}, u32[]{:S(2)}) collective-permute-start(bf16[2,256,384]{2,1,0:T(8,128)(2,1)S(1)} %get-tuple-element.70), channel_id=1, source_target_pairs={{0,2},{1,3},{2,0},{3,1},{4,6},{5,7},{6,4},{7,5},{8,10},{9,11},{10,... | collective-permute-start | bytes 1179656 | tf_op jit(solution)/shard_map/ppermute | solution.py:355
  71.4 1.6 %collective-permute-start.13 = (bf16[320,384]{1,0:T(8,128)(2,1)S(1)}, bf16[320,384]{1,0:T(8,128)(2,1)S(1)}, u32[]{:S(2)}, u32[]{:S(2)}) collective-permute-start(bf16[320,384]{1,0:T(8,128)(2,1)S(1)} %get-tuple-element.74.m1), channel_id=1, source_target_pairs={{0,1},{1,0},{2,3},{3,2},{4,5},{5,4},{6,7},{7,6},{8,9},{9,8},{10,11... | collective-permute-start | bytes 737288 | tf_op jit(solution)/shard_map/ppermute | solution.py:355
  71.5 1.9 %collective-permute-start.12 = (bf16[320,384]{1,0:T(8,128)(2,1)S(1)}, bf16[320,384]{1,0:T(8,128)(2,1)S(1)}, u32[]{:S(2)}, u32[]{:S(2)}) collective-permute-start(bf16[320,384]{1,0:T(8,128)(2,1)S(1)} %get-tuple-element.73.m0.mid_a), channel_id=1, source_target_pairs={{0,1},{1,0},{2,3},{3,2},{4,5},{5,4},{6,7},{7,6},{8,9},{9,8},{10,11... | collective-permute-start | bytes 737288 | tf_op jit(solution)/shard_map/ppermute | solution.py:355
  78.0 2.6 %collective-permute-start.17 = (bf16[320,384]{1,0:T(8,128)(2,1)S(1)}, bf16[320,384]{1,0:T(8,128)(2,1)S(1)}, u32[]{:S(2)}, u32[]{:S(2)}) collective-permute-start(bf16[320,384]{1,0:T(8,128)(2,1)S(1)} %get-tuple-element.81), channel_id=1, source_target_pairs={{0,1},{1,0},{2,3},{3,2},{4,5},{5,4},{6,7},{7,6},{8,9},{9,8},{10,11... | collective-permute-start | bytes 737288 | tf_op jit(solution)/shard_map/ppermute | solution.py:355
  78.9 1.5 %collective-permute-start.16 = (bf16[192,384]{1,0:T(8,128)(2,1)S(1)}, bf16[192,384]{1,0:T(8,128)(2,1)S(1)}, u32[]{:S(2)}, u32[]{:S(2)}) collective-permute-start(bf16[192,384]{1,0:T(8,128)(2,1)S(1)} %get-tuple-element.79.m1), channel_id=1, source_target_pairs={{0,1},{1,0},{2,3},{3,2},{4,5},{5,4},{6,7},{7,6},{8,9},{9,8},{10,11... | collective-permute-start | bytes 442376 | tf_op jit(solution)/shard_map/ppermute | solution.py:355
  79.0 1.6 %collective-permute-start.15 = (bf16[192,384]{1,0:T(8,128)(2,1)S(1)}, bf16[192,384]{1,0:T(8,128)(2,1)S(1)}, u32[]{:S(2)}, u32[]{:S(2)}) collective-permute-start(bf16[192,384]{1,0:T(8,128)(2,1)S(1)} %get-tuple-element.78.m0.mid_b), channel_id=1, source_target_pairs={{0,1},{1,0},{2,3},{3,2},{4,5},{5,4},{6,7},{7,6},{8,9},{9,8},{10,11... | collective-permute-start | bytes 442376 | tf_op jit(solution)/shard_map/ppermute | solution.py:355
  80.6 8.2 %collective-permute-start.18 = (bf16[320,384]{1,0:T(8,128)(2,1)S(1)}, bf16[320,384]{1,0:T(8,128)(2,1)S(1)}, u32[]{:S(2)}, u32[]{:S(2)}) collective-permute-start(bf16[320,384]{1,0:T(8,128)(2,1)S(1)} %away.2), channel_id=1, source_target_pairs={{0,2},{1,3},{2,0},{3,1},{4,6},{5,7},{6,4},{7,5},{8,10},{9,11},{10,... | collective-permute-start | bytes 737288 | tf_op jit(solution)/shard_map/ppermute | solution.py:355
  81.8 7.1 %collective-permute-start.14 = (bf16[320,384]{1,0:T(8,128)(2,1)S(1)}, bf16[320,384]{1,0:T(8,128)(2,1)S(1)}, u32[]{:S(2)}, u32[]{:S(2)}) collective-permute-start(bf16[320,384]{1,0:T(8,128)(2,1)S(1)} %get-tuple-element.76), channel_id=1, source_target_pairs={{0,1},{1,0},{2,3},{3,2},{4,5},{5,4},{6,7},{7,6},{8,9},{9,8},{10,11... | collective-permute-start | bytes 737288 | tf_op jit(solution)/shard_map/ppermute | solution.py:355
  84.6 4.4 %collective-permute-start.20 = (bf16[192,384]{1,0:T(8,128)(2,1)S(1)}, bf16[192,384]{1,0:T(8,128)(2,1)S(1)}, u32[]{:S(2)}, u32[]{:S(2)}) collective-permute-start(bf16[192,384]{1,0:T(8,128)(2,1)S(1)} %get-tuple-element.89), channel_id=1, source_target_pairs={{0,1},{1,0},{2,3},{3,2},{4,5},{5,4},{6,7},{7,6},{8,9},{9,8},{10,11... | collective-permute-start | bytes 442376 | tf_op jit(solution)/shard_map/ppermute | solution.py:355
  85.2 5.0 %collective-permute-start.19 = (bf16[192,384]{1,0:T(8,128)(2,1)S(1)}, bf16[192,384]{1,0:T(8,128)(2,1)S(1)}, u32[]{:S(2)}, u32[]{:S(2)}) collective-permute-start(bf16[192,384]{1,0:T(8,128)(2,1)S(1)} %get-tuple-element.87), channel_id=1, source_target_pairs={{0,1},{1,0},{2,3},{3,2},{4,5},{5,4},{6,7},{7,6},{8,9},{9,8},{10,11... | collective-permute-start | bytes 442376 | tf_op jit(solution)/shard_map/ppermute | solution.py:355
  89.1 5.3 %collective-permute-start.21 = (bf16[192,384]{1,0:T(8,128)(2,1)S(1)}, bf16[192,384]{1,0:T(8,128)(2,1)S(1)}, u32[]{:S(2)}, u32[]{:S(2)}) collective-permute-start(bf16[192,384]{1,0:T(8,128)(2,1)S(1)} %away.3), channel_id=1, source_target_pairs={{0,2},{1,3},{2,0},{3,1},{4,6},{5,7},{6,4},{7,5},{8,10},{9,11},{10,... | collective-permute-start | bytes 442376 | tf_op jit(solution)/shard_map/ppermute | solution.py:355
